TPU v7x, 32 devices: a whole 2x2x4 slice. The times are simulated.
32 devices in a mesh: dp: 8 (over z, core), ctx: 4 (over y, x).
Axes of the slice: x: 2, y: 2, z: 4, core: 2. Of those that a mesh axis runs over, the one named last changes fastest.
Arguments:
- mixer_input: bfloat16 [8, 512, 768], P('dp', 'ctx'), may hold values from -6 to 6
- step_input: float32 [8, 512, 4], P('dp', 'ctx'), may hold values from -3 to 6
- conv_weight: float32 [4, 768], replicated, may hold values from -3 to 3
- decay_log: float32 [4], replicated, as said below
- step_bias: float32 [4], replicated, may hold values from -1 to 1
- residual_coefficient: float32 [4], replicated, may hold values from 0.5 to 1.5
- mixer_cotangent: bfloat16 [8, 512, 512], P('dp', 'ctx'), may hold values from -6 to 6
- queries: bfloat16 [8, 512, 512], P('dp', 'ctx'), may hold values from -4.5 to 4.5
- attn_keys: bfloat16 [8, 512, 128], P('dp', 'ctx'), may hold values from -4.5 to 4.5
- attn_values: bfloat16 [8, 512, 128], P('dp', 'ctx'), may hold values from -6 to 6
- attn_cotangent: bfloat16 [8, 512, 512], P('dp', 'ctx'), may hold values from -6 to 6
Outputs:
- input_grad: bfloat16 [8, 512, 768], P('dp', 'ctx')
- step_grad: float32 [8, 512, 4], P('dp', 'ctx')
- conv_grad: float32 [4, 768], replicated
- decay_grad: float32 [4], replicated
- bias_grad: float32 [4], replicated
- skip_grad: float32 [4], replicated
- query_grad: bfloat16 [8, 512, 512], P('dp', 'ctx')
- key_grad: bfloat16 [8, 512, 128], P('dp', 'ctx')
- value_grad: bfloat16 [8, 512, 128], P('dp', 'ctx')
Inputs may be any that keep to these rules, and one draw needn't show every extreme that they name: decay_log lies between log(0.2 / 512) and log(0.05).
All inputs are finite; a program needn't handle non-finite values.
Results may differ from a plain program's by a relative error of at most 0.011.
Values may be sent and summed in bfloat16 or wider, within the bound.
No kernel may reach another device: no remote copies, remote signals or barrier semaphores. Data moves between devices by JAX's collectives and lax.ppermute only.
A program may use at most 64 MiB of HBM per device.

v0:
```python
import jax
import jax.numpy as jnp
from jax import lax
from jax.experimental import pallas as pl
from jax.experimental.pallas import tpu as pltpu
from jax.sharding import PartitionSpec as P


F32 = jnp.float32
BF16 = jnp.bfloat16
HEADS = 4
TAPS = 4
W = 128
GROUPS = HEADS + 2
KV_ROWS = 2 * W
STEP_ROW = (HEADS + 1) * W
EDGE_ROW = STEP_ROW + 16
BULK_ROWS = EDGE_ROW + 16
PAY_ROWS = 40
LIMIT = 16 << 20
LOG2E = 1.4426950408889634


def dot(a, b, dims=((1,), (0,)), precise=False):
    return lax.dot_general(
        a,
        b,
        (dims, ((), ())),
        precision=lax.Precision.HIGHEST if precise else None,
        preferred_element_type=F32,
    )


def split(array):
    high = array.astype(BF16)
    return high, (array - high.astype(F32)).astype(BF16)


def dot_split(a, b, dims=((1,), (0,))):
    a = a if isinstance(a, tuple) else (a,)
    b = b if isinstance(b, tuple) else (b,)
    total = dot(a[0], b[0], dims)
    if len(a) > 1:
        total = total + dot(a[1], b[0], dims)
    if len(b) > 1:
        total = total + dot(a[0], b[1], dims)
    return total


NT = ((1,), (1,))
TN = ((0,), (0,))


def iota2(dim):
    return lax.broadcasted_iota(jnp.int32, (W, W), dim)


def cols(g):
    return slice(g * W, (g + 1) * W)


def pack_body(bits, mixer, step, cotan, keys, values, near, *refs):
    bulk, (size, extra, sems) = refs[:bits], refs[bits:]
    me = lax.axis_index("ctx")

    def copy(source, target, at):
        return pltpu.make_async_copy(source, target, sems.at[at])

    first = [
        copy(step.at[0], size, 0),
        copy(keys.at[0], near.at[0:W, :], 1),
        copy(values.at[0], near.at[W : 2 * W, :], 2),
    ]
    for c in first:
        c.start()
    later = [jnp.bitwise_and(lax.shift_right_logical(me, b), 1) == 0 for b in range(bits)]
    forward, backward = [], []
    for b in range(bits):
        at = 3 + b * (GROUPS + 6)
        forward.append(
            [
                copy(mixer.at[0, :, cols(g)], bulk[b].at[cols(g), :], at + g)
                for g in range(HEADS + 1)
            ]
            + [
                copy(
                    mixer.at[0, W - 16 : W, cols(HEADS + 1)],
                    bulk[b].at[EDGE_ROW:BULK_ROWS, :],
                    at + HEADS + 1,
                )
            ]
        )
        backward.append(
            [
                copy(cotan.at[0, :, cols(g)], bulk[b].at[cols(g), :], at + GROUPS + g)
                for g in range(HEADS)
            ]
            + [
                copy(
                    mixer.at[0, :, cols(HEADS + 1)],
                    bulk[b].at[cols(HEADS), :],
                    at + GROUPS + HEADS,
                )
            ]
        )

        @pl.when(later[b])
        def _(b=b):
            for c in forward[b]:
                c.start()

        @pl.when(jnp.logical_not(later[b]))
        def _(b=b):
            for c in backward[b]:
                c.start()

    for c in first:
        c.wait()
    rows = size[...]
    high = rows.astype(BF16).astype(F32)
    mid = (rows - high).astype(BF16).astype(F32)
    low = rows - high - mid
    extra[0:16, :] = jnp.concatenate([high, mid, low, jnp.zeros_like(low)], axis=0).astype(BF16)
    extra[16:32, :] = jnp.zeros((16, W), BF16)
    for b in range(bits):
        at = 3 + bits * (GROUPS + 6) + 2 * b
        sized = copy(extra.at[0:16, :], bulk[b].at[STEP_ROW:EDGE_ROW, :], at)
        empty = copy(extra.at[16:32, :], bulk[b].at[EDGE_ROW:BULK_ROWS, :], at + 1)
        forward[b].append(sized)
        backward[b] += [sized, empty]
        sized.start()

        @pl.when(later[b])
        def _(b=b):
            for c in forward[b]:
                c.wait()

        @pl.when(jnp.logical_not(later[b]))
        def _(b=b, empty=empty):
            empty.start()
            for c in backward[b]:
                c.wait()


def attend_body(peers, queries, keys, values, cotan, *refs):
    near = refs[:peers]
    query_grad, own, *parts = refs[peers:]
    me = lax.axis_index("ctx")
    scale = W ** (-0.5)
    keys_all = jnp.concatenate([keys[0]] + [m[0:W, :] for m in near], axis=0)
    values_all = jnp.concatenate([values[0]] + [m[W : 2 * W, :] for m in near], axis=0)
    causal = iota2(0) >= iota2(1)
    rounded_heads, dscore_heads = [], []
    for r in range(HEADS):
        query = queries[0, :, cols(r)]
        cot = cotan[0, :, cols(r)]
        scores = dot(query, keys_all, NT) * (scale * LOG2E)
        blocks = [jnp.where(causal, scores[:, 0:W], -jnp.inf)]
        for k in range(1, peers + 1):
            bit = k.bit_length() - 1
            earlier = jnp.bitwise_and(lax.shift_right_logical(me, bit), 1) == 1
            blocks.append(jnp.where(earlier, scores[:, cols(k)], -jnp.inf))
        scores = jnp.concatenate(blocks, axis=1)
        top = jnp.max(scores, axis=1, keepdims=True)
        weights = jnp.exp2(scores - top)
        probs = weights * (1.0 / jnp.sum(weights, axis=1, keepdims=True))
        rounded = probs.astype(BF16)
        attended = dot(rounded, values_all)
        delta = jnp.sum(cot.astype(F32) * attended, axis=1, keepdims=True)
        dprob = dot(cot, values_all, NT)
        dscore = (probs * (dprob - delta) * scale).astype(BF16)
        query_grad[0, :, cols(r)] = dot(dscore, keys_all).astype(BF16)
        rounded_heads.append(rounded)
        dscore_heads.append(dscore)
    query_rows = jnp.concatenate([queries[0, :, cols(r)] for r in range(HEADS)], axis=0)
    cotan_rows = jnp.concatenate([cotan[0, :, cols(r)] for r in range(HEADS)], axis=0)
    key_acc = dot(jnp.concatenate(dscore_heads, axis=0), query_rows, TN)
    value_acc = dot(jnp.concatenate(rounded_heads, axis=0), cotan_rows, TN)
    own[0:W, :] = key_acc[0:W]
    own[W : 2 * W, :] = value_acc[0:W]
    for k in range(1, peers + 1):
        parts[k - 1][0:W, :] = key_acc[cols(k)].astype(BF16)
        parts[k - 1][W : 2 * W, :] = value_acc[cols(k)].astype(BF16)


def head_column(ref, lanes):
    return jnp.concatenate([jnp.full((1, lanes), ref[h], F32) for h in range(HEADS)], axis=0)


def sigmoid(v):
    return 0.5 * jnp.tanh(0.5 * v) + 0.5


def mixer_body(peers, *refs):
    mixer, step, weight, decay_log, bias, residual, cotan = refs[:7]
    bulk = refs[7 : 7 + peers]
    input_grad, step_grad, edge, first, pay = refs[7 + peers : 12 + peers]
    tails, ext, grads, peer_ext, states, adjoints, acts, slopes = refs[12 + peers :]
    me = lax.axis_index("ctx")
    slots = peers + 1
    index = [me] + [jnp.bitwise_xor(me, k) for k in range(1, slots)]

    tails[0] = jnp.zeros((16 * GROUPS, W), BF16)
    for g in range(GROUPS):
        tails[me + 1, 16 * g : 16 * g + 16, :] = mixer[0, W - 16 : W, cols(g)]
    for k in range(1, slots):
        earlier = index[k] < me

        @pl.when(earlier)
        def _(k=k):
            for g in range(HEADS + 1):
                tails[index[k] + 1, 16 * g : 16 * g + 16, :] = bulk[k - 1][
                    (g + 1) * W - 16 : (g + 1) * W, :
                ]
            tails[index[k] + 1, 16 * (GROUPS - 1) : 16 * GROUPS, :] = bulk[k - 1][
                EDGE_ROW:BULK_ROWS, :
            ]

        @pl.when(jnp.logical_not(earlier))
        def _(k=k):
            tails[index[k] + 1, 16 * (GROUPS - 1) : 16 * GROUPS, :] = bulk[k - 1][
                STEP_ROW - 16 : STEP_ROW, :
            ]

    pieces = [step[0]]
    for k in range(1, slots):
        sent = bulk[k - 1][STEP_ROW:EDGE_ROW, :].astype(F32)
        pieces.append(sent[0:4] + sent[4:8] + sent[8:12])
    rate = -jnp.exp(head_column(decay_log, W))
    raw = jnp.concatenate(pieces, axis=0) + jnp.concatenate([head_column(bias, W)] * slots, axis=0)
    sizes = jnp.maximum(raw, 0.0) + jnp.log(1.0 + jnp.exp(-jnp.abs(raw)))
    decays = sizes * jnp.concatenate([rate] * slots, axis=0)
    upto = (iota2(0) <= iota2(1)).astype(F32)
    cumulative = dot(decays, upto, precise=True)

    def rows_of(array, k):
        return array[HEADS * k : HEADS * (k + 1)]

    totals = [
        jnp.broadcast_to(rows_of(cumulative, k)[:, W - 1 : W], (HEADS, W)) for k in range(slots)
    ]
    own_cum = rows_of(cumulative, 0)
    own_size = rows_of(sizes, 0)
    table = [own_cum, own_size, jnp.exp(own_cum), jnp.exp(totals[0] - own_cum)]
    for k in range(1, slots):
        low, high = jnp.minimum(me, index[k]), jnp.maximum(me, index[k])
        between = jnp.zeros((HEADS, W), F32)
        for m in range(1, slots):
            inside = jnp.logical_and(index[m] > low, index[m] < high)
            between = between + jnp.where(inside, totals[m], 0.0)
        earlier = index[k] < me
        cum = rows_of(cumulative, k)
        span = jnp.where(earlier, totals[k] - cum, cum) + between
        table.append(jnp.exp(span) * jnp.where(earlier, rows_of(sizes, k), 1.0))
    table.append(jnp.zeros((W - HEADS * len(table), W), F32))
    columns = jnp.transpose(jnp.concatenate(table, axis=0))

    def column(group, h):
        at = HEADS * group + h
        return columns[:, at : at + 1]

    def convolve(place, g):
        total = place[5 : 5 + W, :] * weight[0:1, cols(g)]
        for offset in range(1, TAPS):
            total = total + place[5 + offset : 5 + offset + W, :] * weight[offset : offset + 1, cols(g)]
        return total

    def peer_act(k, at, g):
        place = peer_ext.at[(k - 1) * GROUPS + g]
        place[0:8, :] = tails[index[k], 16 * g : 16 * g + 16, :].astype(F32)[8:16]
        place[8 : 8 + W, :] = bulk[k - 1][cols(at), :].astype(F32)
        pre = convolve(place, g)
        return pre * sigmoid(pre)

    states[...] = jnp.zeros_like(states)
    adjoints[...] = jnp.zeros_like(adjoints)
    for k in range(1, slots):
        earlier = index[k] < me

        @pl.when(earlier)
        def _(k=k):
            map_in = split(peer_act(k, HEADS, HEADS))
            for h in range(HEADS):
                rows = split(peer_act(k, h, h) * column(3 + k, h))
                states[h] = states[h] + dot_split(rows, map_in, TN)

        @pl.when(jnp.logical_not(earlier))
        def _(k=k):
            map_out = peer_act(k, HEADS, HEADS + 1)
            for h in range(HEADS):
                read = split(map_out * column(3 + k, h))
                adjoints[h] = adjoints[h] + dot_split(bulk[k - 1][cols(h), :], read, TN)

    for g in range(GROUPS):
        place = ext.at[g]
        place[0:8, :] = tails[me, 16 * g : 16 * g + 16, :].astype(F32)[8:16]
        place[8 : 8 + W, :] = mixer[0, :, cols(g)].astype(F32)
        pre = convolve(place, g)
        sig = sigmoid(pre)
        acts[g] = pre * sig
        slopes[g] = sig + pre * sig * (1.0 - sig)

    map_in, map_out = acts[HEADS], acts[HEADS + 1]
    map_in_s, map_out_s = split(map_in), split(map_out)
    map_in_b, map_out_b = map_in_s[0], map_out_s[0]
    meets = dot_split(map_out_s, map_in_s, NT)
    lower = iota2(0) >= iota2(1)
    ones = jnp.ones((16, W), BF16)
    grad_in = jnp.zeros((W, W), F32)
    grad_out = jnp.zeros((W, W), F32)
    grad_meets = jnp.zeros((W, W), F32)
    flow_rows, tail_rows, size_rows, pass_rows, skip_rows = [], [], [], [], []
    for h in range(HEADS):
        cot_b = cotan[0, :, cols(h)]
        cot = cot_b.astype(F32)
        act = acts[h]
        size = column(1, h)
        tail = column(3, h)
        scaled = act * size
        state = states[h]
        adjoint = adjoints[h]
        adjoint_s = split(adjoint)
        falloff = jnp.where(lower, jnp.exp(column(0, h) - own_cum[h : h + 1]), 0.0)
        pair = dot_split(cot_b, split(scaled), NT) * falloff
        grad_meets = grad_meets + pair
        flow = split(pair * meets)
        projected = tail * dot_split(map_in_s, adjoint_s, NT)
        mixed = dot_split(split(falloff * meets), cot_b, TN)
        grad_scaled = mixed + projected
        lead_read = column(2, h) * dot_split(cot_b, split(state))
        grad_out = grad_out + lead_read
        grad_in = grad_in + dot((scaled * tail).astype(BF16), adjoint_s[0])
        carried = split(lead_read * map_out)
        trailing = split(projected * act)
        sized = split(mixed * act)
        flow_rows.append(
            (dot_split(ones, flow, NT) - dot_split(ones, flow) + dot_split(ones, carried, NT))[0:1]
        )
        trail = dot_split(ones, trailing, NT)[0:1]
        tail_rows.append(trail * own_size[h : h + 1])
        size_rows.append(dot_split(ones, sized, NT)[0:1] + trail)
        passed = jnp.sum(jnp.sum(state * adjoint, axis=0, keepdims=True), axis=1, keepdims=True)
        pass_rows.append(jnp.broadcast_to(passed, (1, W)))
        skip_rows.append(jnp.sum(cot * act, axis=0, keepdims=True))
        grads[h, 0:W, :] = (residual[h] * cot + grad_scaled * size) * slopes[h]
    grad_meets_b = grad_meets.astype(BF16)
    grad_out = grad_out + dot(grad_meets_b, map_in_b)
    grad_in = grad_in + dot(grad_meets_b, map_out_b, TN)
    grads[HEADS, 0:W, :] = grad_in * slopes[HEADS]
    grads[HEADS + 1, 0:W, :] = grad_out * slopes[HEADS + 1]

    since = (iota2(0) >= iota2(1)).astype(F32)
    before = (iota2(0) < iota2(1)).astype(F32)
    grad_decay = (
        dot(jnp.concatenate(flow_rows, axis=0), since, precise=True)
        + dot(jnp.concatenate(tail_rows, axis=0), before, precise=True)
        + jnp.exp(totals[0]) * jnp.concatenate(pass_rows, axis=0)
    )
    grad_step = grad_decay * rate + jnp.concatenate(size_rows, axis=0)
    grad_raw = grad_step * sigmoid(rows_of(raw, 0))
    step_grad[0] = grad_raw
    pay[24:28, :] = grad_decay * own_size * rate
    pay[28:32, :] = grad_raw
    pay[32:36, :] = jnp.concatenate(skip_rows, axis=0)
    pay[36:40, :] = jnp.zeros((4, W), F32)

    for g in range(GROUPS):
        grads[g, W : W + 8, :] = jnp.zeros((8, W), F32)
        grad = grads[g, 0:W, :]
        first[:, cols(g)] = grad[0:8]
        total = grads[g, TAPS - 1 : TAPS - 1 + W, :] * weight[0:1, cols(g)]
        for offset in range(1, TAPS):
            at = TAPS - 1 - offset
            total = total + grads[g, at : at + W, :] * weight[offset : offset + 1, cols(g)]
        input_grad[0, :, cols(g)] = total.astype(BF16)
        edge[:, cols(g)] = total[W - 16 : W]
        for offset in range(TAPS):
            pay[4 * g + offset : 4 * g + offset + 1, :] = jnp.sum(
                grad * ext[g, 5 + offset : 5 + offset + W, :], axis=0, keepdims=True
            )


def finish_body(peers, count, *refs):
    last, edge, halo, weight, own, total_a, total_b = refs[:7]
    parts = refs[7 : 7 + peers]
    input_grad, key_grad, value_grad, conv_grad, decay_grad, bias_grad, skip_grad = refs[7 + peers :]
    del last
    both = own[...]
    for part in parts:
        both = both + part[...].astype(F32)
    key_grad[0] = both[0:W].astype(BF16)
    value_grad[0] = both[W : 2 * W].astype(BF16)
    row = lax.broadcasted_iota(jnp.int32, (16, W), 0)
    for g in range(GROUPS):
        rows = edge[:, cols(g)]
        for offset in range(TAPS - 1):
            for t in range(TAPS - 1 - offset):
                at = 16 - (TAPS - 1 - offset) + t
                piece = halo[t : t + 1, cols(g)] * weight[offset : offset + 1, cols(g)]
                rows = rows + jnp.where(row == at, piece, 0.0)
        input_grad[0, :, cols(g)] = rows.astype(BF16)
    total = (total_a[...] + total_b[...]) * (1.0 / count)
    for g in range(GROUPS):
        conv_grad[:, cols(g)] = total[4 * g : 4 * g + 4]
    sums = jnp.sum(total[24:40], axis=1, keepdims=True)
    for h in range(HEADS):
        decay_grad[h] = jnp.sum(sums[h : h + 1])
        bias_grad[h] = jnp.sum(sums[4 + h : 5 + h])
        skip_grad[h] = jnp.sum(sums[8 + h : 9 + h])


def shape(dims, dtype):
    return jax.ShapeDtypeStruct(dims, dtype)


def on_device(sizes, *args):
    (
        mixer_input,
        step_input,
        conv_weight,
        decay_log,
        step_bias,
        residual,
        mixer_cotangent,
        queries,
        attn_keys,
        attn_values,
        attn_cotangent,
    ) = args
    ctx, dp = sizes["ctx"], sizes["dp"]
    step_input = jnp.swapaxes(step_input, 1, 2)
    peers = ctx - 1
    bits = ctx.bit_length() - 1
    vmem = pl.BlockSpec(memory_space=pltpu.VMEM)
    smem = pl.BlockSpec(memory_space=pltpu.SMEM)

    hbm = pl.BlockSpec(memory_space=pltpu.HBM)
    params = pltpu.CompilerParams(vmem_limit_bytes=LIMIT)
    near, *bulk = pl.pallas_call(
        lambda *refs: pack_body(bits, *refs),
        out_shape=[shape((KV_ROWS, W), BF16)] + [shape((BULK_ROWS, W), BF16)] * bits,
        in_specs=[hbm] * 5,
        out_specs=[vmem] * (1 + bits),
        scratch_shapes=[
            pltpu.VMEM((HEADS, W), F32),
            pltpu.VMEM((32, W), BF16),
            pltpu.SemaphoreType.DMA((3 + bits * (GROUPS + 8),)),
        ],
        compiler_params=params,
        name="pack",
    )(
        *(
            pltpu.with_memory_space_constraint(array, pltpu.HBM)
            for array in (mixer_input, step_input, mixer_cotangent, attn_keys, attn_values)
        )
    )

    def swap(array, k, keep=lambda i, j: True, axis="ctx"):
        pairs = [(i, i ^ k) for i in range(sizes[axis]) if keep(i, i ^ k)]
        return lax.ppermute(array, axis, pairs)

    nears = [swap(near, k, lambda i, j: j > i) for k in range(1, ctx)]
    bulks = [swap(bulk[k.bit_length() - 1], k) for k in range(1, ctx)]

    query_grad, own, *parts = pl.pallas_call(
        lambda *refs: attend_body(peers, *refs),
        out_shape=[shape(queries.shape, BF16), shape((KV_ROWS, W), F32)]
        + [shape((KV_ROWS, W), BF16)] * peers,
        in_specs=[vmem] * (4 + peers),
        out_specs=[vmem] * (2 + peers),
        compiler_params=params,
        name="attend",
    )(queries, attn_keys, attn_values, attn_cotangent, *nears)

    input_grad, step_grad, edge, first, pay = pl.pallas_call(
        lambda *refs: mixer_body(peers, *refs),
        out_shape=[
            shape(mixer_input.shape, BF16),
            shape(step_input.shape, F32),
            shape((16, GROUPS * W), F32),
            shape((8, GROUPS * W), F32),
            shape((PAY_ROWS, W), F32),
        ],
        in_specs=[vmem] * 3 + [smem] * 3 + [vmem] * (1 + peers),
        out_specs=[vmem] * 5,
        scratch_shapes=[
            pltpu.VMEM((ctx + 1, 16 * GROUPS, W), BF16),
            pltpu.VMEM((GROUPS, W + 8, W), F32),
            pltpu.VMEM((GROUPS, W + 8, W), F32),
            pltpu.VMEM((peers * GROUPS, W + 8, W), F32),
            pltpu.VMEM((HEADS, W, W), F32),
            pltpu.VMEM((HEADS, W, W), F32),
            pltpu.VMEM((GROUPS, W, W), F32),
            pltpu.VMEM((GROUPS, W, W), F32),
        ],
        compiler_params=params,
        name="mixer",
    )(mixer_input, step_input, conv_weight, decay_log, step_bias, residual, mixer_cotangent, *bulks)

    returned = [swap(parts[k - 1], k, lambda i, j: j < i) for k in range(1, ctx)]
    halo = lax.ppermute(first, "ctx", [(i + 1, i) for i in range(ctx - 1)])
    stages = [("dp", 1 << b) for b in range(dp.bit_length() - 1)]
    stages += [("ctx", 1 << b) for b in range(bits)]
    for n, (axis, k) in enumerate(stages):
        other = swap(pay, k, axis=axis)
        if n + 1 < len(stages):
            pay = pay + other

    blocks = mixer_input.shape[1] // 16
    last = pl.BlockSpec((1, 16, GROUPS * W), lambda i: (0, blocks - 1, 0))
    input_grad, key_grad, value_grad, conv_grad, decay_grad, bias_grad, skip_grad = pl.pallas_call(
        lambda *refs: finish_body(peers, dp, *refs),
        out_shape=[
            shape(mixer_input.shape, BF16),
            shape(attn_keys.shape, BF16),
            shape(attn_values.shape, BF16),
            shape(conv_weight.shape, F32),
        ]
        + [shape((HEADS,), F32)] * 3,
        grid=(1,),
        in_specs=[last] + [vmem] * (6 + peers),
        out_specs=[last] + [vmem] * 3 + [smem] * 3,
        input_output_aliases={0: 0},
        compiler_params=pltpu.CompilerParams(vmem_limit_bytes=LIMIT),
        name="finish",
    )(input_grad, edge, halo, conv_weight, own, pay, other, *returned)
    return (
        input_grad,
        jnp.swapaxes(step_grad, 1, 2),
        conv_grad,
        decay_grad,
        bias_grad,
        skip_grad,
        query_grad,
        key_grad,
        value_grad,
    )


def solution(mesh):
    split = P("dp", "ctx", None)
    sizes = dict(mesh.shape)

    def step(*args):
        return on_device(sizes, *args)

    return jax.shard_map(
        step,
        mesh=mesh,
        in_specs=(split, split, P(), P(), P(), P(), split, split, split, split, split),
        out_specs=(split, split, P(), P(), P(), P(), split, split, split),
        check_vma=False,
    )
```

profile of v0, /device:TPU:0, one launch (start us, length us, event | category | flops | bytes accessed | tf_op | source)
XLA Modules:
  0.0 47.4 jit_solution(647284169401555439)
XLA Ops:
  0.7 1.3 %pack.1 = (bf16[256,128]{1,0:T(8,128)(2,1)S(1)}, bf16[672,128]{1,0:T(8,128)(2,1)S(1)}, bf16[672,128]{1,0:T(8,128)(2,1)S(1)}) custom-call(bf16[1,128,768]{2,1,0:T(8,128)(2,1)} %refs_0_.4, f32[1,4,128]{2,1,0:T(4,128)} %bitcast.2, bf16[1,128,512]{2,1,0:T(8,128)(2,1)} %refs_6_.1, bf16[1,128,128]{2,1,0:T(8,128)(2,1)} %refs_1_.1, bf16[1,128,128]{2,1,0:T(8,128)(2,1)} %refs_2_.5), custom_call_target="tpu_custom_call" | custom-call | tf_op jit(solution)/shard_map/pack/pallas_call | solution.py:439
  2.0 0.0 copy-start.7
  2.0 3.0 %collective-permute-start = (bf16[672,128]{1,0:T(8,128)(2,1)S(1)}, bf16[672,128]{1,0:T(8,128)(2,1)S(1)}, u32[]{:S(2)}, u32[]{:S(2)}) collective-permute-start(bf16[672,128]{1,0:T(8,128)(2,1)S(1)} %get-tuple-element.29), channel_id=1, source_target_pairs={{0,1},{1,0},{2,3},{3,2},{4,5},{5,4},{6,7},{7,6},{8,9},{9,8},{10,11... | collective-permute-start | bytes 516104 | tf_op jit(solution)/shard_map/ppermute | solution.py:460
  5.0 1.5 %collective-permute-start.2 = (bf16[672,128]{1,0:T(8,128)(2,1)S(1)}, bf16[672,128]{1,0:T(8,128)(2,1)S(1)}, u32[]{:S(2)}, u32[]{:S(2)}) collective-permute-start(bf16[672,128]{1,0:T(8,128)(2,1)S(1)} %get-tuple-element.30), channel_id=1, source_target_pairs={{0,3},{1,2},{2,1},{3,0},{4,7},{5,6},{6,5},{7,4},{8,11},{9,10},{10,... | collective-permute-start | bytes 516104 | tf_op jit(solution)/shard_map/ppermute | solution.py:460
  6.5 0.1 collective-permute-start.1
  6.6 4.7 %collective-permute-start.6 = (bf16[256,128]{1,0:T(8,128)(2,1)S(1)}, bf16[256,128]{1,0:T(8,128)(2,1)S(1)}, u32[]{:S(2)}, u32[]{:S(2)}) collective-permute-start(bf16[256,128]{1,0:T(8,128)(2,1)S(1)} %get-tuple-element.34), channel_id=1, source_target_pairs={{0,3},{1,2},{4,7},{5,6},{8,11},{9,10},{12,15},{13,14},{16,19},{17,... | collective-permute-start | bytes 196616 | tf_op jit(solution)/shard_map/ppermute | solution.py:460
  11.4 1.3 %collective-permute-start.5 = (bf16[256,128]{1,0:T(8,128)(2,1)S(1)}, bf16[256,128]{1,0:T(8,128)(2,1)S(1)}, u32[]{:S(2)}, u32[]{:S(2)}) collective-permute-start(bf16[256,128]{1,0:T(8,128)(2,1)S(1)} %get-tuple-element.34), channel_id=1, source_target_pairs={{0,2},{1,3},{4,6},{5,7},{8,10},{9,11},{12,14},{13,15},{16,18},{17,... | collective-permute-start | bytes 196616 | tf_op jit(solution)/shard_map/ppermute | solution.py:460
  12.7 2.5 %collective-permute-start.4 = (bf16[256,128]{1,0:T(8,128)(2,1)S(1)}, bf16[256,128]{1,0:T(8,128)(2,1)S(1)}, u32[]{:S(2)}, u32[]{:S(2)}) collective-permute-start(bf16[256,128]{1,0:T(8,128)(2,1)S(1)} %get-tuple-element.34), channel_id=1, source_target_pairs={{0,1},{2,3},{4,5},{6,7},{8,9},{10,11},{12,13},{14,15},{16,17},{18,... | collective-permute-start | bytes 196616 | tf_op jit(solution)/shard_map/ppermute | solution.py:460
  15.2 0.6 %collective-permute-done.1.refs_8_ = bf16[672,128]{1,0:T(8,128)(2,1)S(1)} collective-permute-done((bf16[672,128]{1,0:T(8,128)(2,1)S(1)}, bf16[672,128]{1,0:T(8,128)(2,1)S(1)}, u32[]{:S(2)}, u32[]{:S(2)}) %collective-permute-start.1) | collective-permute-done | bytes 172064 | tf_op jit(solution)/shard_map/ppermute | solution.py:460
  15.8 0.0 copy-start.3
  15.8 0.0 copy-start.4
  15.8 0.0 copy-start.5
  15.8 5.0 %mixer.1 = (bf16[1,128,768]{2,1,0:T(8,128)(2,1)}, f32[1,4,128]{2,1,0:T(4,128)}, f32[16,768]{1,0:T(8,128)S(1)}, f32[8,768]{1,0:T(8,128)S(1)}, f32[40,128]{1,0:T(8,128)S(1)}) custom-call(bf16[1,128,768]{2,1,0:T(8,128)(2,1)S(1)} %copy-done, f32[1,4,128]{2,1,0:T(4,128)S(1)} %bitcast.3, f32[4,768]{1,0:T(4,128)S(1)} %copy-done.6, f32[4]{0:T(128)S(1)} %copy-done.8, ...), custom_call_target="tpu_custom_call" | custom-call | tf_op jit(solution)/shard_map/mixer/pallas_call | solution.py:475
  20.9 0.0 collective-permute-start.7
  20.9 1.2 %collective-permute-done.7 = f32[40,128]{1,0:T(8,128)S(1)} collective-permute-done((f32[40,128]{1,0:T(8,128)S(1)}, f32[40,128]{1,0:T(8,128)S(1)}, u32[]{:S(2)}, u32[]{:S(2)}) %collective-permute-start.7) | collective-permute-done | bytes 20512 | tf_op jit(solution)/shard_map/ppermute | solution.py:460
  22.1 1.7 %collective-permute-start.8 = (f32[40,128]{1,0:T(8,128)S(1)}, f32[40,128]{1,0:T(8,128)S(1)}, u32[]{:S(2)}, u32[]{:S(2)}) collective-permute-start(f32[40,128]{1,0:T(8,128)S(1)} %add.12), channel_id=1, source_target_pairs={{0,8},{4,12},{8,0},{12,4},{16,24},{20,28},{24,16},{28,20},{1,9},{5... | collective-permute-start | bytes 61448 | tf_op jit(solution)/shard_map/ppermute | solution.py:460
  23.8 0.0 collective-permute-done.6.refs_6_
  23.8 3.1 %attend.1 = (bf16[1,128,512]{2,1,0:T(8,128)(2,1)}, f32[256,128]{1,0:T(8,128)S(1)}, bf16[256,128]{1,0:T(8,128)(2,1)S(1)}, bf16[256,128]{1,0:T(8,128)(2,1)S(1)}, bf16[256,128]{1,0:T(8,128)(2,1)S(1)}) custom-call(bf16[1,128,512]{2,1,0:T(8,128)(2,1)S(1)} %copy-done.4, bf16[1,128,128]{2,1,0:T(8,128)(2,1)S(1)} %copy-done.2, bf16[1,128,128]{2,1,0:T(8,128)(2,1)S(1)} %copy-done.3, ...), custom_call_target="tpu_custom_call" | custom-call | tf_op jit(solution)/shard_map/attend/pallas_call | solution.py:465
  26.9 1.3 %collective-permute-start.12 = (bf16[256,128]{1,0:T(8,128)(2,1)S(1)}, bf16[256,128]{1,0:T(8,128)(2,1)S(1)}, u32[]{:S(2)}, u32[]{:S(2)}) collective-permute-start(bf16[256,128]{1,0:T(8,128)(2,1)S(1)} %get-tuple-element.37), channel_id=1, source_target_pairs={{1,0},{3,2},{5,4},{7,6},{9,8},{11,10},{13,12},{15,14},{17,16},{19,... | collective-permute-start | bytes 196616 | tf_op jit(solution)/shard_map/ppermute | solution.py:460
  28.2 1.3 %collective-permute-start.13 = (bf16[256,128]{1,0:T(8,128)(2,1)S(1)}, bf16[256,128]{1,0:T(8,128)(2,1)S(1)}, u32[]{:S(2)}, u32[]{:S(2)}) collective-permute-start(bf16[256,128]{1,0:T(8,128)(2,1)S(1)} %get-tuple-element.38), channel_id=1, source_target_pairs={{2,0},{3,1},{6,4},{7,5},{10,8},{11,9},{14,12},{15,13},{18,16},{19,... | collective-permute-start | bytes 196616 | tf_op jit(solution)/shard_map/ppermute | solution.py:460
  29.5 1.3 %collective-permute-start.14 = (bf16[256,128]{1,0:T(8,128)(2,1)S(1)}, bf16[256,128]{1,0:T(8,128)(2,1)S(1)}, u32[]{:S(2)}, u32[]{:S(2)}) collective-permute-start(bf16[256,128]{1,0:T(8,128)(2,1)S(1)} %get-tuple-element.39), channel_id=1, source_target_pairs={{2,1},{3,0},{6,5},{7,4},{10,9},{11,8},{14,13},{15,12},{18,17},{19,... | collective-permute-start | bytes 196616 | tf_op jit(solution)/shard_map/ppermute | solution.py:460
  30.8 0.0 collective-permute-done.8
  30.8 2.7 %collective-permute-start.9 = (f32[40,128]{1,0:T(8,128)S(1)}, f32[40,128]{1,0:T(8,128)S(1)}, u32[]{:S(2)}, u32[]{:S(2)}) collective-permute-start(f32[40,128]{1,0:T(8,128)S(1)} %add.13), channel_id=1, source_target_pairs={{0,16},{4,20},{8,24},{12,28},{16,0},{20,4},{24,8},{28,12},{1,17},{... | collective-permute-start | bytes 61448 | tf_op jit(solution)/shard_map/ppermute | solution.py:460
  33.5 2.1 %collective-permute-done.9 = f32[40,128]{1,0:T(8,128)S(1)} collective-permute-done((f32[40,128]{1,0:T(8,128)S(1)}, f32[40,128]{1,0:T(8,128)S(1)}, u32[]{:S(2)}, u32[]{:S(2)}) %collective-permute-start.9) | collective-permute-done | bytes 20512 | tf_op jit(solution)/shard_map/ppermute | solution.py:460
  35.6 2.6 %collective-permute-start.10 = (f32[40,128]{1,0:T(8,128)S(1)}, f32[40,128]{1,0:T(8,128)S(1)}, u32[]{:S(2)}, u32[]{:S(2)}) collective-permute-start(f32[40,128]{1,0:T(8,128)S(1)} %add.14), channel_id=1, source_target_pairs={{0,1},{1,0},{2,3},{3,2},{4,5},{5,4},{6,7},{7,6},{8,9},{9,8},{10,11... | collective-permute-start | bytes 61448 | tf_op jit(solution)/shard_map/ppermute | solution.py:460
  38.2 1.3 %collective-permute-start.3 = (f32[8,768]{1,0:T(8,128)S(1)}, f32[8,768]{1,0:T(8,128)S(1)}, u32[]{:S(2)}, u32[]{:S(2)}) collective-permute-start(f32[8,768]{1,0:T(8,128)S(1)} %get-tuple-element.33), channel_id=1, source_target_pairs={{1,0},{2,1},{3,2},{5,4},{6,5},{7,6},{9,8},{10,9},{11,10},{13,12},{... | collective-permute-start | bytes 73736 | tf_op jit(solution)/shard_map/ppermute | solution.py:501
  39.5 0.5 collective-permute-done.10
  40.0 4.1 %collective-permute-start.11 = (f32[40,128]{1,0:T(8,128)S(1)}, f32[40,128]{1,0:T(8,128)S(1)}, u32[]{:S(2)}, u32[]{:S(2)}) collective-permute-start(f32[40,128]{1,0:T(8,128)S(1)} %add.15.refs_5_), channel_id=1, source_target_pairs={{0,2},{1,3},{2,0},{3,1},{4,6},{5,7},{6,4},{7,5},{8,10},{9,11},{10,... | collective-permute-start | bytes 61448 | tf_op jit(solution)/shard_map/ppermute | solution.py:460
  44.1 0.0 collective-permute-done.12.refs_7_
  44.1 0.0 collective-permute-done.13.refs_8_
  44.2 1.7 %collective-permute-done.11.refs_6_ = f32[40,128]{1,0:T(8,128)S(1)} collective-permute-done((f32[40,128]{1,0:T(8,128)S(1)}, f32[40,128]{1,0:T(8,128)S(1)}, u32[]{:S(2)}, u32[]{:S(2)}) %collective-permute-start.11) | collective-permute-done | bytes 20512 | tf_op jit(solution)/shard_map/ppermute | solution.py:460
  45.9 1.5 %finish.1 = (bf16[1,128,768]{2,1,0:T(8,128)(2,1)}, bf16[1,128,128]{2,1,0:T(8,128)(2,1)}, bf16[1,128,128]{2,1,0:T(8,128)(2,1)}, f32[4,768]{1,0:T(4,128)}, f32[4]{0:T(128)}, /*index=5*/f32[4]{0:T(128)}, f32[4]{0:T(128)}) custom-call(bf16[1,128,768]{2,1,0:T(8,128)(2,1)} %get-tuple-element.31.refs_0_, ...), custom_call_target="tpu_custom_call", output_to_operand_aliasing={{0}: (0, {})} | custom-call | tf_op jit(solution)/shard_map/finish/pallas_call | solution.py:511
  (28 shorter events, 0.1 us)
Async XLA Ops:
  0.6 15.1 %copy-start = (bf16[1,128,768]{2,1,0:T(8,128)(2,1)S(1)}, bf16[1,128,768]{2,1,0:T(8,128)(2,1)}, u32[]{:S(2)}) copy-start(bf16[1,128,768]{2,1,0:T(8,128)(2,1)} %refs_0_.4) | copy-start | bytes 589828
  0.7 15.1 %copy-start.1 = (bf16[1,128,512]{2,1,0:T(8,128)(2,1)S(1)}, bf16[1,128,512]{2,1,0:T(8,128)(2,1)}, u32[]{:S(2)}) copy-start(bf16[1,128,512]{2,1,0:T(8,128)(2,1)} %refs_6_.1) | copy-start | bytes 393220
  0.7 15.1 %copy-start.6 = (f32[4,768]{1,0:T(4,128)S(1)}, f32[4,768]{1,0:T(4,128)}, u32[]{:S(2)}) copy-start(f32[4,768]{1,0:T(4,128)} %refs_3_.7) | copy-start | bytes 36868
  2.0 13.8 %copy-start.7 = (f32[1,128,4]{1,2,0:T(4,128)S(1)}, f32[1,128,4]{1,2,0:T(4,128)}, u32[]{:S(2)}) copy-start(f32[1,128,4]{1,2,0:T(4,128)} %param.12) | copy-start | bytes 6148
  2.0 10.7 %collective-permute-start = (bf16[672,128]{1,0:T(8,128)(2,1)S(1)}, bf16[672,128]{1,0:T(8,128)(2,1)S(1)}, u32[]{:S(2)}, u32[]{:S(2)}) collective-permute-start(bf16[672,128]{1,0:T(8,128)(2,1)S(1)} %get-tuple-element.29), channel_id=1, source_target_pairs={{0,1},{1,0},{2,3},{3,2},{4,5},{5,4},{6,7},{7,6},{8,9},{9,8},{10,11... | collective-permute-start | bytes 516104 | tf_op jit(solution)/shard_map/ppermute | solution.py:460
  5.0 10.8 %copy-start.8 = (f32[4]{0:T(128)S(1)}, f32[4]{0:T(128)}, u32[]{:S(2)}) copy-start(f32[4]{0:T(128)} %refs_3_.5) | copy-start | bytes 52
  5.0 10.8 %copy-start.9 = (f32[4]{0:T(128)S(1)}, f32[4]{0:T(128)}, u32[]{:S(2)}) copy-start(f32[4]{0:T(128)} %refs_4_.3) | copy-start | bytes 52
  5.0 10.8 %copy-start.10 = (f32[4]{0:T(128)S(1)}, f32[4]{0:T(128)}, u32[]{:S(2)}) copy-start(f32[4]{0:T(128)} %refs_5_.1) | copy-start | bytes 52
  5.0 10.1 %collective-permute-start.2 = (bf16[672,128]{1,0:T(8,128)(2,1)S(1)}, bf16[672,128]{1,0:T(8,128)(2,1)S(1)}, u32[]{:S(2)}, u32[]{:S(2)}) collective-permute-start(bf16[672,128]{1,0:T(8,128)(2,1)S(1)} %get-tuple-element.30), channel_id=1, source_target_pairs={{0,3},{1,2},{2,1},{3,0},{4,7},{5,6},{6,5},{7,4},{8,11},{9,10},{10,... | collective-permute-start | bytes 516104 | tf_op jit(solution)/shard_map/ppermute | solution.py:460
  6.5 9.2 %collective-permute-start.1 = (bf16[672,128]{1,0:T(8,128)(2,1)S(1)}, bf16[672,128]{1,0:T(8,128)(2,1)S(1)}, u32[]{:S(2)}, u32[]{:S(2)}) collective-permute-start(bf16[672,128]{1,0:T(8,128)(2,1)S(1)} %get-tuple-element.30), channel_id=1, source_target_pairs={{0,2},{1,3},{2,0},{3,1},{4,6},{5,7},{6,4},{7,5},{8,10},{9,11},{10,... | collective-permute-start | bytes 516104 | tf_op jit(solution)/shard_map/ppermute | solution.py:460
  6.6 17.2 %collective-permute-start.6 = (bf16[256,128]{1,0:T(8,128)(2,1)S(1)}, bf16[256,128]{1,0:T(8,128)(2,1)S(1)}, u32[]{:S(2)}, u32[]{:S(2)}) collective-permute-start(bf16[256,128]{1,0:T(8,128)(2,1)S(1)} %get-tuple-element.34), channel_id=1, source_target_pairs={{0,3},{1,2},{4,7},{5,6},{8,11},{9,10},{12,15},{13,14},{16,19},{17,... | collective-permute-start | bytes 196616 | tf_op jit(solution)/shard_map/ppermute | solution.py:460
  11.4 12.4 %collective-permute-start.5 = (bf16[256,128]{1,0:T(8,128)(2,1)S(1)}, bf16[256,128]{1,0:T(8,128)(2,1)S(1)}, u32[]{:S(2)}, u32[]{:S(2)}) collective-permute-start(bf16[256,128]{1,0:T(8,128)(2,1)S(1)} %get-tuple-element.34), channel_id=1, source_target_pairs={{0,2},{1,3},{4,6},{5,7},{8,10},{9,11},{12,14},{13,15},{16,18},{17,... | collective-permute-start | bytes 196616 | tf_op jit(solution)/shard_map/ppermute | solution.py:460
  12.7 11.1 %collective-permute-start.4 = (bf16[256,128]{1,0:T(8,128)(2,1)S(1)}, bf16[256,128]{1,0:T(8,128)(2,1)S(1)}, u32[]{:S(2)}, u32[]{:S(2)}) collective-permute-start(bf16[256,128]{1,0:T(8,128)(2,1)S(1)} %get-tuple-element.34), channel_id=1, source_target_pairs={{0,1},{2,3},{4,5},{6,7},{8,9},{10,11},{12,13},{14,15},{16,17},{18,... | collective-permute-start | bytes 196616 | tf_op jit(solution)/shard_map/ppermute | solution.py:460
  15.8 8.0 %copy-start.3 = (bf16[1,128,128]{2,1,0:T(8,128)(2,1)S(1)}, bf16[1,128,128]{2,1,0:T(8,128)(2,1)}, u32[]{:S(2)}) copy-start(bf16[1,128,128]{2,1,0:T(8,128)(2,1)} %refs_2_.5) | copy-start | bytes 98308
  15.8 8.0 %copy-start.4 = (bf16[1,128,512]{2,1,0:T(8,128)(2,1)S(1)}, bf16[1,128,512]{2,1,0:T(8,128)(2,1)}, u32[]{:S(2)}) copy-start(bf16[1,128,512]{2,1,0:T(8,128)(2,1)} %refs_0_.5) | copy-start | bytes 393220
  15.8 8.0 %copy-start.5 = (bf16[1,128,512]{2,1,0:T(8,128)(2,1)S(1)}, bf16[1,128,512]{2,1,0:T(8,128)(2,1)}, u32[]{:S(2)}) copy-start(bf16[1,128,512]{2,1,0:T(8,128)(2,1)} %refs_3_.6) | copy-start | bytes 393220
  20.9 2.9 %copy-start.2 = (bf16[1,128,128]{2,1,0:T(8,128)(2,1)S(1)}, bf16[1,128,128]{2,1,0:T(8,128)(2,1)}, u32[]{:S(2)}) copy-start(bf16[1,128,128]{2,1,0:T(8,128)(2,1)} %refs_1_.1) | copy-start | bytes 98308
  20.9 1.2 %collective-permute-start.7 = (f32[40,128]{1,0:T(8,128)S(1)}, f32[40,128]{1,0:T(8,128)S(1)}, u32[]{:S(2)}, u32[]{:S(2)}) collective-permute-start(f32[40,128]{1,0:T(8,128)S(1)} %get-tuple-element.36), channel_id=1, source_target_pairs={{0,4},{4,0},{8,12},{12,8},{16,20},{20,16},{24,28},{28,24},{1,5},{5... | collective-permute-start | bytes 61448 | tf_op jit(solution)/shard_map/ppermute | solution.py:460
  22.1 8.8 %collective-permute-start.8 = (f32[40,128]{1,0:T(8,128)S(1)}, f32[40,128]{1,0:T(8,128)S(1)}, u32[]{:S(2)}, u32[]{:S(2)}) collective-permute-start(f32[40,128]{1,0:T(8,128)S(1)} %add.12), channel_id=1, source_target_pairs={{0,8},{4,12},{8,0},{12,4},{16,24},{20,28},{24,16},{28,20},{1,9},{5... | collective-permute-start | bytes 61448 | tf_op jit(solution)/shard_map/ppermute | solution.py:460
  26.9 17.2 %collective-permute-start.12 = (bf16[256,128]{1,0:T(8,128)(2,1)S(1)}, bf16[256,128]{1,0:T(8,128)(2,1)S(1)}, u32[]{:S(2)}, u32[]{:S(2)}) collective-permute-start(bf16[256,128]{1,0:T(8,128)(2,1)S(1)} %get-tuple-element.37), channel_id=1, source_target_pairs={{1,0},{3,2},{5,4},{7,6},{9,8},{11,10},{13,12},{15,14},{17,16},{19,... | collective-permute-start | bytes 196616 | tf_op jit(solution)/shard_map/ppermute | solution.py:460
  28.2 15.9 %collective-permute-start.13 = (bf16[256,128]{1,0:T(8,128)(2,1)S(1)}, bf16[256,128]{1,0:T(8,128)(2,1)S(1)}, u32[]{:S(2)}, u32[]{:S(2)}) collective-permute-start(bf16[256,128]{1,0:T(8,128)(2,1)S(1)} %get-tuple-element.38), channel_id=1, source_target_pairs={{2,0},{3,1},{6,4},{7,5},{10,8},{11,9},{14,12},{15,13},{18,16},{19,... | collective-permute-start | bytes 196616 | tf_op jit(solution)/shard_map/ppermute | solution.py:460
  29.5 14.6 %collective-permute-start.14 = (bf16[256,128]{1,0:T(8,128)(2,1)S(1)}, bf16[256,128]{1,0:T(8,128)(2,1)S(1)}, u32[]{:S(2)}, u32[]{:S(2)}) collective-permute-start(bf16[256,128]{1,0:T(8,128)(2,1)S(1)} %get-tuple-element.39), channel_id=1, source_target_pairs={{2,1},{3,0},{6,5},{7,4},{10,9},{11,8},{14,13},{15,12},{18,17},{19,... | collective-permute-start | bytes 196616 | tf_op jit(solution)/shard_map/ppermute | solution.py:460
  30.8 4.7 %collective-permute-start.9 = (f32[40,128]{1,0:T(8,128)S(1)}, f32[40,128]{1,0:T(8,128)S(1)}, u32[]{:S(2)}, u32[]{:S(2)}) collective-permute-start(f32[40,128]{1,0:T(8,128)S(1)} %add.13), channel_id=1, source_target_pairs={{0,16},{4,20},{8,24},{12,28},{16,0},{20,4},{24,8},{28,12},{1,17},{... | collective-permute-start | bytes 61448 | tf_op jit(solution)/shard_map/ppermute | solution.py:460
  35.6 4.4 %collective-permute-start.10 = (f32[40,128]{1,0:T(8,128)S(1)}, f32[40,128]{1,0:T(8,128)S(1)}, u32[]{:S(2)}, u32[]{:S(2)}) collective-permute-start(f32[40,128]{1,0:T(8,128)S(1)} %add.14), channel_id=1, source_target_pairs={{0,1},{1,0},{2,3},{3,2},{4,5},{5,4},{6,7},{7,6},{8,9},{9,8},{10,11... | collective-permute-start | bytes 61448 | tf_op jit(solution)/shard_map/ppermute | solution.py:460
  38.2 5.9 %collective-permute-start.3 = (f32[8,768]{1,0:T(8,128)S(1)}, f32[8,768]{1,0:T(8,128)S(1)}, u32[]{:S(2)}, u32[]{:S(2)}) collective-permute-start(f32[8,768]{1,0:T(8,128)S(1)} %get-tuple-element.33), channel_id=1, source_target_pairs={{1,0},{2,1},{3,2},{5,4},{6,5},{7,6},{9,8},{10,9},{11,10},{13,12},{... | collective-permute-start | bytes 73736 | tf_op jit(solution)/shard_map/ppermute | solution.py:501
  40.0 5.9 %collective-permute-start.11 = (f32[40,128]{1,0:T(8,128)S(1)}, f32[40,128]{1,0:T(8,128)S(1)}, u32[]{:S(2)}, u32[]{:S(2)}) collective-permute-start(f32[40,128]{1,0:T(8,128)S(1)} %add.15.refs_5_), channel_id=1, source_target_pairs={{0,2},{1,3},{2,0},{3,1},{4,6},{5,7},{6,4},{7,5},{8,10},{9,11},{10,... | collective-permute-start | bytes 61448 | tf_op jit(solution)/shard_map/ppermute | solution.py:460
where the time goes:
time: 47.7 us; the launch traced here: 47.4 us
  starting transfers between devices  29.4 us (62%)
  Pallas kernels  10.9 us (23%)
  waiting for transfers between devices  6.1 us (13%)
  between operations  0.88 us (2%)
    ppermute x14, starting transfers between devices, swap(): return lax.ppermute(array, axis, pairs)  28.1 us
    ppermute x14, waiting for transfers between devices, swap(): return lax.ppermute(array, axis, pairs)  6.1 us
    pallas_call x1, Pallas kernels, on_device(): pl.pallas_call(lambda *refs: mixer_body(peers, *refs), out_shape=[shape(m...  5.03 us
    pallas_call x1, Pallas kernels, on_device(): pl.pallas_call(lambda *refs: attend_body(peers, *refs), out_shape=[shape(...  3.11 us
    pallas_call x1, Pallas kernels, on_device(): pl.pallas_call(lambda *refs: finish_body(peers, dp, *refs), out_shape=[sh...  1.45 us
    pallas_call x1, Pallas kernels, on_device(): pl.pallas_call(lambda *refs: pack_body(bits, *refs), out_shape=[shape((KV...  1.29 us
    ppermute x1, starting transfers between devices, on_device(): halo = lax.ppermute(first, 'ctx', [(i + 1, i) for i in range(ctx - 1)])  1.28 us
  transfers between devices with their start and end apart: 15, of which 5 were waited for; matrix products, arithmetic and copies ran while one was open for 0% of the time, Pallas kernels for 17%

commit v1 on v0

--- a/solution.py
+++ b/solution.py
@@ -13,6 +13,7 @@
 W = 128
 GROUPS = HEADS + 2
 KV_ROWS = 2 * W
+NEAR_ROWS = KV_ROWS + 32
 STEP_ROW = (HEADS + 1) * W
 EDGE_ROW = STEP_ROW + 16
 BULK_ROWS = EDGE_ROW + 16
@@ -57,6 +58,11 @@
 
 def cols(g):
     return slice(g * W, (g + 1) * W)
+
+
+def small_rows(rows):
+    rows = rows + [jnp.zeros((32 - 3 * GROUPS, W), F32)]
+    return jnp.concatenate(rows, axis=0).astype(BF16)
 
 
 def pack_body(bits, mixer, step, cotan, keys, values, near, *refs):
@@ -142,16 +148,14 @@
                 c.wait()
 
 
-def attend_body(peers, queries, keys, values, cotan, *refs):
-    near = refs[:peers]
-    query_grad, own, *parts = refs[peers:]
+def attend_heads(peers, heads, queries, keys, values, cotan, near, query_grad, sums):
     me = lax.axis_index("ctx")
     scale = W ** (-0.5)
     keys_all = jnp.concatenate([keys[0]] + [m[0:W, :] for m in near], axis=0)
     values_all = jnp.concatenate([values[0]] + [m[W : 2 * W, :] for m in near], axis=0)
     causal = iota2(0) >= iota2(1)
     rounded_heads, dscore_heads = [], []
-    for r in range(HEADS):
+    for r in heads:
         query = queries[0, :, cols(r)]
         cot = cotan[0, :, cols(r)]
         scores = dot(query, keys_all, NT) * (scale * LOG2E)
@@ -172,15 +176,34 @@
         query_grad[0, :, cols(r)] = dot(dscore, keys_all).astype(BF16)
         rounded_heads.append(rounded)
         dscore_heads.append(dscore)
-    query_rows = jnp.concatenate([queries[0, :, cols(r)] for r in range(HEADS)], axis=0)
-    cotan_rows = jnp.concatenate([cotan[0, :, cols(r)] for r in range(HEADS)], axis=0)
+    query_rows = jnp.concatenate([queries[0, :, cols(r)] for r in heads], axis=0)
+    cotan_rows = jnp.concatenate([cotan[0, :, cols(r)] for r in heads], axis=0)
     key_acc = dot(jnp.concatenate(dscore_heads, axis=0), query_rows, TN)
     value_acc = dot(jnp.concatenate(rounded_heads, axis=0), cotan_rows, TN)
+    if sums is not None:
+        key_acc, value_acc = key_acc + sums[0], value_acc + sums[1]
+    return key_acc, value_acc
+
+
+def half_body(peers, *refs):
+    near = refs[4 : 4 + peers]
+    query_grad, sums = refs[4 + peers :]
+    sums[0], sums[1] = attend_heads(peers, range(HEADS // 2), *refs[:4], near, query_grad, None)
+
+
+def attend_body(peers, *refs):
+    near = refs[4 : 4 + peers]
+    half, sums, halo, query_grad, own, *parts = refs[4 + peers :]
+    query_grad[0, :, 0 : HEADS // 2 * W] = half[0]
+    key_acc, value_acc = attend_heads(
+        peers, range(HEADS // 2, HEADS), *refs[:4], near, query_grad, sums
+    )
     own[0:W, :] = key_acc[0:W]
     own[W : 2 * W, :] = value_acc[0:W]
     for k in range(1, peers + 1):
         parts[k - 1][0:W, :] = key_acc[cols(k)].astype(BF16)
         parts[k - 1][W : 2 * W, :] = value_acc[cols(k)].astype(BF16)
+        parts[k - 1][KV_ROWS:NEAR_ROWS, :] = halo[...]
 
 
 def head_column(ref, lanes):
@@ -194,7 +217,7 @@
 def mixer_body(peers, *refs):
     mixer, step, weight, decay_log, bias, residual, cotan = refs[:7]
     bulk = refs[7 : 7 + peers]
-    input_grad, step_grad, edge, first, pay = refs[7 + peers : 12 + peers]
+    input_grad, step_grad, edge, halo, pay = refs[7 + peers : 12 + peers]
     tails, ext, grads, peer_ext, states, adjoints, acts, slopes = refs[12 + peers :]
     me = lax.axis_index("ctx")
     slots = peers + 1
@@ -364,10 +387,10 @@
     pay[32:36, :] = jnp.concatenate(skip_rows, axis=0)
     pay[36:40, :] = jnp.zeros((4, W), F32)
 
+    halo[...] = small_rows([grads[g, 0:8, :][0:3] for g in range(GROUPS)])
     for g in range(GROUPS):
         grads[g, W : W + 8, :] = jnp.zeros((8, W), F32)
         grad = grads[g, 0:W, :]
-        first[:, cols(g)] = grad[0:8]
         total = grads[g, TAPS - 1 : TAPS - 1 + W, :] * weight[0:1, cols(g)]
         for offset in range(1, TAPS):
             at = TAPS - 1 - offset
@@ -380,14 +403,17 @@
             )
 
 
-def finish_body(peers, count, *refs):
-    last, edge, halo, weight, own, total_a, total_b = refs[:7]
-    parts = refs[7 : 7 + peers]
-    input_grad, key_grad, value_grad, conv_grad, decay_grad, bias_grad, skip_grad = refs[7 + peers :]
-    del last
+def finish_body(peers, *refs):
+    partial, edge, weight, own = refs[:4]
+    parts = refs[4 : 4 + peers]
+    input_grad, key_grad, value_grad = refs[4 + peers :]
+    me = lax.axis_index("ctx")
     both = own[...]
-    for part in parts:
-        both = both + part[...].astype(F32)
+    halo = jnp.zeros((32, W), F32)
+    for k in range(1, peers + 1):
+        both = both + parts[k - 1][0:KV_ROWS, :].astype(F32)
+        after = jnp.bitwise_xor(me, k) == me + 1
+        halo = halo + jnp.where(after, parts[k - 1][KV_ROWS:NEAR_ROWS, :].astype(F32), 0.0)
     key_grad[0] = both[0:W].astype(BF16)
     value_grad[0] = both[W : 2 * W].astype(BF16)
     row = lax.broadcasted_iota(jnp.int32, (16, W), 0)
@@ -396,9 +422,13 @@
         for offset in range(TAPS - 1):
             for t in range(TAPS - 1 - offset):
                 at = 16 - (TAPS - 1 - offset) + t
-                piece = halo[t : t + 1, cols(g)] * weight[offset : offset + 1, cols(g)]
+                piece = halo[3 * g + t : 3 * g + t + 1] * weight[offset : offset + 1, cols(g)]
                 rows = rows + jnp.where(row == at, piece, 0.0)
-        input_grad[0, :, cols(g)] = rows.astype(BF16)
+        input_grad[0, 0 : W - 16, cols(g)] = partial[0, 0 : W - 16, cols(g)]
+        input_grad[0, W - 16 : W, cols(g)] = rows.astype(BF16)
+
+
+def total_body(count, total_a, total_b, conv_grad, decay_grad, bias_grad, skip_grad):
     total = (total_a[...] + total_b[...]) * (1.0 / count)
     for g in range(GROUPS):
         conv_grad[:, cols(g)] = total[4 * g : 4 * g + 4]
@@ -462,23 +492,13 @@
     nears = [swap(near, k, lambda i, j: j > i) for k in range(1, ctx)]
     bulks = [swap(bulk[k.bit_length() - 1], k) for k in range(1, ctx)]
 
-    query_grad, own, *parts = pl.pallas_call(
-        lambda *refs: attend_body(peers, *refs),
-        out_shape=[shape(queries.shape, BF16), shape((KV_ROWS, W), F32)]
-        + [shape((KV_ROWS, W), BF16)] * peers,
-        in_specs=[vmem] * (4 + peers),
-        out_specs=[vmem] * (2 + peers),
-        compiler_params=params,
-        name="attend",
-    )(queries, attn_keys, attn_values, attn_cotangent, *nears)
-
-    input_grad, step_grad, edge, first, pay = pl.pallas_call(
+    input_grad, step_grad, edge, halo, pay = pl.pallas_call(
         lambda *refs: mixer_body(peers, *refs),
         out_shape=[
             shape(mixer_input.shape, BF16),
             shape(step_input.shape, F32),
             shape((16, GROUPS * W), F32),
-            shape((8, GROUPS * W), F32),
+            shape((32, W), BF16),
             shape((PAY_ROWS, W), F32),
         ],
         in_specs=[vmem] * 3 + [smem] * 3 + [vmem] * (1 + peers),
@@ -497,8 +517,29 @@
         name="mixer",
     )(mixer_input, step_input, conv_weight, decay_log, step_bias, residual, mixer_cotangent, *bulks)
 
+    half, sums = pl.pallas_call(
+        lambda *refs: half_body(peers, *refs),
+        out_shape=[
+            shape((1, W, HEADS // 2 * W), BF16),
+            shape((2, ctx * W, W), F32),
+        ],
+        in_specs=[vmem] * (4 + peers),
+        out_specs=[vmem] * 2,
+        compiler_params=params,
+        name="half",
+    )(queries, attn_keys, attn_values, attn_cotangent, *nears)
+
+    query_grad, own, *parts = pl.pallas_call(
+        lambda *refs: attend_body(peers, *refs),
+        out_shape=[shape(queries.shape, BF16), shape((KV_ROWS, W), F32)]
+        + [shape((NEAR_ROWS, W), BF16)] * peers,
+        in_specs=[vmem] * (7 + peers),
+        out_specs=[vmem] * (2 + peers),
+        compiler_params=params,
+        name="attend",
+    )(queries, attn_keys, attn_values, attn_cotangent, *nears, half, sums, halo)
+
     returned = [swap(parts[k - 1], k, lambda i, j: j < i) for k in range(1, ctx)]
-    halo = lax.ppermute(first, "ctx", [(i + 1, i) for i in range(ctx - 1)])
     stages = [("dp", 1 << b) for b in range(dp.bit_length() - 1)]
     stages += [("ctx", 1 << b) for b in range(bits)]
     for n, (axis, k) in enumerate(stages):
@@ -506,24 +547,26 @@
         if n + 1 < len(stages):
             pay = pay + other
 
-    blocks = mixer_input.shape[1] // 16
-    last = pl.BlockSpec((1, 16, GROUPS * W), lambda i: (0, blocks - 1, 0))
-    input_grad, key_grad, value_grad, conv_grad, decay_grad, bias_grad, skip_grad = pl.pallas_call(
-        lambda *refs: finish_body(peers, dp, *refs),
+    input_grad, key_grad, value_grad = pl.pallas_call(
+        lambda *refs: finish_body(peers, *refs),
         out_shape=[
             shape(mixer_input.shape, BF16),
             shape(attn_keys.shape, BF16),
             shape(attn_values.shape, BF16),
-            shape(conv_weight.shape, F32),
-        ]
-        + [shape((HEADS,), F32)] * 3,
-        grid=(1,),
-        in_specs=[last] + [vmem] * (6 + peers),
-        out_specs=[last] + [vmem] * 3 + [smem] * 3,
-        input_output_aliases={0: 0},
-        compiler_params=pltpu.CompilerParams(vmem_limit_bytes=LIMIT),
+        ],
+        in_specs=[vmem] * (4 + peers),
+        out_specs=[vmem] * 3,
+        compiler_params=params,
         name="finish",
-    )(input_grad, edge, halo, conv_weight, own, pay, other, *returned)
+    )(input_grad, edge, conv_weight, own, *returned)
+    conv_grad, decay_grad, bias_grad, skip_grad = pl.pallas_call(
+        lambda *refs: total_body(dp, *refs),
+        out_shape=[shape(conv_weight.shape, F32)] + [shape((HEADS,), F32)] * 3,
+        in_specs=[vmem] * 2,
+        out_specs=[vmem] + [smem] * 3,
+        compiler_params=params,
+        name="total",
+    )(pay, other)
     return (
         input_grad,
         jnp.swapaxes(step_grad, 1, 2),

time: 47.7 us -> 47.2 us (0.990)
  starting transfers between devices: 29.4 us -> 28.1 us
  waiting for transfers between devices: 6.1 us -> 6.65 us
    pallas_call x1 -> x3, Pallas kernels: 1.45 us -> 2.86 us  [the longest x1 1.46 us: on_device(): pl.pallas_call(lambda *refs: half_body(peers, *refs), out_shape=[shape((1...]
    ppermute x1 -> x0, starting transfers between devices: 1.28 us -> none  [on_device(): halo = lax.ppermute(first, 'ctx', [(i + 1, i) for i in range(ctx - 1)])]
    pallas_call x1, Pallas kernels: 3.11 us -> 2.06 us  [on_device(): pl.pallas_call(lambda *refs: attend_body(peers, *refs), out_shape=[shape(...]
    ppermute x14, waiting for transfers between devices: 6.1 us -> 6.65 us  [swap(): return lax.ppermute(array, axis, pairs)]
  transfers between devices with their start and end apart: 15 -> 14, of which waited for: 5 -> 5; matrix products, arithmetic and copies ran while one was open for 0% -> 0% of each run, Pallas kernels for 17% -> 20%
where the time goes in v1:
time: 47.2 us; the launch traced here: 46.9 us
  starting transfers between devices  28.1 us (60%)
  Pallas kernels  11.2 us (24%)
  waiting for transfers between devices  6.65 us (14%)
  between operations  0.87 us (2%)
    ppermute x14, starting transfers between devices, swap(): return lax.ppermute(array, axis, pairs)  28.1 us
    ppermute x14, waiting for transfers between devices, swap(): return lax.ppermute(array, axis, pairs)  6.65 us
    pallas_call x1, Pallas kernels, on_device(): pl.pallas_call(lambda *refs: mixer_body(peers, *refs), out_shape=[shape(m...  5.04 us
    pallas_call x1, Pallas kernels, on_device(): pl.pallas_call(lambda *refs: attend_body(peers, *refs), out_shape=[shape(...  2.06 us
    pallas_call x1, Pallas kernels, on_device(): pl.pallas_call(lambda *refs: half_body(peers, *refs), out_shape=[shape((1...  1.46 us
    pallas_call x1, Pallas kernels, on_device(): pl.pallas_call(lambda *refs: pack_body(bits, *refs), out_shape=[shape((KV...  1.29 us
  transfers between devices with their start and end apart: 14, of which 5 were waited for; matrix products, arithmetic and copies ran while one was open for 0% of the time, Pallas kernels for 20%

profile of v1, /device:TPU:0, one launch (start us, length us, event | category | flops | bytes accessed | tf_op | source)
XLA Modules:
  0.0 46.9 jit_solution(14239598736646364968)
XLA Ops:
  0.7 1.3 %pack.1 = (bf16[256,128]{1,0:T(8,128)(2,1)S(1)}, bf16[672,128]{1,0:T(8,128)(2,1)S(1)}, bf16[672,128]{1,0:T(8,128)(2,1)S(1)}) custom-call(bf16[1,128,768]{2,1,0:T(8,128)(2,1)} %refs_0_.5, f32[1,4,128]{2,1,0:T(4,128)} %bitcast.2, bf16[1,128,512]{2,1,0:T(8,128)(2,1)} %refs_6_.1, bf16[1,128,128]{2,1,0:T(8,128)(2,1)} %refs_1_.3, bf16[1,128,128]{2,1,0:T(8,128)(2,1)} %refs_2_.8), custom_call_target="tpu_custom_call" | custom-call | tf_op jit(solution)/shard_map/pack/pallas_call | solution.py:469
  2.0 0.0 copy-start.7
  2.0 3.0 %collective-permute-start = (bf16[672,128]{1,0:T(8,128)(2,1)S(1)}, bf16[672,128]{1,0:T(8,128)(2,1)S(1)}, u32[]{:S(2)}, u32[]{:S(2)}) collective-permute-start(bf16[672,128]{1,0:T(8,128)(2,1)S(1)} %get-tuple-element.31), channel_id=1, source_target_pairs={{0,1},{1,0},{2,3},{3,2},{4,5},{5,4},{6,7},{7,6},{8,9},{9,8},{10,11... | collective-permute-start | bytes 516104 | tf_op jit(solution)/shard_map/ppermute | solution.py:490
  5.0 1.5 %collective-permute-start.2 = (bf16[672,128]{1,0:T(8,128)(2,1)S(1)}, bf16[672,128]{1,0:T(8,128)(2,1)S(1)}, u32[]{:S(2)}, u32[]{:S(2)}) collective-permute-start(bf16[672,128]{1,0:T(8,128)(2,1)S(1)} %get-tuple-element.32), channel_id=1, source_target_pairs={{0,3},{1,2},{2,1},{3,0},{4,7},{5,6},{6,5},{7,4},{8,11},{9,10},{10,... | collective-permute-start | bytes 516104 | tf_op jit(solution)/shard_map/ppermute | solution.py:490
  6.5 0.1 collective-permute-start.1
  6.6 4.7 %collective-permute-start.5 = (bf16[256,128]{1,0:T(8,128)(2,1)S(1)}, bf16[256,128]{1,0:T(8,128)(2,1)S(1)}, u32[]{:S(2)}, u32[]{:S(2)}) collective-permute-start(bf16[256,128]{1,0:T(8,128)(2,1)S(1)} %get-tuple-element.35), channel_id=1, source_target_pairs={{0,3},{1,2},{4,7},{5,6},{8,11},{9,10},{12,15},{13,14},{16,19},{17,... | collective-permute-start | bytes 196616 | tf_op jit(solution)/shard_map/ppermute | solution.py:490
  11.4 1.3 %collective-permute-start.4 = (bf16[256,128]{1,0:T(8,128)(2,1)S(1)}, bf16[256,128]{1,0:T(8,128)(2,1)S(1)}, u32[]{:S(2)}, u32[]{:S(2)}) collective-permute-start(bf16[256,128]{1,0:T(8,128)(2,1)S(1)} %get-tuple-element.35), channel_id=1, source_target_pairs={{0,2},{1,3},{4,6},{5,7},{8,10},{9,11},{12,14},{13,15},{16,18},{17,... | collective-permute-start | bytes 196616 | tf_op jit(solution)/shard_map/ppermute | solution.py:490
  12.7 2.5 %collective-permute-start.3 = (bf16[256,128]{1,0:T(8,128)(2,1)S(1)}, bf16[256,128]{1,0:T(8,128)(2,1)S(1)}, u32[]{:S(2)}, u32[]{:S(2)}) collective-permute-start(bf16[256,128]{1,0:T(8,128)(2,1)S(1)} %get-tuple-element.35), channel_id=1, source_target_pairs={{0,1},{2,3},{4,5},{6,7},{8,9},{10,11},{12,13},{14,15},{16,17},{18,... | collective-permute-start | bytes 196616 | tf_op jit(solution)/shard_map/ppermute | solution.py:490
  15.2 0.6 %collective-permute-done.1.refs_8_ = bf16[672,128]{1,0:T(8,128)(2,1)S(1)} collective-permute-done((bf16[672,128]{1,0:T(8,128)(2,1)S(1)}, bf16[672,128]{1,0:T(8,128)(2,1)S(1)}, u32[]{:S(2)}, u32[]{:S(2)}) %collective-permute-start.1) | collective-permute-done | bytes 172064 | tf_op jit(solution)/shard_map/ppermute | solution.py:490
  15.8 0.0 copy-start.2
  15.8 0.0 copy-start.3
  15.8 0.0 copy-start.5
  15.8 5.0 %mixer.1 = (bf16[1,128,768]{2,1,0:T(8,128)(2,1)S(1)}, f32[1,4,128]{2,1,0:T(4,128)}, f32[16,768]{1,0:T(8,128)S(1)}, bf16[32,128]{1,0:T(8,128)(2,1)S(1)}, f32[40,128]{1,0:T(8,128)S(1)}) custom-call(bf16[1,128,768]{2,1,0:T(8,128)(2,1)S(1)} %copy-done, f32[1,4,128]{2,1,0:T(4,128)S(1)} %bitcast.3, f32[4,768]{1,0:T(4,128)S(1)} %copy-done.6, f32[4]{0:T(128)S(1)} %copy-done.8, ...), custom_call_target="tpu_custom_call" | custom-call | tf_op jit(solution)/shard_map/mixer/pallas_call | solution.py:495
  20.9 0.0 collective-permute-start.9
  20.9 1.2 %collective-permute-done.9 = f32[40,128]{1,0:T(8,128)S(1)} collective-permute-done((f32[40,128]{1,0:T(8,128)S(1)}, f32[40,128]{1,0:T(8,128)S(1)}, u32[]{:S(2)}, u32[]{:S(2)}) %collective-permute-start.9) | collective-permute-done | bytes 20512 | tf_op jit(solution)/shard_map/ppermute | solution.py:490
  22.1 1.7 %collective-permute-start.10 = (f32[40,128]{1,0:T(8,128)S(1)}, f32[40,128]{1,0:T(8,128)S(1)}, u32[]{:S(2)}, u32[]{:S(2)}) collective-permute-start(f32[40,128]{1,0:T(8,128)S(1)} %add.12), channel_id=1, source_target_pairs={{0,8},{4,12},{8,0},{12,4},{16,24},{20,28},{24,16},{28,20},{1,9},{5... | collective-permute-start | bytes 61448 | tf_op jit(solution)/shard_map/ppermute | solution.py:490
  23.8 0.0 collective-permute-done.5.refs_6_
  23.8 0.0 collective-permute-done.4.refs_5_
  23.8 0.0 collective-permute-done.3.refs_4_
  23.8 1.5 %half.1 = (bf16[1,128,256]{2,1,0:T(8,128)(2,1)S(1)}, f32[2,512,128]{2,1,0:T(8,128)S(1)}) custom-call(bf16[1,128,512]{2,1,0:T(8,128)(2,1)S(1)} %copy-done.2, bf16[1,128,128]{2,1,0:T(8,128)(2,1)S(1)} %copy-done.4, bf16[1,128,128]{2,1,0:T(8,128)(2,1)S(1)} %copy-done.5, bf16[1,128,512]{2,1,0:T(8,128)(2,1)S(1)} %copy-done.3, ...), custom_call_target="tpu_custom_call" | custom-call | tf_op jit(solution)/shard_map/half/pallas_call | solution.py:520
  25.3 2.1 %attend.1 = (bf16[1,128,512]{2,1,0:T(8,128)(2,1)}, f32[256,128]{1,0:T(8,128)S(1)}, bf16[288,128]{1,0:T(8,128)(2,1)S(1)}, bf16[288,128]{1,0:T(8,128)(2,1)S(1)}, bf16[288,128]{1,0:T(8,128)(2,1)S(1)}) custom-call(bf16[1,128,512]{2,1,0:T(8,128)(2,1)S(1)} %copy-done.2, bf16[1,128,128]{2,1,0:T(8,128)(2,1)S(1)} %copy-done.4, bf16[1,128,128]{2,1,0:T(8,128)(2,1)S(1)} %copy-done.5, ...), custom_call_target="tpu_custom_call" | custom-call | tf_op jit(solution)/shard_map/attend/pallas_call | solution.py:532
  27.3 1.3 %collective-permute-start.6 = (bf16[288,128]{1,0:T(8,128)(2,1)S(1)}, bf16[288,128]{1,0:T(8,128)(2,1)S(1)}, u32[]{:S(2)}, u32[]{:S(2)}) collective-permute-start(bf16[288,128]{1,0:T(8,128)(2,1)S(1)} %get-tuple-element.40), channel_id=1, source_target_pairs={{1,0},{3,2},{5,4},{7,6},{9,8},{11,10},{13,12},{15,14},{17,16},{19,... | collective-permute-start | bytes 221192 | tf_op jit(solution)/shard_map/ppermute | solution.py:490
  28.6 1.3 %collective-permute-start.7 = (bf16[288,128]{1,0:T(8,128)(2,1)S(1)}, bf16[288,128]{1,0:T(8,128)(2,1)S(1)}, u32[]{:S(2)}, u32[]{:S(2)}) collective-permute-start(bf16[288,128]{1,0:T(8,128)(2,1)S(1)} %get-tuple-element.41), channel_id=1, source_target_pairs={{2,0},{3,1},{6,4},{7,5},{10,8},{11,9},{14,12},{15,13},{18,16},{19,... | collective-permute-start | bytes 221192 | tf_op jit(solution)/shard_map/ppermute | solution.py:490
  29.9 1.3 %collective-permute-start.8 = (bf16[288,128]{1,0:T(8,128)(2,1)S(1)}, bf16[288,128]{1,0:T(8,128)(2,1)S(1)}, u32[]{:S(2)}, u32[]{:S(2)}) collective-permute-start(bf16[288,128]{1,0:T(8,128)(2,1)S(1)} %get-tuple-element.42), channel_id=1, source_target_pairs={{2,1},{3,0},{6,5},{7,4},{10,9},{11,8},{14,13},{15,12},{18,17},{19,... | collective-permute-start | bytes 221192 | tf_op jit(solution)/shard_map/ppermute | solution.py:490
  31.3 2.7 %collective-permute-start.11 = (f32[40,128]{1,0:T(8,128)S(1)}, f32[40,128]{1,0:T(8,128)S(1)}, u32[]{:S(2)}, u32[]{:S(2)}) collective-permute-start(f32[40,128]{1,0:T(8,128)S(1)} %add.13), channel_id=1, source_target_pairs={{0,16},{4,20},{8,24},{12,28},{16,0},{20,4},{24,8},{28,12},{1,17},{... | collective-permute-start | bytes 61448 | tf_op jit(solution)/shard_map/ppermute | solution.py:490
  33.9 2.1 %collective-permute-done.11 = f32[40,128]{1,0:T(8,128)S(1)} collective-permute-done((f32[40,128]{1,0:T(8,128)S(1)}, f32[40,128]{1,0:T(8,128)S(1)}, u32[]{:S(2)}, u32[]{:S(2)}) %collective-permute-start.11) | collective-permute-done | bytes 20512 | tf_op jit(solution)/shard_map/ppermute | solution.py:490
  36.0 2.6 %collective-permute-start.12 = (f32[40,128]{1,0:T(8,128)S(1)}, f32[40,128]{1,0:T(8,128)S(1)}, u32[]{:S(2)}, u32[]{:S(2)}) collective-permute-start(f32[40,128]{1,0:T(8,128)S(1)} %add.14), channel_id=1, source_target_pairs={{0,1},{1,0},{2,3},{3,2},{4,5},{5,4},{6,7},{7,6},{8,9},{9,8},{10,11... | collective-permute-start | bytes 61448 | tf_op jit(solution)/shard_map/ppermute | solution.py:490
  38.7 1.8 %collective-permute-done.12 = f32[40,128]{1,0:T(8,128)S(1)} collective-permute-done((f32[40,128]{1,0:T(8,128)S(1)}, f32[40,128]{1,0:T(8,128)S(1)}, u32[]{:S(2)}, u32[]{:S(2)}) %collective-permute-start.12) | collective-permute-done | bytes 20512 | tf_op jit(solution)/shard_map/ppermute | solution.py:490
  40.4 4.1 %collective-permute-start.13 = (f32[40,128]{1,0:T(8,128)S(1)}, f32[40,128]{1,0:T(8,128)S(1)}, u32[]{:S(2)}, u32[]{:S(2)}) collective-permute-start(f32[40,128]{1,0:T(8,128)S(1)} %add.15.refs_0_), channel_id=1, source_target_pairs={{0,2},{1,3},{2,0},{3,1},{4,6},{5,7},{6,4},{7,5},{8,10},{9,11},{10,... | collective-permute-start | bytes 61448 | tf_op jit(solution)/shard_map/ppermute | solution.py:490
  44.5 0.7 %finish.1 = (bf16[1,128,768]{2,1,0:T(8,128)(2,1)}, bf16[1,128,128]{2,1,0:T(8,128)(2,1)}, bf16[1,128,128]{2,1,0:T(8,128)(2,1)}) custom-call(bf16[1,128,768]{2,1,0:T(8,128)(2,1)S(1)} %get-tuple-element.33.refs_0_, f32[16,768]{1,0:T(8,128)S(1)} %get-tuple-element.34.refs_1_, f32[4,768]{1,0:T(4,128)S(1)} %copy-done.6, f32[256,128]{1,0:T(8,128)S(1)} %get-tuple-element.39.refs_3_, ...), custom_call_target="tpu_custom_call" | custom-call | tf_op jit(solution)/shard_map/finish/pallas_call | solution.py:550
  45.3 1.0 %collective-permute-done.13.refs_1_ = f32[40,128]{1,0:T(8,128)S(1)} collective-permute-done((f32[40,128]{1,0:T(8,128)S(1)}, f32[40,128]{1,0:T(8,128)S(1)}, u32[]{:S(2)}, u32[]{:S(2)}) %collective-permute-start.13) | collective-permute-done | bytes 20512 | tf_op jit(solution)/shard_map/ppermute | solution.py:490
  46.3 0.7 %total.1 = (f32[4,768]{1,0:T(4,128)}, f32[4]{0:T(128)}, f32[4]{0:T(128)}, f32[4]{0:T(128)}) custom-call(f32[40,128]{1,0:T(8,128)S(1)} %add.15.refs_0_, f32[40,128]{1,0:T(8,128)S(1)} %collective-permute-done.13.refs_1_), custom_call_target="tpu_custom_call" | custom-call | tf_op jit(solution)/shard_map/total/pallas_call | solution.py:562
  (28 shorter events, 0.1 us)
Async XLA Ops:
  0.6 15.1 %copy-start = (bf16[1,128,768]{2,1,0:T(8,128)(2,1)S(1)}, bf16[1,128,768]{2,1,0:T(8,128)(2,1)}, u32[]{:S(2)}) copy-start(bf16[1,128,768]{2,1,0:T(8,128)(2,1)} %refs_0_.5) | copy-start | bytes 589828
  0.7 15.1 %copy-start.1 = (bf16[1,128,512]{2,1,0:T(8,128)(2,1)S(1)}, bf16[1,128,512]{2,1,0:T(8,128)(2,1)}, u32[]{:S(2)}) copy-start(bf16[1,128,512]{2,1,0:T(8,128)(2,1)} %refs_6_.1) | copy-start | bytes 393220
  0.7 15.1 %copy-start.6 = (f32[4,768]{1,0:T(4,128)S(1)}, f32[4,768]{1,0:T(4,128)}, u32[]{:S(2)}) copy-start(f32[4,768]{1,0:T(4,128)} %refs_2_.9) | copy-start | bytes 36868
  2.0 13.8 %copy-start.7 = (f32[1,128,4]{1,2,0:T(4,128)S(1)}, f32[1,128,4]{1,2,0:T(4,128)}, u32[]{:S(2)}) copy-start(f32[1,128,4]{1,2,0:T(4,128)} %param.12) | copy-start | bytes 6148
  2.0 10.7 %collective-permute-start = (bf16[672,128]{1,0:T(8,128)(2,1)S(1)}, bf16[672,128]{1,0:T(8,128)(2,1)S(1)}, u32[]{:S(2)}, u32[]{:S(2)}) collective-permute-start(bf16[672,128]{1,0:T(8,128)(2,1)S(1)} %get-tuple-element.31), channel_id=1, source_target_pairs={{0,1},{1,0},{2,3},{3,2},{4,5},{5,4},{6,7},{7,6},{8,9},{9,8},{10,11... | collective-permute-start | bytes 516104 | tf_op jit(solution)/shard_map/ppermute | solution.py:490
  5.0 10.8 %copy-start.8 = (f32[4]{0:T(128)S(1)}, f32[4]{0:T(128)}, u32[]{:S(2)}) copy-start(f32[4]{0:T(128)} %refs_3_.5) | copy-start | bytes 52
  5.0 10.8 %copy-start.9 = (f32[4]{0:T(128)S(1)}, f32[4]{0:T(128)}, u32[]{:S(2)}) copy-start(f32[4]{0:T(128)} %refs_4_.3) | copy-start | bytes 52
  5.0 10.8 %copy-start.10 = (f32[4]{0:T(128)S(1)}, f32[4]{0:T(128)}, u32[]{:S(2)}) copy-start(f32[4]{0:T(128)} %refs_5_.1) | copy-start | bytes 52
  5.0 10.1 %collective-permute-start.2 = (bf16[672,128]{1,0:T(8,128)(2,1)S(1)}, bf16[672,128]{1,0:T(8,128)(2,1)S(1)}, u32[]{:S(2)}, u32[]{:S(2)}) collective-permute-start(bf16[672,128]{1,0:T(8,128)(2,1)S(1)} %get-tuple-element.32), channel_id=1, source_target_pairs={{0,3},{1,2},{2,1},{3,0},{4,7},{5,6},{6,5},{7,4},{8,11},{9,10},{10,... | collective-permute-start | bytes 516104 | tf_op jit(solution)/shard_map/ppermute | solution.py:490
  6.5 9.2 %collective-permute-start.1 = (bf16[672,128]{1,0:T(8,128)(2,1)S(1)}, bf16[672,128]{1,0:T(8,128)(2,1)S(1)}, u32[]{:S(2)}, u32[]{:S(2)}) collective-permute-start(bf16[672,128]{1,0:T(8,128)(2,1)S(1)} %get-tuple-element.32), channel_id=1, source_target_pairs={{0,2},{1,3},{2,0},{3,1},{4,6},{5,7},{6,4},{7,5},{8,10},{9,11},{10,... | collective-permute-start | bytes 516104 | tf_op jit(solution)/shard_map/ppermute | solution.py:490
  6.6 17.2 %collective-permute-start.5 = (bf16[256,128]{1,0:T(8,128)(2,1)S(1)}, bf16[256,128]{1,0:T(8,128)(2,1)S(1)}, u32[]{:S(2)}, u32[]{:S(2)}) collective-permute-start(bf16[256,128]{1,0:T(8,128)(2,1)S(1)} %get-tuple-element.35), channel_id=1, source_target_pairs={{0,3},{1,2},{4,7},{5,6},{8,11},{9,10},{12,15},{13,14},{16,19},{17,... | collective-permute-start | bytes 196616 | tf_op jit(solution)/shard_map/ppermute | solution.py:490
  11.4 12.4 %collective-permute-start.4 = (bf16[256,128]{1,0:T(8,128)(2,1)S(1)}, bf16[256,128]{1,0:T(8,128)(2,1)S(1)}, u32[]{:S(2)}, u32[]{:S(2)}) collective-permute-start(bf16[256,128]{1,0:T(8,128)(2,1)S(1)} %get-tuple-element.35), channel_id=1, source_target_pairs={{0,2},{1,3},{4,6},{5,7},{8,10},{9,11},{12,14},{13,15},{16,18},{17,... | collective-permute-start | bytes 196616 | tf_op jit(solution)/shard_map/ppermute | solution.py:490
  12.7 11.1 %collective-permute-start.3 = (bf16[256,128]{1,0:T(8,128)(2,1)S(1)}, bf16[256,128]{1,0:T(8,128)(2,1)S(1)}, u32[]{:S(2)}, u32[]{:S(2)}) collective-permute-start(bf16[256,128]{1,0:T(8,128)(2,1)S(1)} %get-tuple-element.35), channel_id=1, source_target_pairs={{0,1},{2,3},{4,5},{6,7},{8,9},{10,11},{12,13},{14,15},{16,17},{18,... | collective-permute-start | bytes 196616 | tf_op jit(solution)/shard_map/ppermute | solution.py:490
  15.8 8.0 %copy-start.2 = (bf16[1,128,512]{2,1,0:T(8,128)(2,1)S(1)}, bf16[1,128,512]{2,1,0:T(8,128)(2,1)}, u32[]{:S(2)}) copy-start(bf16[1,128,512]{2,1,0:T(8,128)(2,1)} %refs_0_.7) | copy-start | bytes 393220
  15.8 8.0 %copy-start.3 = (bf16[1,128,512]{2,1,0:T(8,128)(2,1)S(1)}, bf16[1,128,512]{2,1,0:T(8,128)(2,1)}, u32[]{:S(2)}) copy-start(bf16[1,128,512]{2,1,0:T(8,128)(2,1)} %refs_3_.7) | copy-start | bytes 393220
  15.8 8.0 %copy-start.5 = (bf16[1,128,128]{2,1,0:T(8,128)(2,1)S(1)}, bf16[1,128,128]{2,1,0:T(8,128)(2,1)}, u32[]{:S(2)}) copy-start(bf16[1,128,128]{2,1,0:T(8,128)(2,1)} %refs_2_.8) | copy-start | bytes 98308
  20.9 2.9 %copy-start.4 = (bf16[1,128,128]{2,1,0:T(8,128)(2,1)S(1)}, bf16[1,128,128]{2,1,0:T(8,128)(2,1)}, u32[]{:S(2)}) copy-start(bf16[1,128,128]{2,1,0:T(8,128)(2,1)} %refs_1_.3) | copy-start | bytes 98308
  20.9 1.2 %collective-permute-start.9 = (f32[40,128]{1,0:T(8,128)S(1)}, f32[40,128]{1,0:T(8,128)S(1)}, u32[]{:S(2)}, u32[]{:S(2)}) collective-permute-start(f32[40,128]{1,0:T(8,128)S(1)} %get-tuple-element.45), channel_id=1, source_target_pairs={{0,4},{4,0},{8,12},{12,8},{16,20},{20,16},{24,28},{28,24},{1,5},{5... | collective-permute-start | bytes 61448 | tf_op jit(solution)/shard_map/ppermute | solution.py:490
  22.1 9.2 %collective-permute-start.10 = (f32[40,128]{1,0:T(8,128)S(1)}, f32[40,128]{1,0:T(8,128)S(1)}, u32[]{:S(2)}, u32[]{:S(2)}) collective-permute-start(f32[40,128]{1,0:T(8,128)S(1)} %add.12), channel_id=1, source_target_pairs={{0,8},{4,12},{8,0},{12,4},{16,24},{20,28},{24,16},{28,20},{1,9},{5... | collective-permute-start | bytes 61448 | tf_op jit(solution)/shard_map/ppermute | solution.py:490
  27.3 17.2 %collective-permute-start.6 = (bf16[288,128]{1,0:T(8,128)(2,1)S(1)}, bf16[288,128]{1,0:T(8,128)(2,1)S(1)}, u32[]{:S(2)}, u32[]{:S(2)}) collective-permute-start(bf16[288,128]{1,0:T(8,128)(2,1)S(1)} %get-tuple-element.40), channel_id=1, source_target_pairs={{1,0},{3,2},{5,4},{7,6},{9,8},{11,10},{13,12},{15,14},{17,16},{19,... | collective-permute-start | bytes 221192 | tf_op jit(solution)/shard_map/ppermute | solution.py:490
  28.6 15.9 %collective-permute-start.7 = (bf16[288,128]{1,0:T(8,128)(2,1)S(1)}, bf16[288,128]{1,0:T(8,128)(2,1)S(1)}, u32[]{:S(2)}, u32[]{:S(2)}) collective-permute-start(bf16[288,128]{1,0:T(8,128)(2,1)S(1)} %get-tuple-element.41), channel_id=1, source_target_pairs={{2,0},{3,1},{6,4},{7,5},{10,8},{11,9},{14,12},{15,13},{18,16},{19,... | collective-permute-start | bytes 221192 | tf_op jit(solution)/shard_map/ppermute | solution.py:490
  29.9 14.6 %collective-permute-start.8 = (bf16[288,128]{1,0:T(8,128)(2,1)S(1)}, bf16[288,128]{1,0:T(8,128)(2,1)S(1)}, u32[]{:S(2)}, u32[]{:S(2)}) collective-permute-start(bf16[288,128]{1,0:T(8,128)(2,1)S(1)} %get-tuple-element.42), channel_id=1, source_target_pairs={{2,1},{3,0},{6,5},{7,4},{10,9},{11,8},{14,13},{15,12},{18,17},{19,... | collective-permute-start | bytes 221192 | tf_op jit(solution)/shard_map/ppermute | solution.py:490
  31.3 4.7 %collective-permute-start.11 = (f32[40,128]{1,0:T(8,128)S(1)}, f32[40,128]{1,0:T(8,128)S(1)}, u32[]{:S(2)}, u32[]{:S(2)}) collective-permute-start(f32[40,128]{1,0:T(8,128)S(1)} %add.13), channel_id=1, source_target_pairs={{0,16},{4,20},{8,24},{12,28},{16,0},{20,4},{24,8},{28,12},{1,17},{... | collective-permute-start | bytes 61448 | tf_op jit(solution)/shard_map/ppermute | solution.py:490
  36.0 4.4 %collective-permute-start.12 = (f32[40,128]{1,0:T(8,128)S(1)}, f32[40,128]{1,0:T(8,128)S(1)}, u32[]{:S(2)}, u32[]{:S(2)}) collective-permute-start(f32[40,128]{1,0:T(8,128)S(1)} %add.14), channel_id=1, source_target_pairs={{0,1},{1,0},{2,3},{3,2},{4,5},{5,4},{6,7},{7,6},{8,9},{9,8},{10,11... | collective-permute-start | bytes 61448 | tf_op jit(solution)/shard_map/ppermute | solution.py:490
  40.4 5.9 %collective-permute-start.13 = (f32[40,128]{1,0:T(8,128)S(1)}, f32[40,128]{1,0:T(8,128)S(1)}, u32[]{:S(2)}, u32[]{:S(2)}) collective-permute-start(f32[40,128]{1,0:T(8,128)S(1)} %add.15.refs_0_), channel_id=1, source_target_pairs={{0,2},{1,3},{2,0},{3,1},{4,6},{5,7},{6,4},{7,5},{8,10},{9,11},{10,... | collective-permute-start | bytes 61448 | tf_op jit(solution)/shard_map/ppermute | solution.py:490

commit v2 on v1

--- a/solution.py
+++ b/solution.py
@@ -13,10 +13,10 @@
 W = 128
 GROUPS = HEADS + 2
 KV_ROWS = 2 * W
-NEAR_ROWS = KV_ROWS + 32
+SUM_ROW = KV_ROWS + 32
+MIX_ROWS = SUM_ROW + 128
 STEP_ROW = (HEADS + 1) * W
-EDGE_ROW = STEP_ROW + 16
-BULK_ROWS = EDGE_ROW + 16
+BULK_ROWS = STEP_ROW + 16
 PAY_ROWS = 40
 LIMIT = 16 << 20
 LOG2E = 1.4426950408889634
@@ -65,8 +65,18 @@
     return jnp.concatenate(rows, axis=0).astype(BF16)
 
 
+def in_pieces(rows, count):
+    high = rows.astype(BF16).astype(F32)
+    mid = (rows - high).astype(BF16).astype(F32)
+    low = rows - high - mid
+    parts = [high, mid, low]
+    if count > 3 * rows.shape[0]:
+        parts.append(jnp.zeros((count - 3 * rows.shape[0], W), F32))
+    return jnp.concatenate(parts, axis=0).astype(BF16)
+
+
 def pack_body(bits, mixer, step, cotan, keys, values, near, *refs):
-    bulk, (size, extra, sems) = refs[:bits], refs[bits:]
+    bulk, (size, ends, extra, sems) = refs[:bits], refs[bits:]
     me = lax.axis_index("ctx")
 
     def copy(source, target, at):
@@ -76,24 +86,18 @@
         copy(step.at[0], size, 0),
         copy(keys.at[0], near.at[0:W, :], 1),
         copy(values.at[0], near.at[W : 2 * W, :], 2),
+        copy(mixer.at[0, W - 16 : W, cols(HEADS + 1)], ends, 3),
     ]
     for c in first:
         c.start()
     later = [jnp.bitwise_and(lax.shift_right_logical(me, b), 1) == 0 for b in range(bits)]
     forward, backward = [], []
     for b in range(bits):
-        at = 3 + b * (GROUPS + 6)
+        at = 4 + b * (GROUPS + 6)
         forward.append(
             [
                 copy(mixer.at[0, :, cols(g)], bulk[b].at[cols(g), :], at + g)
                 for g in range(HEADS + 1)
-            ]
-            + [
-                copy(
-                    mixer.at[0, W - 16 : W, cols(HEADS + 1)],
-                    bulk[b].at[EDGE_ROW:BULK_ROWS, :],
-                    at + HEADS + 1,
-                )
             ]
         )
         backward.append(
@@ -122,18 +126,14 @@
 
     for c in first:
         c.wait()
-    rows = size[...]
-    high = rows.astype(BF16).astype(F32)
-    mid = (rows - high).astype(BF16).astype(F32)
-    low = rows - high - mid
-    extra[0:16, :] = jnp.concatenate([high, mid, low, jnp.zeros_like(low)], axis=0).astype(BF16)
-    extra[16:32, :] = jnp.zeros((16, W), BF16)
+    pieces = in_pieces(size[...], 12).astype(F32)
+    last = ends[...].astype(F32)[12:16]
+    extra[...] = jnp.concatenate([pieces, last], axis=0).astype(BF16)
     for b in range(bits):
-        at = 3 + bits * (GROUPS + 6) + 2 * b
-        sized = copy(extra.at[0:16, :], bulk[b].at[STEP_ROW:EDGE_ROW, :], at)
-        empty = copy(extra.at[16:32, :], bulk[b].at[EDGE_ROW:BULK_ROWS, :], at + 1)
+        at = 4 + bits * (GROUPS + 6) + b
+        sized = copy(extra, bulk[b].at[STEP_ROW:BULK_ROWS, :], at)
         forward[b].append(sized)
-        backward[b] += [sized, empty]
+        backward[b].append(sized)
         sized.start()
 
         @pl.when(later[b])
@@ -142,8 +142,7 @@
                 c.wait()
 
         @pl.when(jnp.logical_not(later[b]))
-        def _(b=b, empty=empty):
-            empty.start()
+        def _(b=b):
             for c in backward[b]:
                 c.wait()
 
@@ -193,7 +192,7 @@
 
 def attend_body(peers, *refs):
     near = refs[4 : 4 + peers]
-    half, sums, halo, query_grad, own, *parts = refs[4 + peers :]
+    half, sums, query_grad, own, *parts = refs[4 + peers :]
     query_grad[0, :, 0 : HEADS // 2 * W] = half[0]
     key_acc, value_acc = attend_heads(
         peers, range(HEADS // 2, HEADS), *refs[:4], near, query_grad, sums
@@ -203,7 +202,6 @@
     for k in range(1, peers + 1):
         parts[k - 1][0:W, :] = key_acc[cols(k)].astype(BF16)
         parts[k - 1][W : 2 * W, :] = value_acc[cols(k)].astype(BF16)
-        parts[k - 1][KV_ROWS:NEAR_ROWS, :] = halo[...]
 
 
 def head_column(ref, lanes):
@@ -217,8 +215,8 @@
 def mixer_body(peers, *refs):
     mixer, step, weight, decay_log, bias, residual, cotan = refs[:7]
     bulk = refs[7 : 7 + peers]
-    input_grad, step_grad, edge, halo, pay = refs[7 + peers : 12 + peers]
-    tails, ext, grads, peer_ext, states, adjoints, acts, slopes = refs[12 + peers :]
+    step_grad, grads, halo, pay = refs[7 + peers : 11 + peers]
+    tails, ext, peer_ext, states, adjoints, acts, slopes = refs[11 + peers :]
     me = lax.axis_index("ctx")
     slots = peers + 1
     index = [me] + [jnp.bitwise_xor(me, k) for k in range(1, slots)]
@@ -236,7 +234,7 @@
                     (g + 1) * W - 16 : (g + 1) * W, :
                 ]
             tails[index[k] + 1, 16 * (GROUPS - 1) : 16 * GROUPS, :] = bulk[k - 1][
-                EDGE_ROW:BULK_ROWS, :
+                STEP_ROW:BULK_ROWS, :
             ]
 
         @pl.when(jnp.logical_not(earlier))
@@ -247,7 +245,7 @@
 
     pieces = [step[0]]
     for k in range(1, slots):
-        sent = bulk[k - 1][STEP_ROW:EDGE_ROW, :].astype(F32)
+        sent = bulk[k - 1][STEP_ROW:BULK_ROWS, :].astype(F32)
         pieces.append(sent[0:4] + sent[4:8] + sent[8:12])
     rate = -jnp.exp(head_column(decay_log, W))
     raw = jnp.concatenate(pieces, axis=0) + jnp.concatenate([head_column(bias, W)] * slots, axis=0)
@@ -302,17 +300,17 @@
 
         @pl.when(earlier)
         def _(k=k):
-            map_in = split(peer_act(k, HEADS, HEADS))
+            map_in = split(jnp.transpose(peer_act(k, HEADS, HEADS)))
             for h in range(HEADS):
                 rows = split(peer_act(k, h, h) * column(3 + k, h))
-                states[h] = states[h] + dot_split(rows, map_in, TN)
+                states[h] = states[h] + dot_split(map_in, rows)
 
         @pl.when(jnp.logical_not(earlier))
         def _(k=k):
-            map_out = peer_act(k, HEADS, HEADS + 1)
+            map_out = jnp.transpose(peer_act(k, HEADS, HEADS + 1))
             for h in range(HEADS):
-                read = split(map_out * column(3 + k, h))
-                adjoints[h] = adjoints[h] + dot_split(bulk[k - 1][cols(h), :], read, TN)
+                read = split(map_out * table[3 + k][h : h + 1])
+                adjoints[h] = adjoints[h] + dot_split(read, bulk[k - 1][cols(h), :])
 
     for g in range(GROUPS):
         place = ext.at[g]
@@ -325,14 +323,18 @@
 
     map_in, map_out = acts[HEADS], acts[HEADS + 1]
     map_in_s, map_out_s = split(map_in), split(map_out)
-    map_in_b, map_out_b = map_in_s[0], map_out_s[0]
-    meets = dot_split(map_out_s, map_in_s, NT)
-    lower = iota2(0) >= iota2(1)
-    ones = jnp.ones((16, W), BF16)
+    meets = dot_split(map_in_s, map_out_s, NT)
+    upper = iota2(0) <= iota2(1)
+    lane = iota2(1)
     grad_in = jnp.zeros((W, W), F32)
     grad_out = jnp.zeros((W, W), F32)
     grad_meets = jnp.zeros((W, W), F32)
-    flow_rows, tail_rows, size_rows, pass_rows, skip_rows = [], [], [], [], []
+    sums = jnp.zeros((W, W), F32)
+    out_rows, pass_rows, skip_rows = [], [], []
+
+    def with_sum(sums, kind, h, array):
+        return jnp.where(lane == HEADS * kind + h, jnp.sum(array, axis=1, keepdims=True), sums)
+
     for h in range(HEADS):
         cot_b = cotan[0, :, cols(h)]
         cot = cot_b.astype(F32)
@@ -343,43 +345,40 @@
         state = states[h]
         adjoint = adjoints[h]
         adjoint_s = split(adjoint)
-        falloff = jnp.where(lower, jnp.exp(column(0, h) - own_cum[h : h + 1]), 0.0)
-        pair = dot_split(cot_b, split(scaled), NT) * falloff
+        falloff = jnp.where(upper, jnp.exp(own_cum[h : h + 1] - column(0, h)), 0.0)
+        pair = dot_split(split(scaled), cot_b, NT) * falloff
         grad_meets = grad_meets + pair
-        flow = split(pair * meets)
-        projected = tail * dot_split(map_in_s, adjoint_s, NT)
-        mixed = dot_split(split(falloff * meets), cot_b, TN)
+        flow = pair * meets
+        projected = tail * dot_split(map_in_s, adjoint_s)
+        mixed = dot_split(split(falloff * meets), cot_b)
         grad_scaled = mixed + projected
-        lead_read = column(2, h) * dot_split(cot_b, split(state))
+        lead_read = column(2, h) * dot_split(cot_b, split(state), NT)
         grad_out = grad_out + lead_read
-        grad_in = grad_in + dot((scaled * tail).astype(BF16), adjoint_s[0])
-        carried = split(lead_read * map_out)
-        trailing = split(projected * act)
-        sized = split(mixed * act)
-        flow_rows.append(
-            (dot_split(ones, flow, NT) - dot_split(ones, flow) + dot_split(ones, carried, NT))[0:1]
-        )
-        trail = dot_split(ones, trailing, NT)[0:1]
-        tail_rows.append(trail * own_size[h : h + 1])
-        size_rows.append(dot_split(ones, sized, NT)[0:1] + trail)
+        grad_in = grad_in + dot((scaled * tail).astype(BF16), adjoint_s[0], NT)
+        out_rows.append(jnp.sum(flow, axis=0, keepdims=True))
+        sums = with_sum(sums, 0, h, lead_read * map_out - flow)
+        sums = with_sum(sums, 1, h, projected * act)
+        sums = with_sum(sums, 2, h, mixed * act)
         passed = jnp.sum(jnp.sum(state * adjoint, axis=0, keepdims=True), axis=1, keepdims=True)
         pass_rows.append(jnp.broadcast_to(passed, (1, W)))
         skip_rows.append(jnp.sum(cot * act, axis=0, keepdims=True))
         grads[h, 0:W, :] = (residual[h] * cot + grad_scaled * size) * slopes[h]
     grad_meets_b = grad_meets.astype(BF16)
-    grad_out = grad_out + dot(grad_meets_b, map_in_b)
-    grad_in = grad_in + dot(grad_meets_b, map_out_b, TN)
+    grad_out = grad_out + dot(grad_meets_b, map_in_s[0], TN)
+    grad_in = grad_in + dot(grad_meets_b, map_out_s[0])
     grads[HEADS, 0:W, :] = grad_in * slopes[HEADS]
     grads[HEADS + 1, 0:W, :] = grad_out * slopes[HEADS + 1]
+    sum_rows = jnp.transpose(sums)
 
     since = (iota2(0) >= iota2(1)).astype(F32)
     before = (iota2(0) < iota2(1)).astype(F32)
+    trail = rows_of(sum_rows, 1)
     grad_decay = (
-        dot(jnp.concatenate(flow_rows, axis=0), since, precise=True)
-        + dot(jnp.concatenate(tail_rows, axis=0), before, precise=True)
+        dot(jnp.concatenate(out_rows, axis=0) + rows_of(sum_rows, 0), since, precise=True)
+        + dot(trail * own_size, before, precise=True)
         + jnp.exp(totals[0]) * jnp.concatenate(pass_rows, axis=0)
     )
-    grad_step = grad_decay * rate + jnp.concatenate(size_rows, axis=0)
+    grad_step = grad_decay * rate + rows_of(sum_rows, 2) + trail
     grad_raw = grad_step * sigmoid(rows_of(raw, 0))
     step_grad[0] = grad_raw
     pay[24:28, :] = grad_decay * own_size * rate
@@ -391,29 +390,53 @@
     for g in range(GROUPS):
         grads[g, W : W + 8, :] = jnp.zeros((8, W), F32)
         grad = grads[g, 0:W, :]
+        for offset in range(TAPS):
+            pay[4 * g + offset : 4 * g + offset + 1, :] = jnp.sum(
+                grad * ext[g, 5 + offset : 5 + offset + W, :], axis=0, keepdims=True
+            )
+
+
+def rows_body(grads, weight, input_grad, edge):
+    for g in range(GROUPS):
         total = grads[g, TAPS - 1 : TAPS - 1 + W, :] * weight[0:1, cols(g)]
         for offset in range(1, TAPS):
             at = TAPS - 1 - offset
             total = total + grads[g, at : at + W, :] * weight[offset : offset + 1, cols(g)]
         input_grad[0, :, cols(g)] = total.astype(BF16)
         edge[:, cols(g)] = total[W - 16 : W]
-        for offset in range(TAPS):
-            pay[4 * g + offset : 4 * g + offset + 1, :] = jnp.sum(
-                grad * ext[g, 5 + offset : 5 + offset + W, :], axis=0, keepdims=True
-            )
-
-
-def finish_body(peers, *refs):
-    partial, edge, weight, own = refs[:4]
-    parts = refs[4 : 4 + peers]
-    input_grad, key_grad, value_grad = refs[4 + peers :]
+
+
+def merge_body(peers, *refs):
+    pay, other, halo = refs[:3]
+    parts = refs[3 : 3 + peers]
+    total_out, *mixed = refs[3 + peers :]
+    total = pay[...] + other[...]
+    total_out[...] = total
+    pieces = in_pieces(total, MIX_ROWS - SUM_ROW)
+    for part, out in zip(parts, mixed):
+        out[0:KV_ROWS, :] = part[...]
+        out[KV_ROWS:SUM_ROW, :] = halo[...]
+        out[SUM_ROW:MIX_ROWS, :] = pieces
+
+
+def finish_body(peers, count, *refs):
+    partial, edge, weight, own, pay = refs[:5]
+    mixed = refs[5 : 5 + peers]
+    input_grad, key_grad, value_grad, conv_grad, decay_grad, bias_grad, skip_grad = refs[5 + peers :]
     me = lax.axis_index("ctx")
     both = own[...]
+    total = pay[...]
     halo = jnp.zeros((32, W), F32)
     for k in range(1, peers + 1):
-        both = both + parts[k - 1][0:KV_ROWS, :].astype(F32)
-        after = jnp.bitwise_xor(me, k) == me + 1
-        halo = halo + jnp.where(after, parts[k - 1][KV_ROWS:NEAR_ROWS, :].astype(F32), 0.0)
+        other = jnp.bitwise_xor(me, k)
+        sent = mixed[k - 1][0:KV_ROWS, :].astype(F32)
+        both = both + jnp.where(other > me, sent, 0.0)
+        edges = mixed[k - 1][KV_ROWS:SUM_ROW, :].astype(F32)
+        halo = halo + jnp.where(other == me + 1, edges, 0.0)
+        pieces = mixed[k - 1][SUM_ROW:MIX_ROWS, :].astype(F32)
+        total = total + (
+            pieces[0:PAY_ROWS] + pieces[PAY_ROWS : 2 * PAY_ROWS] + pieces[2 * PAY_ROWS : 3 * PAY_ROWS]
+        )
     key_grad[0] = both[0:W].astype(BF16)
     value_grad[0] = both[W : 2 * W].astype(BF16)
     row = lax.broadcasted_iota(jnp.int32, (16, W), 0)
@@ -426,10 +449,7 @@
                 rows = rows + jnp.where(row == at, piece, 0.0)
         input_grad[0, 0 : W - 16, cols(g)] = partial[0, 0 : W - 16, cols(g)]
         input_grad[0, W - 16 : W, cols(g)] = rows.astype(BF16)
-
-
-def total_body(count, total_a, total_b, conv_grad, decay_grad, bias_grad, skip_grad):
-    total = (total_a[...] + total_b[...]) * (1.0 / count)
+    total = total * (1.0 / count)
     for g in range(GROUPS):
         conv_grad[:, cols(g)] = total[4 * g : 4 * g + 4]
     sums = jnp.sum(total[24:40], axis=1, keepdims=True)
@@ -473,8 +493,9 @@
         out_specs=[vmem] * (1 + bits),
         scratch_shapes=[
             pltpu.VMEM((HEADS, W), F32),
-            pltpu.VMEM((32, W), BF16),
-            pltpu.SemaphoreType.DMA((3 + bits * (GROUPS + 8),)),
+            pltpu.VMEM((16, W), BF16),
+            pltpu.VMEM((16, W), BF16),
+            pltpu.SemaphoreType.DMA((4 + bits * (GROUPS + 7),)),
         ],
         compiler_params=params,
         name="pack",
@@ -492,20 +513,18 @@
     nears = [swap(near, k, lambda i, j: j > i) for k in range(1, ctx)]
     bulks = [swap(bulk[k.bit_length() - 1], k) for k in range(1, ctx)]
 
-    input_grad, step_grad, edge, halo, pay = pl.pallas_call(
+    step_grad, grads, halo, pay = pl.pallas_call(
         lambda *refs: mixer_body(peers, *refs),
         out_shape=[
-            shape(mixer_input.shape, BF16),
             shape(step_input.shape, F32),
-            shape((16, GROUPS * W), F32),
+            shape((GROUPS, W + 8, W), F32),
             shape((32, W), BF16),
             shape((PAY_ROWS, W), F32),
         ],
         in_specs=[vmem] * 3 + [smem] * 3 + [vmem] * (1 + peers),
-        out_specs=[vmem] * 5,
+        out_specs=[vmem] * 4,
         scratch_shapes=[
             pltpu.VMEM((ctx + 1, 16 * GROUPS, W), BF16),
-            pltpu.VMEM((GROUPS, W + 8, W), F32),
             pltpu.VMEM((GROUPS, W + 8, W), F32),
             pltpu.VMEM((peers * GROUPS, W + 8, W), F32),
             pltpu.VMEM((HEADS, W, W), F32),
@@ -516,6 +535,15 @@
         compiler_params=params,
         name="mixer",
     )(mixer_input, step_input, conv_weight, decay_log, step_bias, residual, mixer_cotangent, *bulks)
+
+    input_grad, edge = pl.pallas_call(
+        rows_body,
+        out_shape=[shape(mixer_input.shape, BF16), shape((16, GROUPS * W), F32)],
+        in_specs=[vmem] * 2,
+        out_specs=[vmem] * 2,
+        compiler_params=params,
+        name="rows",
+    )(grads, conv_weight)
 
     half, sums = pl.pallas_call(
         lambda *refs: half_body(peers, *refs),
@@ -532,41 +560,42 @@
     query_grad, own, *parts = pl.pallas_call(
         lambda *refs: attend_body(peers, *refs),
         out_shape=[shape(queries.shape, BF16), shape((KV_ROWS, W), F32)]
-        + [shape((NEAR_ROWS, W), BF16)] * peers,
-        in_specs=[vmem] * (7 + peers),
+        + [shape((KV_ROWS, W), BF16)] * peers,
+        in_specs=[vmem] * (6 + peers),
         out_specs=[vmem] * (2 + peers),
         compiler_params=params,
         name="attend",
-    )(queries, attn_keys, attn_values, attn_cotangent, *nears, half, sums, halo)
-
-    returned = [swap(parts[k - 1], k, lambda i, j: j < i) for k in range(1, ctx)]
-    stages = [("dp", 1 << b) for b in range(dp.bit_length() - 1)]
-    stages += [("ctx", 1 << b) for b in range(bits)]
-    for n, (axis, k) in enumerate(stages):
-        other = swap(pay, k, axis=axis)
-        if n + 1 < len(stages):
+    )(queries, attn_keys, attn_values, attn_cotangent, *nears, half, sums)
+
+    last = dp.bit_length() - 2
+    for n in range(last + 1):
+        other = swap(pay, 1 << n, axis="dp")
+        if n < last:
             pay = pay + other
-
-    input_grad, key_grad, value_grad = pl.pallas_call(
-        lambda *refs: finish_body(peers, *refs),
+    pay, *mixed = pl.pallas_call(
+        lambda *refs: merge_body(peers, *refs),
+        out_shape=[shape((PAY_ROWS, W), F32)] + [shape((MIX_ROWS, W), BF16)] * peers,
+        in_specs=[vmem] * (3 + peers),
+        out_specs=[vmem] * (1 + peers),
+        compiler_params=params,
+        name="merge",
+    )(pay, other, halo, *parts)
+    mixed = [swap(mixed[k - 1], k) for k in range(1, ctx)]
+    outs = pl.pallas_call(
+        lambda *refs: finish_body(peers, dp, *refs),
         out_shape=[
             shape(mixer_input.shape, BF16),
             shape(attn_keys.shape, BF16),
             shape(attn_values.shape, BF16),
-        ],
-        in_specs=[vmem] * (4 + peers),
-        out_specs=[vmem] * 3,
+            shape(conv_weight.shape, F32),
+        ]
+        + [shape((HEADS,), F32)] * 3,
+        in_specs=[vmem] * (5 + peers),
+        out_specs=[vmem] * 4 + [smem] * 3,
         compiler_params=params,
         name="finish",
-    )(input_grad, edge, conv_weight, own, *returned)
-    conv_grad, decay_grad, bias_grad, skip_grad = pl.pallas_call(
-        lambda *refs: total_body(dp, *refs),
-        out_shape=[shape(conv_weight.shape, F32)] + [shape((HEADS,), F32)] * 3,
-        in_specs=[vmem] * 2,
-        out_specs=[vmem] + [smem] * 3,
-        compiler_params=params,
-        name="total",
-    )(pay, other)
+    )(input_grad, edge, conv_weight, own, pay, *mixed)
+    input_grad, key_grad, value_grad, conv_grad, decay_grad, bias_grad, skip_grad = outs
     return (
         input_grad,
         jnp.swapaxes(step_grad, 1, 2),

time: 47.2 us -> 39.1 us (0.83)
  starting transfers between devices: 28.1 us -> 20.9 us
  Pallas kernels: 11.2 us -> 9.7 us
  waiting for transfers between devices: 6.65 us -> 7.38 us
    ppermute x14 -> x12, starting transfers between devices: 28.1 us -> 20.9 us  [swap(): return lax.ppermute(array, axis, pairs)]
    pallas_call x3 -> x4, Pallas kernels: 6.44 us -> 4.89 us  [the longest x1 3.99 us: on_device(): pl.pallas_call(lambda *refs: mixer_body(peers, *refs), out_shape=[shape(s...]
    ppermute x14 -> x12, waiting for transfers between devices: 6.65 us -> 7.38 us  [swap(): return lax.ppermute(array, axis, pairs)]
  transfers between devices with their start and end apart: 14 -> 12, of which waited for: 5 -> 5; matrix products, arithmetic and copies ran while one was open for 0% -> 0% of each run, Pallas kernels for 20% -> 20%
where the time goes in v2:
time: 39.1 us; the launch traced here: 38.9 us
  starting transfers between devices  20.9 us (53%)
  Pallas kernels  9.7 us (25%)
  waiting for transfers between devices  7.38 us (19%)
  between operations  0.87 us (2%)
    ppermute x12, starting transfers between devices, swap(): return lax.ppermute(array, axis, pairs)  20.9 us
    ppermute x12, waiting for transfers between devices, swap(): return lax.ppermute(array, axis, pairs)  7.38 us
    pallas_call x1, Pallas kernels, on_device(): pl.pallas_call(lambda *refs: mixer_body(peers, *refs), out_shape=[shape(s...  3.99 us
    pallas_call x1, Pallas kernels, on_device(): pl.pallas_call(lambda *refs: attend_body(peers, *refs), out_shape=[shape(...  2.06 us
    pallas_call x1, Pallas kernels, on_device(): pl.pallas_call(lambda *refs: half_body(peers, *refs), out_shape=[shape((1...  1.46 us
    pallas_call x1, Pallas kernels, on_device(): pl.pallas_call(lambda *refs: pack_body(bits, *refs), out_shape=[shape((KV...  1.29 us
  transfers between devices with their start and end apart: 12, of which 5 were waited for; matrix products, arithmetic and copies ran while one was open for 0% of the time, Pallas kernels for 20%

profile of v2, /device:TPU:0, one launch (start us, length us, event | category | flops | bytes accessed | tf_op | source)
XLA Modules:
  0.0 38.9 jit_solution(14142352013116726306)
XLA Ops:
  0.7 1.3 %pack.1 = (bf16[256,128]{1,0:T(8,128)(2,1)S(1)}, bf16[656,128]{1,0:T(8,128)(2,1)S(1)}, bf16[656,128]{1,0:T(8,128)(2,1)S(1)}) custom-call(bf16[1,128,768]{2,1,0:T(8,128)(2,1)} %refs_0_.5, f32[1,4,128]{2,1,0:T(4,128)} %bitcast.2, bf16[1,128,512]{2,1,0:T(8,128)(2,1)} %refs_6_.1, bf16[1,128,128]{2,1,0:T(8,128)(2,1)} %refs_1_.3, bf16[1,128,128]{2,1,0:T(8,128)(2,1)} %refs_2_.8), custom_call_target="tpu_custom_call" | custom-call | tf_op jit(solution)/shard_map/pack/pallas_call | solution.py:489
  2.0 0.0 copy-start.7
  2.0 3.0 %collective-permute-start = (bf16[656,128]{1,0:T(8,128)(2,1)S(1)}, bf16[656,128]{1,0:T(8,128)(2,1)S(1)}, u32[]{:S(2)}, u32[]{:S(2)}) collective-permute-start(bf16[656,128]{1,0:T(8,128)(2,1)S(1)} %get-tuple-element.36), channel_id=1, source_target_pairs={{0,1},{1,0},{2,3},{3,2},{4,5},{5,4},{6,7},{7,6},{8,9},{9,8},{10,11... | collective-permute-start | bytes 503816 | tf_op jit(solution)/shard_map/ppermute | solution.py:511
  5.0 1.5 %collective-permute-start.1 = (bf16[656,128]{1,0:T(8,128)(2,1)S(1)}, bf16[656,128]{1,0:T(8,128)(2,1)S(1)}, u32[]{:S(2)}, u32[]{:S(2)}) collective-permute-start(bf16[656,128]{1,0:T(8,128)(2,1)S(1)} %get-tuple-element.37), channel_id=1, source_target_pairs={{0,2},{1,3},{2,0},{3,1},{4,6},{5,7},{6,4},{7,5},{8,10},{9,11},{10,... | collective-permute-start | bytes 503816 | tf_op jit(solution)/shard_map/ppermute | solution.py:511
  6.5 0.1 collective-permute-start.2
  6.6 3.8 %collective-permute-start.3 = (bf16[256,128]{1,0:T(8,128)(2,1)S(1)}, bf16[256,128]{1,0:T(8,128)(2,1)S(1)}, u32[]{:S(2)}, u32[]{:S(2)}) collective-permute-start(bf16[256,128]{1,0:T(8,128)(2,1)S(1)} %get-tuple-element.41), channel_id=1, source_target_pairs={{0,1},{2,3},{4,5},{6,7},{8,9},{10,11},{12,13},{14,15},{16,17},{18,... | collective-permute-start | bytes 196616 | tf_op jit(solution)/shard_map/ppermute | solution.py:511
  10.4 3.4 %collective-permute-start.4 = (bf16[256,128]{1,0:T(8,128)(2,1)S(1)}, bf16[256,128]{1,0:T(8,128)(2,1)S(1)}, u32[]{:S(2)}, u32[]{:S(2)}) collective-permute-start(bf16[256,128]{1,0:T(8,128)(2,1)S(1)} %get-tuple-element.41), channel_id=1, source_target_pairs={{0,2},{1,3},{4,6},{5,7},{8,10},{9,11},{12,14},{13,15},{16,18},{17,... | collective-permute-start | bytes 196616 | tf_op jit(solution)/shard_map/ppermute | solution.py:511
  13.8 0.0 collective-permute-done.refs_7_
  13.9 1.3 %collective-permute-start.5 = (bf16[256,128]{1,0:T(8,128)(2,1)S(1)}, bf16[256,128]{1,0:T(8,128)(2,1)S(1)}, u32[]{:S(2)}, u32[]{:S(2)}) collective-permute-start(bf16[256,128]{1,0:T(8,128)(2,1)S(1)} %get-tuple-element.41), channel_id=1, source_target_pairs={{0,3},{1,2},{4,7},{5,6},{8,11},{9,10},{12,15},{13,14},{16,19},{17,... | collective-permute-start | bytes 196616 | tf_op jit(solution)/shard_map/ppermute | solution.py:511
  15.2 0.0 collective-permute-done.1.refs_8_
  15.2 0.0 collective-permute-done.2.refs_9_
  15.2 0.0 copy-start.2
  15.3 0.0 copy-start.3
  15.3 4.0 %mixer.1 = (f32[1,4,128]{2,1,0:T(4,128)}, f32[6,136,128]{2,1,0:T(8,128)S(1)}, bf16[32,128]{1,0:T(8,128)(2,1)S(1)}, f32[40,128]{1,0:T(8,128)S(1)}) custom-call(bf16[1,128,768]{2,1,0:T(8,128)(2,1)S(1)} %copy-done, f32[1,4,128]{2,1,0:T(4,128)S(1)} %bitcast.3, f32[4,768]{1,0:T(4,128)S(1)} %copy-done.6, f32[4]{0:T(128)S(1)} %copy-done.8, f32[4]{0:T(128)S(1)} %copy-done.9, ...), custom_call_target="tpu_custom_call" | custom-call | tf_op jit(solution)/shard_map/mixer/pallas_call | solution.py:516
  19.3 0.0 collective-permute-start.6
  19.3 1.2 %collective-permute-done.6 = f32[40,128]{1,0:T(8,128)S(1)} collective-permute-done((f32[40,128]{1,0:T(8,128)S(1)}, f32[40,128]{1,0:T(8,128)S(1)}, u32[]{:S(2)}, u32[]{:S(2)}) %collective-permute-start.6) | collective-permute-done | bytes 20512 | tf_op jit(solution)/shard_map/ppermute | solution.py:511
  20.5 1.6 %collective-permute-start.7 = (f32[40,128]{1,0:T(8,128)S(1)}, f32[40,128]{1,0:T(8,128)S(1)}, u32[]{:S(2)}, u32[]{:S(2)}) collective-permute-start(f32[40,128]{1,0:T(8,128)S(1)} %add.6), channel_id=1, source_target_pairs={{0,8},{4,12},{8,0},{12,4},{16,24},{20,28},{24,16},{28,20},{1,9},{5... | collective-permute-start | bytes 61448 | tf_op jit(solution)/shard_map/ppermute | solution.py:511
  22.1 2.2 %collective-permute-done.7 = f32[40,128]{1,0:T(8,128)S(1)} collective-permute-done((f32[40,128]{1,0:T(8,128)S(1)}, f32[40,128]{1,0:T(8,128)S(1)}, u32[]{:S(2)}, u32[]{:S(2)}) %collective-permute-start.7) | collective-permute-done | bytes 20512 | tf_op jit(solution)/shard_map/ppermute | solution.py:511
  24.3 2.6 %collective-permute-start.8 = (f32[40,128]{1,0:T(8,128)S(1)}, f32[40,128]{1,0:T(8,128)S(1)}, u32[]{:S(2)}, u32[]{:S(2)}) collective-permute-start(f32[40,128]{1,0:T(8,128)S(1)} %add.7.refs_0_), channel_id=1, source_target_pairs={{0,16},{4,20},{8,24},{12,28},{16,0},{20,4},{24,8},{28,12},{1,17},{... | collective-permute-start | bytes 61448 | tf_op jit(solution)/shard_map/ppermute | solution.py:511
  26.9 0.0 collective-permute-done.3.refs_4_
  26.9 0.0 collective-permute-done.4.refs_5_
  26.9 0.0 collective-permute-done.5.refs_6_
  27.0 1.5 %half.1 = (bf16[1,128,256]{2,1,0:T(8,128)(2,1)S(1)}, f32[2,512,128]{2,1,0:T(8,128)S(1)}) custom-call(bf16[1,128,512]{2,1,0:T(8,128)(2,1)S(1)} %copy-done.2, bf16[1,128,128]{2,1,0:T(8,128)(2,1)S(1)} %copy-done.4, bf16[1,128,128]{2,1,0:T(8,128)(2,1)S(1)} %copy-done.5, bf16[1,128,512]{2,1,0:T(8,128)(2,1)S(1)} %copy-done.3, ...), custom_call_target="tpu_custom_call" | custom-call | tf_op jit(solution)/shard_map/half/pallas_call | solution.py:548
  28.4 2.1 %attend.1 = (bf16[1,128,512]{2,1,0:T(8,128)(2,1)}, f32[256,128]{1,0:T(8,128)S(1)}, bf16[256,128]{1,0:T(8,128)(2,1)S(1)}, bf16[256,128]{1,0:T(8,128)(2,1)S(1)}, bf16[256,128]{1,0:T(8,128)(2,1)S(1)}) custom-call(bf16[1,128,512]{2,1,0:T(8,128)(2,1)S(1)} %copy-done.2, bf16[1,128,128]{2,1,0:T(8,128)(2,1)S(1)} %copy-done.4, bf16[1,128,128]{2,1,0:T(8,128)(2,1)S(1)} %copy-done.5, ...), custom_call_target="tpu_custom_call" | custom-call | tf_op jit(solution)/shard_map/attend/pallas_call | solution.py:560
  30.5 1.6 %collective-permute-start.9 = (bf16[416,128]{1,0:T(8,128)(2,1)S(1)}, bf16[416,128]{1,0:T(8,128)(2,1)S(1)}, u32[]{:S(2)}, u32[]{:S(2)}) collective-permute-start(bf16[416,128]{1,0:T(8,128)(2,1)S(1)} %get-tuple-element.51), channel_id=1, source_target_pairs={{0,1},{1,0},{2,3},{3,2},{4,5},{5,4},{6,7},{7,6},{8,9},{9,8},{10,11... | collective-permute-start | bytes 319496 | tf_op jit(solution)/shard_map/ppermute | solution.py:511
  32.1 0.4 %collective-permute-start.10 = (bf16[416,128]{1,0:T(8,128)(2,1)S(1)}, bf16[416,128]{1,0:T(8,128)(2,1)S(1)}, u32[]{:S(2)}, u32[]{:S(2)}) collective-permute-start(bf16[416,128]{1,0:T(8,128)(2,1)S(1)} %get-tuple-element.52), channel_id=1, source_target_pairs={{0,2},{1,3},{2,0},{3,1},{4,6},{5,7},{6,4},{7,5},{8,10},{9,11},{10,... | collective-permute-start | bytes 319496 | tf_op jit(solution)/shard_map/ppermute | solution.py:511
  32.5 1.5 %collective-permute-start.11 = (bf16[416,128]{1,0:T(8,128)(2,1)S(1)}, bf16[416,128]{1,0:T(8,128)(2,1)S(1)}, u32[]{:S(2)}, u32[]{:S(2)}) collective-permute-start(bf16[416,128]{1,0:T(8,128)(2,1)S(1)} %get-tuple-element.53), channel_id=1, source_target_pairs={{0,3},{1,2},{2,1},{3,0},{4,7},{5,6},{6,5},{7,4},{8,11},{9,10},{10,... | collective-permute-start | bytes 319496 | tf_op jit(solution)/shard_map/ppermute | solution.py:511
  34.1 0.1 rows.1
  34.2 2.0 %collective-permute-done.9.refs_5_ = bf16[416,128]{1,0:T(8,128)(2,1)S(1)} collective-permute-done((bf16[416,128]{1,0:T(8,128)(2,1)S(1)}, bf16[416,128]{1,0:T(8,128)(2,1)S(1)}, u32[]{:S(2)}, u32[]{:S(2)}) %collective-permute-start.9) | collective-permute-done | bytes 106528 | tf_op jit(solution)/shard_map/ppermute | solution.py:511
  36.2 0.7 %collective-permute-done.10.refs_6_ = bf16[416,128]{1,0:T(8,128)(2,1)S(1)} collective-permute-done((bf16[416,128]{1,0:T(8,128)(2,1)S(1)}, bf16[416,128]{1,0:T(8,128)(2,1)S(1)}, u32[]{:S(2)}, u32[]{:S(2)}) %collective-permute-start.10) | collective-permute-done | bytes 106528 | tf_op jit(solution)/shard_map/ppermute | solution.py:511
  36.9 1.3 %collective-permute-done.11.refs_7_ = bf16[416,128]{1,0:T(8,128)(2,1)S(1)} collective-permute-done((bf16[416,128]{1,0:T(8,128)(2,1)S(1)}, bf16[416,128]{1,0:T(8,128)(2,1)S(1)}, u32[]{:S(2)}, u32[]{:S(2)}) %collective-permute-start.11) | collective-permute-done | bytes 106528 | tf_op jit(solution)/shard_map/ppermute | solution.py:511
  38.1 0.8 %finish.1 = (bf16[1,128,768]{2,1,0:T(8,128)(2,1)}, bf16[1,128,128]{2,1,0:T(8,128)(2,1)}, bf16[1,128,128]{2,1,0:T(8,128)(2,1)}, f32[4,768]{1,0:T(4,128)}, f32[4]{0:T(128)}, /*index=5*/f32[4]{0:T(128)}, f32[4]{0:T(128)}) custom-call(bf16[1,128,768]{2,1,0:T(8,128)(2,1)S(1)} %get-tuple-element.39.refs_0_, f32[16,768]{1,0:T(8,128)S(1)} %get-tuple-element.40.refs_1_, ...), custom_call_target="tpu_custom_call" | custom-call | tf_op jit(solution)/shard_map/finish/pallas_call | solution.py:584
  (23 shorter events, 0.1 us)
Async XLA Ops:
  0.6 14.5 %copy-start = (bf16[1,128,768]{2,1,0:T(8,128)(2,1)S(1)}, bf16[1,128,768]{2,1,0:T(8,128)(2,1)}, u32[]{:S(2)}) copy-start(bf16[1,128,768]{2,1,0:T(8,128)(2,1)} %refs_0_.5) | copy-start | bytes 589828
  0.7 14.5 %copy-start.1 = (bf16[1,128,512]{2,1,0:T(8,128)(2,1)S(1)}, bf16[1,128,512]{2,1,0:T(8,128)(2,1)}, u32[]{:S(2)}) copy-start(bf16[1,128,512]{2,1,0:T(8,128)(2,1)} %refs_6_.1) | copy-start | bytes 393220
  0.7 14.5 %copy-start.6 = (f32[4,768]{1,0:T(4,128)S(1)}, f32[4,768]{1,0:T(4,128)}, u32[]{:S(2)}) copy-start(f32[4,768]{1,0:T(4,128)} %refs_2_.9) | copy-start | bytes 36868
  2.0 13.2 %copy-start.7 = (f32[1,128,4]{1,2,0:T(4,128)S(1)}, f32[1,128,4]{1,2,0:T(4,128)}, u32[]{:S(2)}) copy-start(f32[1,128,4]{1,2,0:T(4,128)} %param.12) | copy-start | bytes 6148
  2.0 11.9 %collective-permute-start = (bf16[656,128]{1,0:T(8,128)(2,1)S(1)}, bf16[656,128]{1,0:T(8,128)(2,1)S(1)}, u32[]{:S(2)}, u32[]{:S(2)}) collective-permute-start(bf16[656,128]{1,0:T(8,128)(2,1)S(1)} %get-tuple-element.36), channel_id=1, source_target_pairs={{0,1},{1,0},{2,3},{3,2},{4,5},{5,4},{6,7},{7,6},{8,9},{9,8},{10,11... | collective-permute-start | bytes 503816 | tf_op jit(solution)/shard_map/ppermute | solution.py:511
  5.0 10.2 %copy-start.8 = (f32[4]{0:T(128)S(1)}, f32[4]{0:T(128)}, u32[]{:S(2)}) copy-start(f32[4]{0:T(128)} %refs_3_.5) | copy-start | bytes 52
  5.0 10.2 %copy-start.9 = (f32[4]{0:T(128)S(1)}, f32[4]{0:T(128)}, u32[]{:S(2)}) copy-start(f32[4]{0:T(128)} %refs_4_.3) | copy-start | bytes 52
  5.0 10.2 %copy-start.10 = (f32[4]{0:T(128)S(1)}, f32[4]{0:T(128)}, u32[]{:S(2)}) copy-start(f32[4]{0:T(128)} %refs_5_.1) | copy-start | bytes 52
  5.0 10.1 %collective-permute-start.1 = (bf16[656,128]{1,0:T(8,128)(2,1)S(1)}, bf16[656,128]{1,0:T(8,128)(2,1)S(1)}, u32[]{:S(2)}, u32[]{:S(2)}) collective-permute-start(bf16[656,128]{1,0:T(8,128)(2,1)S(1)} %get-tuple-element.37), channel_id=1, source_target_pairs={{0,2},{1,3},{2,0},{3,1},{4,6},{5,7},{6,4},{7,5},{8,10},{9,11},{10,... | collective-permute-start | bytes 503816 | tf_op jit(solution)/shard_map/ppermute | solution.py:511
  6.5 8.6 %collective-permute-start.2 = (bf16[656,128]{1,0:T(8,128)(2,1)S(1)}, bf16[656,128]{1,0:T(8,128)(2,1)S(1)}, u32[]{:S(2)}, u32[]{:S(2)}) collective-permute-start(bf16[656,128]{1,0:T(8,128)(2,1)S(1)} %get-tuple-element.37), channel_id=1, source_target_pairs={{0,3},{1,2},{2,1},{3,0},{4,7},{5,6},{6,5},{7,4},{8,11},{9,10},{10,... | collective-permute-start | bytes 503816 | tf_op jit(solution)/shard_map/ppermute | solution.py:511
  6.6 20.3 %collective-permute-start.3 = (bf16[256,128]{1,0:T(8,128)(2,1)S(1)}, bf16[256,128]{1,0:T(8,128)(2,1)S(1)}, u32[]{:S(2)}, u32[]{:S(2)}) collective-permute-start(bf16[256,128]{1,0:T(8,128)(2,1)S(1)} %get-tuple-element.41), channel_id=1, source_target_pairs={{0,1},{2,3},{4,5},{6,7},{8,9},{10,11},{12,13},{14,15},{16,17},{18,... | collective-permute-start | bytes 196616 | tf_op jit(solution)/shard_map/ppermute | solution.py:511
  10.4 16.5 %collective-permute-start.4 = (bf16[256,128]{1,0:T(8,128)(2,1)S(1)}, bf16[256,128]{1,0:T(8,128)(2,1)S(1)}, u32[]{:S(2)}, u32[]{:S(2)}) collective-permute-start(bf16[256,128]{1,0:T(8,128)(2,1)S(1)} %get-tuple-element.41), channel_id=1, source_target_pairs={{0,2},{1,3},{4,6},{5,7},{8,10},{9,11},{12,14},{13,15},{16,18},{17,... | collective-permute-start | bytes 196616 | tf_op jit(solution)/shard_map/ppermute | solution.py:511
  13.9 13.1 %collective-permute-start.5 = (bf16[256,128]{1,0:T(8,128)(2,1)S(1)}, bf16[256,128]{1,0:T(8,128)(2,1)S(1)}, u32[]{:S(2)}, u32[]{:S(2)}) collective-permute-start(bf16[256,128]{1,0:T(8,128)(2,1)S(1)} %get-tuple-element.41), channel_id=1, source_target_pairs={{0,3},{1,2},{4,7},{5,6},{8,11},{9,10},{12,15},{13,14},{16,19},{17,... | collective-permute-start | bytes 196616 | tf_op jit(solution)/shard_map/ppermute | solution.py:511
  15.2 11.7 %copy-start.2 = (bf16[1,128,512]{2,1,0:T(8,128)(2,1)S(1)}, bf16[1,128,512]{2,1,0:T(8,128)(2,1)}, u32[]{:S(2)}) copy-start(bf16[1,128,512]{2,1,0:T(8,128)(2,1)} %refs_0_.7) | copy-start | bytes 393220
  15.3 11.7 %copy-start.3 = (bf16[1,128,512]{2,1,0:T(8,128)(2,1)S(1)}, bf16[1,128,512]{2,1,0:T(8,128)(2,1)}, u32[]{:S(2)}) copy-start(bf16[1,128,512]{2,1,0:T(8,128)(2,1)} %refs_3_.7) | copy-start | bytes 393220
  19.3 1.2 %collective-permute-start.6 = (f32[40,128]{1,0:T(8,128)S(1)}, f32[40,128]{1,0:T(8,128)S(1)}, u32[]{:S(2)}, u32[]{:S(2)}) collective-permute-start(f32[40,128]{1,0:T(8,128)S(1)} %get-tuple-element.45), channel_id=1, source_target_pairs={{0,4},{4,0},{8,12},{12,8},{16,20},{20,16},{24,28},{28,24},{1,5},{5... | collective-permute-start | bytes 61448 | tf_op jit(solution)/shard_map/ppermute | solution.py:511
  20.5 6.5 %copy-start.5 = (bf16[1,128,128]{2,1,0:T(8,128)(2,1)S(1)}, bf16[1,128,128]{2,1,0:T(8,128)(2,1)}, u32[]{:S(2)}) copy-start(bf16[1,128,128]{2,1,0:T(8,128)(2,1)} %refs_2_.8) | copy-start | bytes 98308
  20.5 6.5 %copy-start.4 = (bf16[1,128,128]{2,1,0:T(8,128)(2,1)S(1)}, bf16[1,128,128]{2,1,0:T(8,128)(2,1)}, u32[]{:S(2)}) copy-start(bf16[1,128,128]{2,1,0:T(8,128)(2,1)} %refs_1_.3) | copy-start | bytes 98308
  20.5 3.8 %collective-permute-start.7 = (f32[40,128]{1,0:T(8,128)S(1)}, f32[40,128]{1,0:T(8,128)S(1)}, u32[]{:S(2)}, u32[]{:S(2)}) collective-permute-start(f32[40,128]{1,0:T(8,128)S(1)} %add.6), channel_id=1, source_target_pairs={{0,8},{4,12},{8,0},{12,4},{16,24},{20,28},{24,16},{28,20},{1,9},{5... | collective-permute-start | bytes 61448 | tf_op jit(solution)/shard_map/ppermute | solution.py:511
  24.3 6.2 %collective-permute-start.8 = (f32[40,128]{1,0:T(8,128)S(1)}, f32[40,128]{1,0:T(8,128)S(1)}, u32[]{:S(2)}, u32[]{:S(2)}) collective-permute-start(f32[40,128]{1,0:T(8,128)S(1)} %add.7.refs_0_), channel_id=1, source_target_pairs={{0,16},{4,20},{8,24},{12,28},{16,0},{20,4},{24,8},{28,12},{1,17},{... | collective-permute-start | bytes 61448 | tf_op jit(solution)/shard_map/ppermute | solution.py:511
  30.5 5.7 %collective-permute-start.9 = (bf16[416,128]{1,0:T(8,128)(2,1)S(1)}, bf16[416,128]{1,0:T(8,128)(2,1)S(1)}, u32[]{:S(2)}, u32[]{:S(2)}) collective-permute-start(bf16[416,128]{1,0:T(8,128)(2,1)S(1)} %get-tuple-element.51), channel_id=1, source_target_pairs={{0,1},{1,0},{2,3},{3,2},{4,5},{5,4},{6,7},{7,6},{8,9},{9,8},{10,11... | collective-permute-start | bytes 319496 | tf_op jit(solution)/shard_map/ppermute | solution.py:511
  32.1 4.7 %collective-permute-start.10 = (bf16[416,128]{1,0:T(8,128)(2,1)S(1)}, bf16[416,128]{1,0:T(8,128)(2,1)S(1)}, u32[]{:S(2)}, u32[]{:S(2)}) collective-permute-start(bf16[416,128]{1,0:T(8,128)(2,1)S(1)} %get-tuple-element.52), channel_id=1, source_target_pairs={{0,2},{1,3},{2,0},{3,1},{4,6},{5,7},{6,4},{7,5},{8,10},{9,11},{10,... | collective-permute-start | bytes 319496 | tf_op jit(solution)/shard_map/ppermute | solution.py:511
  32.5 5.6 %collective-permute-start.11 = (bf16[416,128]{1,0:T(8,128)(2,1)S(1)}, bf16[416,128]{1,0:T(8,128)(2,1)S(1)}, u32[]{:S(2)}, u32[]{:S(2)}) collective-permute-start(bf16[416,128]{1,0:T(8,128)(2,1)S(1)} %get-tuple-element.53), channel_id=1, source_target_pairs={{0,3},{1,2},{2,1},{3,0},{4,7},{5,6},{6,5},{7,4},{8,11},{9,10},{10,... | collective-permute-start | bytes 319496 | tf_op jit(solution)/shard_map/ppermute | solution.py:511

commit v3 on v2

--- a/solution.py
+++ b/solution.py
@@ -13,8 +13,8 @@
 W = 128
 GROUPS = HEADS + 2
 KV_ROWS = 2 * W
-SUM_ROW = KV_ROWS + 32
-MIX_ROWS = SUM_ROW + 128
+MIX_ROWS = KV_ROWS + 96
+SUM_ROWS = 36
 STEP_ROW = (HEADS + 1) * W
 BULK_ROWS = STEP_ROW + 16
 PAY_ROWS = 40
@@ -60,11 +60,6 @@
     return slice(g * W, (g + 1) * W)
 
 
-def small_rows(rows):
-    rows = rows + [jnp.zeros((32 - 3 * GROUPS, W), F32)]
-    return jnp.concatenate(rows, axis=0).astype(BF16)
-
-
 def in_pieces(rows, count):
     high = rows.astype(BF16).astype(F32)
     mid = (rows - high).astype(BF16).astype(F32)
@@ -75,8 +70,8 @@
     return jnp.concatenate(parts, axis=0).astype(BF16)
 
 
-def pack_body(bits, mixer, step, cotan, keys, values, near, *refs):
-    bulk, (size, ends, extra, sems) = refs[:bits], refs[bits:]
+def pack_body(bits, mixer, step, cotan, keys, values, decay_log, bias, residual, near, *refs):
+    bulk, (consts, size, ends, extra, scalars, sems) = refs[:bits], refs[bits:]
     me = lax.axis_index("ctx")
 
     def copy(source, target, at):
@@ -87,13 +82,15 @@
         copy(keys.at[0], near.at[0:W, :], 1),
         copy(values.at[0], near.at[W : 2 * W, :], 2),
         copy(mixer.at[0, W - 16 : W, cols(HEADS + 1)], ends, 3),
+    ] + [
+        copy(source, scalars.at[n], 4 + n) for n, source in enumerate((decay_log, bias, residual))
     ]
     for c in first:
         c.start()
     later = [jnp.bitwise_and(lax.shift_right_logical(me, b), 1) == 0 for b in range(bits)]
     forward, backward = [], []
     for b in range(bits):
-        at = 4 + b * (GROUPS + 6)
+        at = 7 + b * (GROUPS + 6)
         forward.append(
             [
                 copy(mixer.at[0, :, cols(g)], bulk[b].at[cols(g), :], at + g)
@@ -126,11 +123,14 @@
 
     for c in first:
         c.wait()
+    rows = [jnp.full((1, W), scalars[n, h], F32) for n in range(3) for h in range(HEADS)]
+    rate = -jnp.exp(jnp.concatenate(rows[:HEADS], axis=0))
+    consts[...] = jnp.concatenate([rate] + rows[HEADS:] + [jnp.zeros((HEADS, W), F32)], axis=0)
     pieces = in_pieces(size[...], 12).astype(F32)
     last = ends[...].astype(F32)[12:16]
     extra[...] = jnp.concatenate([pieces, last], axis=0).astype(BF16)
     for b in range(bits):
-        at = 4 + bits * (GROUPS + 6) + b
+        at = 7 + bits * (GROUPS + 6) + b
         sized = copy(extra, bulk[b].at[STEP_ROW:BULK_ROWS, :], at)
         forward[b].append(sized)
         backward[b].append(sized)
@@ -204,19 +204,92 @@
         parts[k - 1][W : 2 * W, :] = value_acc[cols(k)].astype(BF16)
 
 
-def head_column(ref, lanes):
-    return jnp.concatenate([jnp.full((1, lanes), ref[h], F32) for h in range(HEADS)], axis=0)
-
-
 def sigmoid(v):
     return 0.5 * jnp.tanh(0.5 * v) + 0.5
 
 
+def convolve(weight, place, g, count=W):
+    total = place[5 : 5 + count, :] * weight[0:1, cols(g)]
+    for offset in range(1, TAPS):
+        at = 5 + offset
+        total = total + place[at : at + count, :] * weight[offset : offset + 1, cols(g)]
+    return total
+
+
+def step_table(pieces, bias, rate):
+    slots = len(pieces)
+    raw = jnp.concatenate(pieces, axis=0) + jnp.concatenate([bias] * slots, axis=0)
+    sizes = jnp.maximum(raw, 0.0) + jnp.log(1.0 + jnp.exp(-jnp.abs(raw)))
+    decays = sizes * jnp.concatenate([rate] * slots, axis=0)
+    upto = (iota2(0) <= iota2(1)).astype(F32)
+    return raw, sizes, dot(decays, upto, precise=True)
+
+
+def as_columns(table):
+    used = HEADS * len(table)
+    columns = jnp.transpose(jnp.concatenate(table + [jnp.zeros((W - used, W), F32)], axis=0))
+
+    def column(group, h):
+        at = HEADS * group + h
+        return columns[:, at : at + 1]
+
+    return column
+
+
+def with_sum(sums, kind, h, array):
+    lane = lax.broadcasted_iota(jnp.int32, sums.shape, 1)
+    return jnp.where(lane == HEADS * kind + h, jnp.sum(array, axis=1, keepdims=True), sums)
+
+
+def join(top, rest):
+    return jnp.concatenate([top, rest], axis=0)
+
+
+def own_body(mixer, step, weight, consts, cotan, *outs):
+    ext, acts, slopes, mixed_out, maps, sums_out, rows_out = outs
+    first = iota2(0) < TAPS - 1
+    for g in range(GROUPS):
+        place = ext.at[g]
+        place[0:8, :] = jnp.zeros((8, W), F32)
+        place[8 : 8 + W, :] = mixer[0, :, cols(g)].astype(F32)
+        pre = convolve(weight, place, g)
+        sig = sigmoid(pre)
+        acts[g] = jnp.where(first, 0.0, pre * sig)
+        slopes[g] = sig + pre * sig * (1.0 - sig)
+    _, size, cum = step_table([step[0]], consts[4:8], consts[0:4])
+    column = as_columns([cum, size])
+    map_in_s, map_out_s = split(acts[HEADS]), split(acts[HEADS + 1])
+    meets = dot_split(map_in_s, map_out_s, NT)
+    upper = iota2(0) <= iota2(1)
+    grad_meets = jnp.zeros((W, W), F32)
+    sums = jnp.zeros((W, W), F32)
+    out_rows, skip_rows = [], []
+    for h in range(HEADS):
+        cot_b = cotan[0, :, cols(h)]
+        act = acts[h]
+        falloff = jnp.where(upper, jnp.exp(cum[h : h + 1] - column(0, h)), 0.0)
+        pair = dot_split(split(act * column(1, h)), cot_b, NT) * falloff
+        grad_meets = grad_meets + pair
+        flow = pair * meets
+        mixed = dot_split(split(falloff * meets), cot_b)
+        mixed_out[h] = mixed
+        out_rows.append(jnp.sum(flow, axis=0, keepdims=True))
+        sums = with_sum(sums, 0, h, -flow)
+        sums = with_sum(sums, 2, h, mixed * act)
+        skip_rows.append(jnp.sum(cot_b.astype(F32) * act, axis=0, keepdims=True))
+    grad_meets_b = grad_meets.astype(BF16)
+    maps[0] = dot(grad_meets_b, map_out_s[0])
+    maps[1] = dot(grad_meets_b, map_in_s[0], TN)
+    sums_out[...] = sums
+    rows_out[...] = jnp.concatenate(out_rows + skip_rows, axis=0)
+
+
 def mixer_body(peers, *refs):
-    mixer, step, weight, decay_log, bias, residual, cotan = refs[:7]
-    bulk = refs[7 : 7 + peers]
-    step_grad, grads, halo, pay = refs[7 + peers : 11 + peers]
-    tails, ext, peer_ext, states, adjoints, acts, slopes = refs[11 + peers :]
+    mixer, step, weight, consts, cotan = refs[:5]
+    ext, acts, slopes, mixed_in, maps, sums_in, rows_in = refs[5:12]
+    bulk = refs[12 : 12 + peers]
+    grads, halo, pay = refs[12 + peers : 15 + peers]
+    tails, first_ext, peer_ext, states, adjoints = refs[15 + peers :]
     me = lax.axis_index("ctx")
     slots = peers + 1
     index = [me] + [jnp.bitwise_xor(me, k) for k in range(1, slots)]
@@ -247,12 +320,8 @@
     for k in range(1, slots):
         sent = bulk[k - 1][STEP_ROW:BULK_ROWS, :].astype(F32)
         pieces.append(sent[0:4] + sent[4:8] + sent[8:12])
-    rate = -jnp.exp(head_column(decay_log, W))
-    raw = jnp.concatenate(pieces, axis=0) + jnp.concatenate([head_column(bias, W)] * slots, axis=0)
-    sizes = jnp.maximum(raw, 0.0) + jnp.log(1.0 + jnp.exp(-jnp.abs(raw)))
-    decays = sizes * jnp.concatenate([rate] * slots, axis=0)
-    upto = (iota2(0) <= iota2(1)).astype(F32)
-    cumulative = dot(decays, upto, precise=True)
+    rate, bias = consts[0:4], consts[4:8]
+    raw, sizes, cumulative = step_table(pieces, bias, rate)
 
     def rows_of(array, k):
         return array[HEADS * k : HEADS * (k + 1)]
@@ -273,24 +342,13 @@
         cum = rows_of(cumulative, k)
         span = jnp.where(earlier, totals[k] - cum, cum) + between
         table.append(jnp.exp(span) * jnp.where(earlier, rows_of(sizes, k), 1.0))
-    table.append(jnp.zeros((W - HEADS * len(table), W), F32))
-    columns = jnp.transpose(jnp.concatenate(table, axis=0))
-
-    def column(group, h):
-        at = HEADS * group + h
-        return columns[:, at : at + 1]
-
-    def convolve(place, g):
-        total = place[5 : 5 + W, :] * weight[0:1, cols(g)]
-        for offset in range(1, TAPS):
-            total = total + place[5 + offset : 5 + offset + W, :] * weight[offset : offset + 1, cols(g)]
-        return total
+    column = as_columns(table)
 
     def peer_act(k, at, g):
         place = peer_ext.at[(k - 1) * GROUPS + g]
         place[0:8, :] = tails[index[k], 16 * g : 16 * g + 16, :].astype(F32)[8:16]
         place[8 : 8 + W, :] = bulk[k - 1][cols(at), :].astype(F32)
-        pre = convolve(place, g)
+        pre = convolve(weight, place, g)
         return pre * sigmoid(pre)
 
     states[...] = jnp.zeros_like(states)
@@ -312,62 +370,77 @@
                 read = split(map_out * table[3 + k][h : h + 1])
                 adjoints[h] = adjoints[h] + dot_split(read, bulk[k - 1][cols(h), :])
 
+    early = lax.broadcasted_iota(jnp.int32, (8, W), 0) < TAPS - 1
+    first_acts, first_slopes, new_acts = [], [], []
     for g in range(GROUPS):
-        place = ext.at[g]
+        place = first_ext.at[g]
         place[0:8, :] = tails[me, 16 * g : 16 * g + 16, :].astype(F32)[8:16]
-        place[8 : 8 + W, :] = mixer[0, :, cols(g)].astype(F32)
-        pre = convolve(place, g)
+        place[8:16, :] = ext[g, 8:16, :]
+        pre = convolve(weight, place, g, 8)
         sig = sigmoid(pre)
-        acts[g] = pre * sig
-        slopes[g] = sig + pre * sig * (1.0 - sig)
-
-    map_in, map_out = acts[HEADS], acts[HEADS + 1]
+        first_acts.append(pre * sig)
+        first_slopes.append(sig + pre * sig * (1.0 - sig))
+        new_acts.append(jnp.where(early, pre * sig, 0.0))
+
+    def act_of(g):
+        return join(first_acts[g], acts[g, 8:W, :])
+
+    def slope_of(g):
+        return join(first_slopes[g], slopes[g, 8:W, :])
+
+    map_in, map_out = act_of(HEADS), act_of(HEADS + 1)
     map_in_s, map_out_s = split(map_in), split(map_out)
-    meets = dot_split(map_in_s, map_out_s, NT)
-    upper = iota2(0) <= iota2(1)
-    lane = iota2(1)
-    grad_in = jnp.zeros((W, W), F32)
-    grad_out = jnp.zeros((W, W), F32)
-    grad_meets = jnp.zeros((W, W), F32)
-    sums = jnp.zeros((W, W), F32)
+    new_in = new_acts[HEADS]
+    new_meets = dot_split(split(new_in), map_out_s, NT)
+    upper = lax.broadcasted_iota(jnp.int32, (8, W), 0) <= lax.broadcasted_iota(
+        jnp.int32, (8, W), 1
+    )
+    grad_in, grad_out = maps[0], maps[1]
+    new_grad_meets = jnp.zeros((8, W), F32)
+    sums = sums_in[...]
     out_rows, pass_rows, skip_rows = [], [], []
-
-    def with_sum(sums, kind, h, array):
-        return jnp.where(lane == HEADS * kind + h, jnp.sum(array, axis=1, keepdims=True), sums)
 
     for h in range(HEADS):
         cot_b = cotan[0, :, cols(h)]
         cot = cot_b.astype(F32)
-        act = acts[h]
+        act = act_of(h)
+        new_act = new_acts[h]
         size = column(1, h)
         tail = column(3, h)
-        scaled = act * size
         state = states[h]
         adjoint = adjoints[h]
         adjoint_s = split(adjoint)
-        falloff = jnp.where(upper, jnp.exp(own_cum[h : h + 1] - column(0, h)), 0.0)
-        pair = dot_split(split(scaled), cot_b, NT) * falloff
-        grad_meets = grad_meets + pair
-        flow = pair * meets
+        falloff = jnp.where(upper, jnp.exp(own_cum[h : h + 1] - column(0, h)[0:8]), 0.0)
+        pair = dot_split(split(new_act * size[0:8]), cot_b, NT) * falloff
+        new_grad_meets = new_grad_meets + pair
+        flow = pair * new_meets
+        new_mixed = dot_split(split(falloff * new_meets), cot_b)
         projected = tail * dot_split(map_in_s, adjoint_s)
-        mixed = dot_split(split(falloff * meets), cot_b)
+        mixed = mixed_in[h]
+        mixed = join(mixed[0:8] + new_mixed, mixed[8:W])
         grad_scaled = mixed + projected
         lead_read = column(2, h) * dot_split(cot_b, split(state), NT)
         grad_out = grad_out + lead_read
-        grad_in = grad_in + dot((scaled * tail).astype(BF16), adjoint_s[0], NT)
-        out_rows.append(jnp.sum(flow, axis=0, keepdims=True))
-        sums = with_sum(sums, 0, h, lead_read * map_out - flow)
-        sums = with_sum(sums, 1, h, projected * act)
-        sums = with_sum(sums, 2, h, mixed * act)
+        grad_in = grad_in + dot((act * size * tail).astype(BF16), adjoint_s[0], NT)
+        out_rows.append(rows_in[h : h + 1] + jnp.sum(flow, axis=0, keepdims=True))
+        carried = lead_read * map_out
+        trailing = projected * act
+        carried = join(carried[0:8] - flow, carried[8:W])
+        extra = with_sum(jnp.zeros((W, W), F32), 0, h, carried)
+        extra = with_sum(extra, 1, h, trailing)
+        extra8 = with_sum(jnp.zeros((8, W), F32), 2, h, new_mixed * new_act)
+        sums = sums + extra
+        sums = join(sums[0:8] + extra8, sums[8:W])
         passed = jnp.sum(jnp.sum(state * adjoint, axis=0, keepdims=True), axis=1, keepdims=True)
         pass_rows.append(jnp.broadcast_to(passed, (1, W)))
-        skip_rows.append(jnp.sum(cot * act, axis=0, keepdims=True))
-        grads[h, 0:W, :] = (residual[h] * cot + grad_scaled * size) * slopes[h]
-    grad_meets_b = grad_meets.astype(BF16)
-    grad_out = grad_out + dot(grad_meets_b, map_in_s[0], TN)
-    grad_in = grad_in + dot(grad_meets_b, map_out_s[0])
-    grads[HEADS, 0:W, :] = grad_in * slopes[HEADS]
-    grads[HEADS + 1, 0:W, :] = grad_out * slopes[HEADS + 1]
+        skipped = jnp.sum(cot[0:8] * new_act, axis=0, keepdims=True)
+        skip_rows.append(rows_in[HEADS + h : HEADS + h + 1] + skipped)
+        grads[h, 0:W, :] = (consts[8 + h : 9 + h] * cot + grad_scaled * size) * slope_of(h)
+    new_b = new_grad_meets.astype(BF16)
+    grad_out = grad_out + dot(new_b, new_in.astype(BF16), TN)
+    grad_in = join(grad_in[0:8] + dot(new_b, map_out_s[0]), grad_in[8:W])
+    grads[HEADS, 0:W, :] = grad_in * slope_of(HEADS)
+    grads[HEADS + 1, 0:W, :] = grad_out * slope_of(HEADS + 1)
     sum_rows = jnp.transpose(sums)
 
     since = (iota2(0) >= iota2(1)).astype(F32)
@@ -380,23 +453,29 @@
     )
     grad_step = grad_decay * rate + rows_of(sum_rows, 2) + trail
     grad_raw = grad_step * sigmoid(rows_of(raw, 0))
-    step_grad[0] = grad_raw
     pay[24:28, :] = grad_decay * own_size * rate
     pay[28:32, :] = grad_raw
     pay[32:36, :] = jnp.concatenate(skip_rows, axis=0)
     pay[36:40, :] = jnp.zeros((4, W), F32)
 
-    halo[...] = small_rows([grads[g, 0:8, :][0:3] for g in range(GROUPS)])
+    for g in range(GROUPS):
+        halo[8 * g : 8 * g + 8, :] = grads[g, 0:8, :]
     for g in range(GROUPS):
         grads[g, W : W + 8, :] = jnp.zeros((8, W), F32)
         grad = grads[g, 0:W, :]
         for offset in range(TAPS):
             pay[4 * g + offset : 4 * g + offset + 1, :] = jnp.sum(
-                grad * ext[g, 5 + offset : 5 + offset + W, :], axis=0, keepdims=True
+                grad * join(
+                    first_ext[g, 5 + offset : 13 + offset, :],
+                    ext[g, 13 + offset : 5 + offset + W, :],
+                ),
+                axis=0,
+                keepdims=True,
             )
 
 
-def rows_body(grads, weight, input_grad, edge):
+def rows_body(grads, weight, pay, input_grad, edge, step_grad):
+    step_grad[0] = pay[28:32, :]
     for g in range(GROUPS):
         total = grads[g, TAPS - 1 : TAPS - 1 + W, :] * weight[0:1, cols(g)]
         for offset in range(1, TAPS):
@@ -412,11 +491,14 @@
     total_out, *mixed = refs[3 + peers :]
     total = pay[...] + other[...]
     total_out[...] = total
-    pieces = in_pieces(total, MIX_ROWS - SUM_ROW)
+    sums = total[0:SUM_ROWS]
+    high = sums.astype(BF16).astype(F32)
+    edges = [halo[8 * g : 8 * g + 3, :] for g in range(GROUPS)]
+    rest = jnp.zeros((MIX_ROWS - KV_ROWS - 2 * SUM_ROWS - 3 * GROUPS, W), F32)
+    pieces = jnp.concatenate([high, sums - high] + edges + [rest], axis=0).astype(BF16)
     for part, out in zip(parts, mixed):
         out[0:KV_ROWS, :] = part[...]
-        out[KV_ROWS:SUM_ROW, :] = halo[...]
-        out[SUM_ROW:MIX_ROWS, :] = pieces
+        out[KV_ROWS:MIX_ROWS, :] = pieces
 
 
 def finish_body(peers, count, *refs):
@@ -425,18 +507,16 @@
     input_grad, key_grad, value_grad, conv_grad, decay_grad, bias_grad, skip_grad = refs[5 + peers :]
     me = lax.axis_index("ctx")
     both = own[...]
-    total = pay[...]
-    halo = jnp.zeros((32, W), F32)
+    total = pay[0:SUM_ROWS, :]
+    halo = jnp.zeros((3 * GROUPS, W), F32)
     for k in range(1, peers + 1):
         other = jnp.bitwise_xor(me, k)
         sent = mixed[k - 1][0:KV_ROWS, :].astype(F32)
         both = both + jnp.where(other > me, sent, 0.0)
-        edges = mixed[k - 1][KV_ROWS:SUM_ROW, :].astype(F32)
+        pieces = mixed[k - 1][KV_ROWS:MIX_ROWS, :].astype(F32)
+        total = total + pieces[0:SUM_ROWS] + pieces[SUM_ROWS : 2 * SUM_ROWS]
+        edges = pieces[2 * SUM_ROWS : 2 * SUM_ROWS + 3 * GROUPS]
         halo = halo + jnp.where(other == me + 1, edges, 0.0)
-        pieces = mixed[k - 1][SUM_ROW:MIX_ROWS, :].astype(F32)
-        total = total + (
-            pieces[0:PAY_ROWS] + pieces[PAY_ROWS : 2 * PAY_ROWS] + pieces[2 * PAY_ROWS : 3 * PAY_ROWS]
-        )
     key_grad[0] = both[0:W].astype(BF16)
     value_grad[0] = both[W : 2 * W].astype(BF16)
     row = lax.broadcasted_iota(jnp.int32, (16, W), 0)
@@ -452,7 +532,7 @@
     total = total * (1.0 / count)
     for g in range(GROUPS):
         conv_grad[:, cols(g)] = total[4 * g : 4 * g + 4]
-    sums = jnp.sum(total[24:40], axis=1, keepdims=True)
+    sums = jnp.sum(total[24:SUM_ROWS], axis=1, keepdims=True)
     for h in range(HEADS):
         decay_grad[h] = jnp.sum(sums[h : h + 1])
         bias_grad[h] = jnp.sum(sums[4 + h : 5 + h])
@@ -486,23 +566,34 @@
 
     hbm = pl.BlockSpec(memory_space=pltpu.HBM)
     params = pltpu.CompilerParams(vmem_limit_bytes=LIMIT)
-    near, *bulk = pl.pallas_call(
+    near, *bulk, consts = pl.pallas_call(
         lambda *refs: pack_body(bits, *refs),
-        out_shape=[shape((KV_ROWS, W), BF16)] + [shape((BULK_ROWS, W), BF16)] * bits,
-        in_specs=[hbm] * 5,
-        out_specs=[vmem] * (1 + bits),
+        out_shape=[shape((KV_ROWS, W), BF16)] + [shape((BULK_ROWS, W), BF16)] * bits
+        + [shape((4 * HEADS, W), F32)],
+        in_specs=[hbm] * 8,
+        out_specs=[vmem] * (2 + bits),
         scratch_shapes=[
             pltpu.VMEM((HEADS, W), F32),
             pltpu.VMEM((16, W), BF16),
             pltpu.VMEM((16, W), BF16),
-            pltpu.SemaphoreType.DMA((4 + bits * (GROUPS + 7),)),
+            pltpu.SMEM((3, HEADS), F32),
+            pltpu.SemaphoreType.DMA((7 + bits * (GROUPS + 7),)),
         ],
         compiler_params=params,
         name="pack",
     )(
         *(
             pltpu.with_memory_space_constraint(array, pltpu.HBM)
-            for array in (mixer_input, step_input, mixer_cotangent, attn_keys, attn_values)
+            for array in (
+                mixer_input,
+                step_input,
+                mixer_cotangent,
+                attn_keys,
+                attn_values,
+                decay_log,
+                step_bias,
+                residual,
+            )
         )
     )
 
@@ -513,37 +604,69 @@
     nears = [swap(near, k, lambda i, j: j > i) for k in range(1, ctx)]
     bulks = [swap(bulk[k.bit_length() - 1], k) for k in range(1, ctx)]
 
-    step_grad, grads, halo, pay = pl.pallas_call(
+    kept = pl.pallas_call(
+        own_body,
+        out_shape=[
+            shape((GROUPS, W + 8, W), F32),
+            shape((GROUPS, W, W), F32),
+            shape((GROUPS, W, W), F32),
+            shape((HEADS, W, W), F32),
+            shape((2, W, W), F32),
+            shape((W, W), F32),
+            shape((2 * HEADS, W), F32),
+        ],
+        in_specs=[vmem] * 5,
+        out_specs=[vmem] * 7,
+        compiler_params=params,
+        name="own",
+    )(
+        mixer_input,
+        step_input,
+        conv_weight,
+        consts,
+        mixer_cotangent,
+    )
+
+    grads, halo, pay = pl.pallas_call(
         lambda *refs: mixer_body(peers, *refs),
         out_shape=[
-            shape(step_input.shape, F32),
             shape((GROUPS, W + 8, W), F32),
-            shape((32, W), BF16),
+            shape((8 * GROUPS, W), F32),
             shape((PAY_ROWS, W), F32),
         ],
-        in_specs=[vmem] * 3 + [smem] * 3 + [vmem] * (1 + peers),
-        out_specs=[vmem] * 4,
+        in_specs=[vmem] * (12 + peers),
+        out_specs=[vmem] * 3,
         scratch_shapes=[
             pltpu.VMEM((ctx + 1, 16 * GROUPS, W), BF16),
-            pltpu.VMEM((GROUPS, W + 8, W), F32),
+            pltpu.VMEM((GROUPS, 24, W), F32),
             pltpu.VMEM((peers * GROUPS, W + 8, W), F32),
             pltpu.VMEM((HEADS, W, W), F32),
             pltpu.VMEM((HEADS, W, W), F32),
-            pltpu.VMEM((GROUPS, W, W), F32),
-            pltpu.VMEM((GROUPS, W, W), F32),
         ],
         compiler_params=params,
         name="mixer",
-    )(mixer_input, step_input, conv_weight, decay_log, step_bias, residual, mixer_cotangent, *bulks)
-
-    input_grad, edge = pl.pallas_call(
+    )(
+        mixer_input,
+        step_input,
+        conv_weight,
+        consts,
+        mixer_cotangent,
+        *kept,
+        *bulks,
+    )
+
+    input_grad, edge, step_grad = pl.pallas_call(
         rows_body,
-        out_shape=[shape(mixer_input.shape, BF16), shape((16, GROUPS * W), F32)],
-        in_specs=[vmem] * 2,
-        out_specs=[vmem] * 2,
+        out_shape=[
+            shape(mixer_input.shape, BF16),
+            shape((16, GROUPS * W), F32),
+            shape(step_input.shape, F32),
+        ],
+        in_specs=[vmem] * 3,
+        out_specs=[vmem] * 3,
         compiler_params=params,
         name="rows",
-    )(grads, conv_weight)
+    )(grads, conv_weight, pay)
 
     half, sums = pl.pallas_call(
         lambda *refs: half_body(peers, *refs),

time: 39.1 us -> 41.4 us (1.059)
  starting transfers between devices: 20.9 us -> 24 us
  waiting for transfers between devices: 7.38 us -> 6.21 us
    ppermute x12, starting transfers between devices: 20.9 us -> 24 us  [swap(): return lax.ppermute(array, axis, pairs)]
    ppermute x12, waiting for transfers between devices: 7.38 us -> 6.21 us  [swap(): return lax.ppermute(array, axis, pairs)]
    pallas_call x1, Pallas kernels: 0.11 us -> 0.66 us  [on_device(): pl.pallas_call(rows_body, out_shape=[shape(mixer_input.shape, BF16), shap...]
    pallas_call x1 -> x2, Pallas kernels: 3.99 us -> 3.75 us  [the longest x1 2.7 us: on_device(): pl.pallas_call(lambda *refs: mixer_body(peers, *refs), out_shape=[shape((...]
  transfers between devices with their start and end apart: 12 -> 12, of which waited for: 5 -> 5; matrix products, arithmetic and copies ran while one was open for 0% -> 0% of each run, Pallas kernels for 20% -> 19%
where the time goes in v3:
time: 41.4 us; the launch traced here: 41.2 us
  starting transfers between devices  24 us (58%)
  Pallas kernels  10 us (24%)
  waiting for transfers between devices  6.21 us (15%)
  between operations  0.86 us (2%)
    ppermute x12, starting transfers between devices, swap(): return lax.ppermute(array, axis, pairs)  24 us
    ppermute x12, waiting for transfers between devices, swap(): return lax.ppermute(array, axis, pairs)  6.21 us
    pallas_call x1, Pallas kernels, on_device(): pl.pallas_call(lambda *refs: mixer_body(peers, *refs), out_shape=[shape((...  2.7 us
    pallas_call x1, Pallas kernels, on_device(): pl.pallas_call(lambda *refs: attend_body(peers, *refs), out_shape=[shape(...  2.06 us
    pallas_call x1, Pallas kernels, on_device(): pl.pallas_call(lambda *refs: half_body(peers, *refs), out_shape=[shape((1...  1.46 us
    pallas_call x1, Pallas kernels, on_device(): pl.pallas_call(lambda *refs: pack_body(bits, *refs), out_shape=[shape((KV...  1.32 us
    pallas_call x1, Pallas kernels, on_device(): pl.pallas_call(own_body, out_shape=[shape((GROUPS, W + 8, W), F32), shape...  1.06 us
  transfers between devices with their start and end apart: 12, of which 5 were waited for; matrix products, arithmetic and copies ran while one was open for 0% of the time, Pallas kernels for 19%

profile of v3, /device:TPU:0, one launch (start us, length us, event | category | flops | bytes accessed | tf_op | source)
XLA Modules:
  0.0 41.2 jit_solution(9297518102961902677)
XLA Ops:
  0.7 1.3 %pack.1 = (bf16[256,128]{1,0:T(8,128)(2,1)S(1)}, bf16[656,128]{1,0:T(8,128)(2,1)S(1)}, bf16[656,128]{1,0:T(8,128)(2,1)S(1)}, f32[16,128]{1,0:T(8,128)S(1)}) custom-call(bf16[1,128,768]{2,1,0:T(8,128)(2,1)} %refs_0_.5, f32[1,4,128]{2,1,0:T(4,128)} %bitcast.2, bf16[1,128,512]{2,1,0:T(8,128)(2,1)} %refs_4_.3, bf16[1,128,128]{2,1,0:T(8,128)(2,1)} %refs_1_.3, ...), custom_call_target="tpu_custom_call" | custom-call | tf_op jit(solution)/shard_map/pack/pallas_call | solution.py:569
  2.0 3.1 %collective-permute-start.1 = (bf16[656,128]{1,0:T(8,128)(2,1)S(1)}, bf16[656,128]{1,0:T(8,128)(2,1)S(1)}, u32[]{:S(2)}, u32[]{:S(2)}) collective-permute-start(bf16[656,128]{1,0:T(8,128)(2,1)S(1)} %get-tuple-element.53), channel_id=1, source_target_pairs={{0,2},{1,3},{2,0},{3,1},{4,6},{5,7},{6,4},{7,5},{8,10},{9,11},{10,... | collective-permute-start | bytes 503816 | tf_op jit(solution)/shard_map/ppermute | solution.py:602
  5.1 1.4 %collective-permute-start.2 = (bf16[656,128]{1,0:T(8,128)(2,1)S(1)}, bf16[656,128]{1,0:T(8,128)(2,1)S(1)}, u32[]{:S(2)}, u32[]{:S(2)}) collective-permute-start(bf16[656,128]{1,0:T(8,128)(2,1)S(1)} %get-tuple-element.53), channel_id=1, source_target_pairs={{0,3},{1,2},{2,1},{3,0},{4,7},{5,6},{6,5},{7,4},{8,11},{9,10},{10,... | collective-permute-start | bytes 503816 | tf_op jit(solution)/shard_map/ppermute | solution.py:602
  6.5 0.1 collective-permute-start
  6.6 3.8 %collective-permute-start.3 = (bf16[256,128]{1,0:T(8,128)(2,1)S(1)}, bf16[256,128]{1,0:T(8,128)(2,1)S(1)}, u32[]{:S(2)}, u32[]{:S(2)}) collective-permute-start(bf16[256,128]{1,0:T(8,128)(2,1)S(1)} %get-tuple-element.58), channel_id=1, source_target_pairs={{0,1},{2,3},{4,5},{6,7},{8,9},{10,11},{12,13},{14,15},{16,17},{18,... | collective-permute-start | bytes 196616 | tf_op jit(solution)/shard_map/ppermute | solution.py:602
  10.4 3.4 %collective-permute-start.4 = (bf16[256,128]{1,0:T(8,128)(2,1)S(1)}, bf16[256,128]{1,0:T(8,128)(2,1)S(1)}, u32[]{:S(2)}, u32[]{:S(2)}) collective-permute-start(bf16[256,128]{1,0:T(8,128)(2,1)S(1)} %get-tuple-element.58), channel_id=1, source_target_pairs={{0,2},{1,3},{4,6},{5,7},{8,10},{9,11},{12,14},{13,15},{16,18},{17,... | collective-permute-start | bytes 196616 | tf_op jit(solution)/shard_map/ppermute | solution.py:602
  13.9 0.0 collective-permute-done.1.refs_13_
  13.9 4.3 %collective-permute-start.5 = (bf16[256,128]{1,0:T(8,128)(2,1)S(1)}, bf16[256,128]{1,0:T(8,128)(2,1)S(1)}, u32[]{:S(2)}, u32[]{:S(2)}) collective-permute-start(bf16[256,128]{1,0:T(8,128)(2,1)S(1)} %get-tuple-element.58), channel_id=1, source_target_pairs={{0,3},{1,2},{4,7},{5,6},{8,11},{9,10},{12,15},{13,14},{16,19},{17,... | collective-permute-start | bytes 196616 | tf_op jit(solution)/shard_map/ppermute | solution.py:602
  18.3 1.1 %own.1 = (f32[6,136,128]{2,1,0:T(8,128)S(1)}, f32[6,128,128]{2,1,0:T(8,128)S(1)}, f32[6,128,128]{2,1,0:T(8,128)S(1)}, f32[4,128,128]{2,1,0:T(8,128)S(1)}, f32[2,...) custom-call(bf16[1,128,768]{2,1,0:T(8,128)(2,1)S(1)} %copy-done, f32[1,4,128]{2,1,0:T(4,128)S(1)} %bitcast.3, ...), custom_call_target="tpu_custom_call" | custom-call | tf_op jit(solution)/shard_map/own/pallas_call | solution.py:607
  19.3 0.0 collective-permute-done.2.refs_14_
  19.3 0.0 collective-permute-done.refs_12_
  19.3 0.0 copy-start.2
  19.4 0.0 copy-start.3
  19.4 2.7 %mixer.3 = (f32[6,136,128]{2,1,0:T(8,128)S(1)}, f32[48,128]{1,0:T(8,128)S(1)}, f32[40,128]{1,0:T(8,128)S(1)}) custom-call(bf16[1,128,768]{2,1,0:T(8,128)(2,1)S(1)} %copy-done, f32[1,4,128]{2,1,0:T(4,128)S(1)} %bitcast.4, f32[4,768]{1,0:T(4,128)S(1)} %copy-done.6, f32[16,128]{1,0:T(8,128)S(1)} %get-tuple-element.44.consts.refs_3_, ...), custom_call_target="tpu_custom_call" | custom-call | tf_op jit(solution)/shard_map/mixer/pallas_call | solution.py:630
  22.1 0.1 collective-permute-start.6
  22.2 1.2 %collective-permute-done.6 = f32[40,128]{1,0:T(8,128)S(1)} collective-permute-done((f32[40,128]{1,0:T(8,128)S(1)}, f32[40,128]{1,0:T(8,128)S(1)}, u32[]{:S(2)}, u32[]{:S(2)}) %collective-permute-start.6) | collective-permute-done | bytes 20512 | tf_op jit(solution)/shard_map/ppermute | solution.py:602
  23.3 1.6 %collective-permute-start.7 = (f32[40,128]{1,0:T(8,128)S(1)}, f32[40,128]{1,0:T(8,128)S(1)}, u32[]{:S(2)}, u32[]{:S(2)}) collective-permute-start(f32[40,128]{1,0:T(8,128)S(1)} %add.6), channel_id=1, source_target_pairs={{0,8},{4,12},{8,0},{12,4},{16,24},{20,28},{24,16},{28,20},{1,9},{5... | collective-permute-start | bytes 61448 | tf_op jit(solution)/shard_map/ppermute | solution.py:602
  25.0 2.2 %collective-permute-done.7 = f32[40,128]{1,0:T(8,128)S(1)} collective-permute-done((f32[40,128]{1,0:T(8,128)S(1)}, f32[40,128]{1,0:T(8,128)S(1)}, u32[]{:S(2)}, u32[]{:S(2)}) %collective-permute-start.7) | collective-permute-done | bytes 20512 | tf_op jit(solution)/shard_map/ppermute | solution.py:602
  27.2 2.6 %collective-permute-start.8 = (f32[40,128]{1,0:T(8,128)S(1)}, f32[40,128]{1,0:T(8,128)S(1)}, u32[]{:S(2)}, u32[]{:S(2)}) collective-permute-start(f32[40,128]{1,0:T(8,128)S(1)} %add.7.refs_0_), channel_id=1, source_target_pairs={{0,16},{4,20},{8,24},{12,28},{16,0},{20,4},{24,8},{28,12},{1,17},{... | collective-permute-start | bytes 61448 | tf_op jit(solution)/shard_map/ppermute | solution.py:602
  29.8 0.0 collective-permute-done.4.refs_5_
  29.8 0.0 collective-permute-done.5.refs_6_
  29.8 1.5 %half.1 = (bf16[1,128,256]{2,1,0:T(8,128)(2,1)S(1)}, f32[2,512,128]{2,1,0:T(8,128)S(1)}) custom-call(bf16[1,128,512]{2,1,0:T(8,128)(2,1)S(1)} %copy-done.2, bf16[1,128,128]{2,1,0:T(8,128)(2,1)S(1)} %copy-done.4, bf16[1,128,128]{2,1,0:T(8,128)(2,1)S(1)} %copy-done.5, bf16[1,128,512]{2,1,0:T(8,128)(2,1)S(1)} %copy-done.3, ...), custom_call_target="tpu_custom_call" | custom-call | tf_op jit(solution)/shard_map/half/pallas_call | solution.py:671
  31.3 2.1 %attend.1 = (bf16[1,128,512]{2,1,0:T(8,128)(2,1)}, f32[256,128]{1,0:T(8,128)S(1)}, bf16[256,128]{1,0:T(8,128)(2,1)S(1)}, bf16[256,128]{1,0:T(8,128)(2,1)S(1)}, bf16[256,128]{1,0:T(8,128)(2,1)S(1)}) custom-call(bf16[1,128,512]{2,1,0:T(8,128)(2,1)S(1)} %copy-done.2, bf16[1,128,128]{2,1,0:T(8,128)(2,1)S(1)} %copy-done.4, bf16[1,128,128]{2,1,0:T(8,128)(2,1)S(1)} %copy-done.5, ...), custom_call_target="tpu_custom_call" | custom-call | tf_op jit(solution)/shard_map/attend/pallas_call | solution.py:683
  33.4 0.0 collective-permute-done.8.refs_1_
  33.4 0.1 collective-permute-start.10
  33.5 1.4 %collective-permute-start.11 = (bf16[352,128]{1,0:T(8,128)(2,1)S(1)}, bf16[352,128]{1,0:T(8,128)(2,1)S(1)}, u32[]{:S(2)}, u32[]{:S(2)}) collective-permute-start(bf16[352,128]{1,0:T(8,128)(2,1)S(1)} %get-tuple-element.69), channel_id=1, source_target_pairs={{0,3},{1,2},{2,1},{3,0},{4,7},{5,6},{6,5},{7,4},{8,11},{9,10},{10,... | collective-permute-start | bytes 270344 | tf_op jit(solution)/shard_map/ppermute | solution.py:602
  34.9 2.1 %collective-permute-start.9 = (bf16[352,128]{1,0:T(8,128)(2,1)S(1)}, bf16[352,128]{1,0:T(8,128)(2,1)S(1)}, u32[]{:S(2)}, u32[]{:S(2)}) collective-permute-start(bf16[352,128]{1,0:T(8,128)(2,1)S(1)} %get-tuple-element.67), channel_id=1, source_target_pairs={{0,1},{1,0},{2,3},{3,2},{4,5},{5,4},{6,7},{7,6},{8,9},{9,8},{10,11... | collective-permute-start | bytes 270344 | tf_op jit(solution)/shard_map/ppermute | solution.py:602
  37.0 0.7 %rows.1 = (bf16[1,128,768]{2,1,0:T(8,128)(2,1)S(1)}, f32[16,768]{1,0:T(8,128)S(1)}, f32[1,4,128]{2,1,0:T(4,128)}) custom-call(f32[6,136,128]{2,1,0:T(8,128)S(1)} %get-tuple-element.54.grads, f32[4,768]{1,0:T(4,128)S(1)} %copy-done.6, f32[40,128]{1,0:T(8,128)S(1)} %get-tuple-element.55.pay), custom_call_target="tpu_custom_call" | custom-call | tf_op jit(solution)/shard_map/rows/pallas_call | solution.py:658
  37.6 0.4 collective-permute-done.10.refs_6_
  38.0 1.0 %collective-permute-done.11.refs_7_ = bf16[352,128]{1,0:T(8,128)(2,1)S(1)} collective-permute-done((bf16[352,128]{1,0:T(8,128)(2,1)S(1)}, bf16[352,128]{1,0:T(8,128)(2,1)S(1)}, u32[]{:S(2)}, u32[]{:S(2)}) %collective-permute-start.11) | collective-permute-done | bytes 90144 | tf_op jit(solution)/shard_map/ppermute | solution.py:602
  39.0 1.5 %collective-permute-done.9.refs_5_ = bf16[352,128]{1,0:T(8,128)(2,1)S(1)} collective-permute-done((bf16[352,128]{1,0:T(8,128)(2,1)S(1)}, bf16[352,128]{1,0:T(8,128)(2,1)S(1)}, u32[]{:S(2)}, u32[]{:S(2)}) %collective-permute-start.9) | collective-permute-done | bytes 90144 | tf_op jit(solution)/shard_map/ppermute | solution.py:602
  40.4 0.8 %finish.1 = (bf16[1,128,768]{2,1,0:T(8,128)(2,1)}, bf16[1,128,128]{2,1,0:T(8,128)(2,1)}, bf16[1,128,128]{2,1,0:T(8,128)(2,1)}, f32[4,768]{1,0:T(4,128)}, f32[4]{0:T(128)}, /*index=5*/f32[4]{0:T(128)}, f32[4]{0:T(128)}) custom-call(bf16[1,128,768]{2,1,0:T(8,128)(2,1)S(1)} %get-tuple-element.56.refs_0_, f32[16,768]{1,0:T(8,128)S(1)} %get-tuple-element.57.refs_1_, ...), custom_call_target="tpu_custom_call" | custom-call | tf_op jit(solution)/shard_map/finish/pallas_call | solution.py:707
  (18 shorter events, 0.1 us)
Async XLA Ops:
  0.6 17.6 %copy-start = (bf16[1,128,768]{2,1,0:T(8,128)(2,1)S(1)}, bf16[1,128,768]{2,1,0:T(8,128)(2,1)}, u32[]{:S(2)}) copy-start(bf16[1,128,768]{2,1,0:T(8,128)(2,1)} %refs_0_.5) | copy-start | bytes 589828
  0.7 17.6 %copy-start.1 = (bf16[1,128,512]{2,1,0:T(8,128)(2,1)S(1)}, bf16[1,128,512]{2,1,0:T(8,128)(2,1)}, u32[]{:S(2)}) copy-start(bf16[1,128,512]{2,1,0:T(8,128)(2,1)} %refs_4_.3) | copy-start | bytes 393220
  0.7 17.6 %copy-start.6 = (f32[4,768]{1,0:T(4,128)S(1)}, f32[4,768]{1,0:T(4,128)}, u32[]{:S(2)}) copy-start(f32[4,768]{1,0:T(4,128)} %refs_2_.9) | copy-start | bytes 36868
  2.0 11.9 %collective-permute-start.1 = (bf16[656,128]{1,0:T(8,128)(2,1)S(1)}, bf16[656,128]{1,0:T(8,128)(2,1)S(1)}, u32[]{:S(2)}, u32[]{:S(2)}) collective-permute-start(bf16[656,128]{1,0:T(8,128)(2,1)S(1)} %get-tuple-element.53), channel_id=1, source_target_pairs={{0,2},{1,3},{2,0},{3,1},{4,6},{5,7},{6,4},{7,5},{8,10},{9,11},{10,... | collective-permute-start | bytes 503816 | tf_op jit(solution)/shard_map/ppermute | solution.py:602
  5.1 14.3 %collective-permute-start.2 = (bf16[656,128]{1,0:T(8,128)(2,1)S(1)}, bf16[656,128]{1,0:T(8,128)(2,1)S(1)}, u32[]{:S(2)}, u32[]{:S(2)}) collective-permute-start(bf16[656,128]{1,0:T(8,128)(2,1)S(1)} %get-tuple-element.53), channel_id=1, source_target_pairs={{0,3},{1,2},{2,1},{3,0},{4,7},{5,6},{6,5},{7,4},{8,11},{9,10},{10,... | collective-permute-start | bytes 503816 | tf_op jit(solution)/shard_map/ppermute | solution.py:602
  6.5 11.8 %copy-start.7 = (f32[1,128,4]{1,2,0:T(4,128)S(1)}, f32[1,128,4]{1,2,0:T(4,128)}, u32[]{:S(2)}) copy-start(f32[1,128,4]{1,2,0:T(4,128)} %param.12) | copy-start | bytes 6148
  6.5 12.8 %collective-permute-start = (bf16[656,128]{1,0:T(8,128)(2,1)S(1)}, bf16[656,128]{1,0:T(8,128)(2,1)S(1)}, u32[]{:S(2)}, u32[]{:S(2)}) collective-permute-start(bf16[656,128]{1,0:T(8,128)(2,1)S(1)} %get-tuple-element.52), channel_id=1, source_target_pairs={{0,1},{1,0},{2,3},{3,2},{4,5},{5,4},{6,7},{7,6},{8,9},{9,8},{10,11... | collective-permute-start | bytes 503816 | tf_op jit(solution)/shard_map/ppermute | solution.py:602
  6.6 23.2 %collective-permute-start.3 = (bf16[256,128]{1,0:T(8,128)(2,1)S(1)}, bf16[256,128]{1,0:T(8,128)(2,1)S(1)}, u32[]{:S(2)}, u32[]{:S(2)}) collective-permute-start(bf16[256,128]{1,0:T(8,128)(2,1)S(1)} %get-tuple-element.58), channel_id=1, source_target_pairs={{0,1},{2,3},{4,5},{6,7},{8,9},{10,11},{12,13},{14,15},{16,17},{18,... | collective-permute-start | bytes 196616 | tf_op jit(solution)/shard_map/ppermute | solution.py:602
  10.4 19.4 %collective-permute-start.4 = (bf16[256,128]{1,0:T(8,128)(2,1)S(1)}, bf16[256,128]{1,0:T(8,128)(2,1)S(1)}, u32[]{:S(2)}, u32[]{:S(2)}) collective-permute-start(bf16[256,128]{1,0:T(8,128)(2,1)S(1)} %get-tuple-element.58), channel_id=1, source_target_pairs={{0,2},{1,3},{4,6},{5,7},{8,10},{9,11},{12,14},{13,15},{16,18},{17,... | collective-permute-start | bytes 196616 | tf_op jit(solution)/shard_map/ppermute | solution.py:602
  13.9 15.9 %collective-permute-start.5 = (bf16[256,128]{1,0:T(8,128)(2,1)S(1)}, bf16[256,128]{1,0:T(8,128)(2,1)S(1)}, u32[]{:S(2)}, u32[]{:S(2)}) collective-permute-start(bf16[256,128]{1,0:T(8,128)(2,1)S(1)} %get-tuple-element.58), channel_id=1, source_target_pairs={{0,3},{1,2},{4,7},{5,6},{8,11},{9,10},{12,15},{13,14},{16,19},{17,... | collective-permute-start | bytes 196616 | tf_op jit(solution)/shard_map/ppermute | solution.py:602
  19.3 10.5 %copy-start.2 = (bf16[1,128,512]{2,1,0:T(8,128)(2,1)S(1)}, bf16[1,128,512]{2,1,0:T(8,128)(2,1)}, u32[]{:S(2)}) copy-start(bf16[1,128,512]{2,1,0:T(8,128)(2,1)} %refs_0_.7) | copy-start | bytes 393220
  19.4 10.5 %copy-start.3 = (bf16[1,128,512]{2,1,0:T(8,128)(2,1)S(1)}, bf16[1,128,512]{2,1,0:T(8,128)(2,1)}, u32[]{:S(2)}) copy-start(bf16[1,128,512]{2,1,0:T(8,128)(2,1)} %refs_3_.5) | copy-start | bytes 393220
  22.1 1.3 %collective-permute-start.6 = (f32[40,128]{1,0:T(8,128)S(1)}, f32[40,128]{1,0:T(8,128)S(1)}, u32[]{:S(2)}, u32[]{:S(2)}) collective-permute-start(f32[40,128]{1,0:T(8,128)S(1)} %get-tuple-element.55.pay), channel_id=1, source_target_pairs={{0,4},{4,0},{8,12},{12,8},{16,20},{20,16},{24,28},{28,24},{1,5},{5... | collective-permute-start | bytes 61448 | tf_op jit(solution)/shard_map/ppermute | solution.py:602
  23.3 6.5 %copy-start.5 = (bf16[1,128,128]{2,1,0:T(8,128)(2,1)S(1)}, bf16[1,128,128]{2,1,0:T(8,128)(2,1)}, u32[]{:S(2)}) copy-start(bf16[1,128,128]{2,1,0:T(8,128)(2,1)} %refs_2_.8) | copy-start | bytes 98308
  23.3 6.5 %copy-start.4 = (bf16[1,128,128]{2,1,0:T(8,128)(2,1)S(1)}, bf16[1,128,128]{2,1,0:T(8,128)(2,1)}, u32[]{:S(2)}) copy-start(bf16[1,128,128]{2,1,0:T(8,128)(2,1)} %refs_1_.3) | copy-start | bytes 98308
  23.3 3.8 %collective-permute-start.7 = (f32[40,128]{1,0:T(8,128)S(1)}, f32[40,128]{1,0:T(8,128)S(1)}, u32[]{:S(2)}, u32[]{:S(2)}) collective-permute-start(f32[40,128]{1,0:T(8,128)S(1)} %add.6), channel_id=1, source_target_pairs={{0,8},{4,12},{8,0},{12,4},{16,24},{20,28},{24,16},{28,20},{1,9},{5... | collective-permute-start | bytes 61448 | tf_op jit(solution)/shard_map/ppermute | solution.py:602
  27.2 6.2 %collective-permute-start.8 = (f32[40,128]{1,0:T(8,128)S(1)}, f32[40,128]{1,0:T(8,128)S(1)}, u32[]{:S(2)}, u32[]{:S(2)}) collective-permute-start(f32[40,128]{1,0:T(8,128)S(1)} %add.7.refs_0_), channel_id=1, source_target_pairs={{0,16},{4,20},{8,24},{12,28},{16,0},{20,4},{24,8},{28,12},{1,17},{... | collective-permute-start | bytes 61448 | tf_op jit(solution)/shard_map/ppermute | solution.py:602
  33.4 4.6 %collective-permute-start.10 = (bf16[352,128]{1,0:T(8,128)(2,1)S(1)}, bf16[352,128]{1,0:T(8,128)(2,1)S(1)}, u32[]{:S(2)}, u32[]{:S(2)}) collective-permute-start(bf16[352,128]{1,0:T(8,128)(2,1)S(1)} %get-tuple-element.68), channel_id=1, source_target_pairs={{0,2},{1,3},{2,0},{3,1},{4,6},{5,7},{6,4},{7,5},{8,10},{9,11},{10,... | collective-permute-start | bytes 270344 | tf_op jit(solution)/shard_map/ppermute | solution.py:602
  33.5 5.5 %collective-permute-start.11 = (bf16[352,128]{1,0:T(8,128)(2,1)S(1)}, bf16[352,128]{1,0:T(8,128)(2,1)S(1)}, u32[]{:S(2)}, u32[]{:S(2)}) collective-permute-start(bf16[352,128]{1,0:T(8,128)(2,1)S(1)} %get-tuple-element.69), channel_id=1, source_target_pairs={{0,3},{1,2},{2,1},{3,0},{4,7},{5,6},{6,5},{7,4},{8,11},{9,10},{10,... | collective-permute-start | bytes 270344 | tf_op jit(solution)/shard_map/ppermute | solution.py:602
  34.9 5.6 %collective-permute-start.9 = (bf16[352,128]{1,0:T(8,128)(2,1)S(1)}, bf16[352,128]{1,0:T(8,128)(2,1)S(1)}, u32[]{:S(2)}, u32[]{:S(2)}) collective-permute-start(bf16[352,128]{1,0:T(8,128)(2,1)S(1)} %get-tuple-element.67), channel_id=1, source_target_pairs={{0,1},{1,0},{2,3},{3,2},{4,5},{5,4},{6,7},{7,6},{8,9},{9,8},{10,11... | collective-permute-start | bytes 270344 | tf_op jit(solution)/shard_map/ppermute | solution.py:602

commit v4 on v3

--- a/solution.py
+++ b/solution.py
@@ -172,7 +172,7 @@
         delta = jnp.sum(cot.astype(F32) * attended, axis=1, keepdims=True)
         dprob = dot(cot, values_all, NT)
         dscore = (probs * (dprob - delta) * scale).astype(BF16)
-        query_grad[0, :, cols(r)] = dot(dscore, keys_all).astype(BF16)
+        query_grad[0, :, cols(r - heads[0])] = dot(dscore, keys_all).astype(BF16)
         rounded_heads.append(rounded)
         dscore_heads.append(dscore)
     query_rows = jnp.concatenate([queries[0, :, cols(r)] for r in heads], axis=0)
@@ -192,8 +192,7 @@
 
 def attend_body(peers, *refs):
     near = refs[4 : 4 + peers]
-    half, sums, query_grad, own, *parts = refs[4 + peers :]
-    query_grad[0, :, 0 : HEADS // 2 * W] = half[0]
+    sums, query_grad, own, *parts = refs[4 + peers :]
     key_acc, value_acc = attend_heads(
         peers, range(HEADS // 2, HEADS), *refs[:4], near, query_grad, sums
     )
@@ -246,7 +245,7 @@
 
 
 def own_body(mixer, step, weight, consts, cotan, *outs):
-    ext, acts, slopes, mixed_out, maps, sums_out, rows_out = outs
+    ext, acts, slopes, mixed_out, maps, rows_out = outs
     first = iota2(0) < TAPS - 1
     for g in range(GROUPS):
         place = ext.at[g]
@@ -280,16 +279,16 @@
     grad_meets_b = grad_meets.astype(BF16)
     maps[0] = dot(grad_meets_b, map_out_s[0])
     maps[1] = dot(grad_meets_b, map_in_s[0], TN)
-    sums_out[...] = sums
-    rows_out[...] = jnp.concatenate(out_rows + skip_rows, axis=0)
+    sum_rows = jnp.transpose(sums)
+    rows_out[...] = jnp.concatenate(out_rows + skip_rows + [sum_rows[0 : 4 * HEADS]], axis=0)
 
 
 def mixer_body(peers, *refs):
     mixer, step, weight, consts, cotan = refs[:5]
-    ext, acts, slopes, mixed_in, maps, sums_in, rows_in = refs[5:12]
-    bulk = refs[12 : 12 + peers]
-    grads, halo, pay = refs[12 + peers : 15 + peers]
-    tails, first_ext, peer_ext, states, adjoints = refs[15 + peers :]
+    ext, acts, slopes, mixed_in, maps, rows_in = refs[5:11]
+    bulk = refs[11 : 11 + peers]
+    grads, halo, pay = refs[11 + peers : 14 + peers]
+    tails, first_ext, peer_ext, states, adjoints, sums, reads, turned = refs[14 + peers :]
     me = lax.axis_index("ctx")
     slots = peers + 1
     index = [me] + [jnp.bitwise_xor(me, k) for k in range(1, slots)]
@@ -397,7 +396,7 @@
     )
     grad_in, grad_out = maps[0], maps[1]
     new_grad_meets = jnp.zeros((8, W), F32)
-    sums = sums_in[...]
+    sums[...] = jnp.zeros((W, W), F32)
     out_rows, pass_rows, skip_rows = [], [], []
 
     for h in range(HEADS):
@@ -421,37 +420,43 @@
         grad_scaled = mixed + projected
         lead_read = column(2, h) * dot_split(cot_b, split(state), NT)
         grad_out = grad_out + lead_read
-        grad_in = grad_in + dot((act * size * tail).astype(BF16), adjoint_s[0], NT)
+        reads[:, cols(h)] = (act * size * tail).astype(BF16)
+        turned[:, cols(h)] = adjoint_s[0]
         out_rows.append(rows_in[h : h + 1] + jnp.sum(flow, axis=0, keepdims=True))
         carried = lead_read * map_out
         trailing = projected * act
         carried = join(carried[0:8] - flow, carried[8:W])
-        extra = with_sum(jnp.zeros((W, W), F32), 0, h, carried)
-        extra = with_sum(extra, 1, h, trailing)
-        extra8 = with_sum(jnp.zeros((8, W), F32), 2, h, new_mixed * new_act)
-        sums = sums + extra
-        sums = join(sums[0:8] + extra8, sums[8:W])
+        sums[:, h : h + 1] = jnp.sum(carried, axis=1, keepdims=True)
+        at = HEADS + h
+        sums[:, at : at + 1] = jnp.sum(trailing, axis=1, keepdims=True)
+        at = 2 * HEADS + h
+        sums[0:8, at : at + 1] = jnp.sum(new_mixed * new_act, axis=1, keepdims=True)
         passed = jnp.sum(jnp.sum(state * adjoint, axis=0, keepdims=True), axis=1, keepdims=True)
         pass_rows.append(jnp.broadcast_to(passed, (1, W)))
         skipped = jnp.sum(cot[0:8] * new_act, axis=0, keepdims=True)
         skip_rows.append(rows_in[HEADS + h : HEADS + h + 1] + skipped)
         grads[h, 0:W, :] = (consts[8 + h : 9 + h] * cot + grad_scaled * size) * slope_of(h)
+    grad_in = grad_in + dot(reads[...], turned[...], NT)
     new_b = new_grad_meets.astype(BF16)
     grad_out = grad_out + dot(new_b, new_in.astype(BF16), TN)
     grad_in = join(grad_in[0:8] + dot(new_b, map_out_s[0]), grad_in[8:W])
     grads[HEADS, 0:W, :] = grad_in * slope_of(HEADS)
     grads[HEADS + 1, 0:W, :] = grad_out * slope_of(HEADS + 1)
-    sum_rows = jnp.transpose(sums)
+    sum_rows = jnp.transpose(sums[...])
 
     since = (iota2(0) >= iota2(1)).astype(F32)
     before = (iota2(0) < iota2(1)).astype(F32)
     trail = rows_of(sum_rows, 1)
     grad_decay = (
-        dot(jnp.concatenate(out_rows, axis=0) + rows_of(sum_rows, 0), since, precise=True)
+        dot(
+            jnp.concatenate(out_rows, axis=0) + rows_of(sum_rows, 0) + rows_in[8:12],
+            since,
+            precise=True,
+        )
         + dot(trail * own_size, before, precise=True)
         + jnp.exp(totals[0]) * jnp.concatenate(pass_rows, axis=0)
     )
-    grad_step = grad_decay * rate + rows_of(sum_rows, 2) + trail
+    grad_step = grad_decay * rate + rows_of(sum_rows, 2) + rows_in[16:20] + trail
     grad_raw = grad_step * sigmoid(rows_of(raw, 0))
     pay[24:28, :] = grad_decay * own_size * rate
     pay[28:32, :] = grad_raw
@@ -502,9 +507,12 @@
 
 
 def finish_body(peers, count, *refs):
-    partial, edge, weight, own, pay = refs[:5]
-    mixed = refs[5 : 5 + peers]
-    input_grad, key_grad, value_grad, conv_grad, decay_grad, bias_grad, skip_grad = refs[5 + peers :]
+    partial, edge, weight, own, pay, half_a, half_b = refs[:7]
+    mixed = refs[7 : 7 + peers]
+    input_grad, key_grad, value_grad, conv_grad, query_grad, *sums_out = refs[7 + peers :]
+    decay_grad, bias_grad, skip_grad = sums_out
+    query_grad[0, :, 0 : HEADS // 2 * W] = half_a[0]
+    query_grad[0, :, HEADS // 2 * W : HEADS * W] = half_b[0]
     me = lax.axis_index("ctx")
     both = own[...]
     total = pay[0:SUM_ROWS, :]
@@ -612,11 +620,10 @@
             shape((GROUPS, W, W), F32),
             shape((HEADS, W, W), F32),
             shape((2, W, W), F32),
-            shape((W, W), F32),
-            shape((2 * HEADS, W), F32),
+            shape((6 * HEADS, W), F32),
         ],
         in_specs=[vmem] * 5,
-        out_specs=[vmem] * 7,
+        out_specs=[vmem] * 6,
         compiler_params=params,
         name="own",
     )(
@@ -634,7 +641,7 @@
             shape((8 * GROUPS, W), F32),
             shape((PAY_ROWS, W), F32),
         ],
-        in_specs=[vmem] * (12 + peers),
+        in_specs=[vmem] * (11 + peers),
         out_specs=[vmem] * 3,
         scratch_shapes=[
             pltpu.VMEM((ctx + 1, 16 * GROUPS, W), BF16),
@@ -642,6 +649,9 @@
             pltpu.VMEM((peers * GROUPS, W + 8, W), F32),
             pltpu.VMEM((HEADS, W, W), F32),
             pltpu.VMEM((HEADS, W, W), F32),
+            pltpu.VMEM((W, W), F32),
+            pltpu.VMEM((W, HEADS * W), BF16),
+            pltpu.VMEM((W, HEADS * W), BF16),
         ],
         compiler_params=params,
         name="mixer",
@@ -668,7 +678,7 @@
         name="rows",
     )(grads, conv_weight, pay)
 
-    half, sums = pl.pallas_call(
+    half_a, sums = pl.pallas_call(
         lambda *refs: half_body(peers, *refs),
         out_shape=[
             shape((1, W, HEADS // 2 * W), BF16),
@@ -680,15 +690,15 @@
         name="half",
     )(queries, attn_keys, attn_values, attn_cotangent, *nears)
 
-    query_grad, own, *parts = pl.pallas_call(
+    half_b, own, *parts = pl.pallas_call(
         lambda *refs: attend_body(peers, *refs),
-        out_shape=[shape(queries.shape, BF16), shape((KV_ROWS, W), F32)]
+        out_shape=[shape((1, W, HEADS // 2 * W), BF16), shape((KV_ROWS, W), F32)]
         + [shape((KV_ROWS, W), BF16)] * peers,
-        in_specs=[vmem] * (6 + peers),
+        in_specs=[vmem] * (5 + peers),
         out_specs=[vmem] * (2 + peers),
         compiler_params=params,
         name="attend",
-    )(queries, attn_keys, attn_values, attn_cotangent, *nears, half, sums)
+    )(queries, attn_keys, attn_values, attn_cotangent, *nears, sums)
 
     last = dp.bit_length() - 2
     for n in range(last + 1):
@@ -711,14 +721,16 @@
             shape(attn_keys.shape, BF16),
             shape(attn_values.shape, BF16),
             shape(conv_weight.shape, F32),
+            shape(queries.shape, BF16),
         ]
         + [shape((HEADS,), F32)] * 3,
-        in_specs=[vmem] * (5 + peers),
-        out_specs=[vmem] * 4 + [smem] * 3,
+        in_specs=[vmem] * (7 + peers),
+        out_specs=[vmem] * 5 + [smem] * 3,
         compiler_params=params,
         name="finish",
-    )(input_grad, edge, conv_weight, own, pay, *mixed)
-    input_grad, key_grad, value_grad, conv_grad, decay_grad, bias_grad, skip_grad = outs
+    )(input_grad, edge, conv_weight, own, pay, half_a, half_b, *mixed)
+    input_grad, key_grad, value_grad, conv_grad, query_grad, *sums_out = outs
+    decay_grad, bias_grad, skip_grad = sums_out
     return (
         input_grad,
         jnp.swapaxes(step_grad, 1, 2),

time: 41.4 us -> 40.7 us (0.983)
  Pallas kernels: 10 us -> 9.4 us
    pallas_call x1, Pallas kernels: 2.06 us -> 1.47 us  [on_device(): pl.pallas_call(lambda *refs: attend_body(peers, *refs), out_shape=[shape(...]
  transfers between devices with their start and end apart: 12 -> 12, of which waited for: 5 -> 5; matrix products, arithmetic and copies ran while one was open for 0% -> 0% of each run, Pallas kernels for 19% -> 18%
where the time goes in v4:
time: 40.7 us; the launch traced here: 40.5 us
  starting transfers between devices  24 us (59%)
  Pallas kernels  9.4 us (23%)
  waiting for transfers between devices  6.21 us (15%)
  between operations  0.86 us (2%)
    ppermute x12, starting transfers between devices, swap(): return lax.ppermute(array, axis, pairs)  24 us
    ppermute x12, waiting for transfers between devices, swap(): return lax.ppermute(array, axis, pairs)  6.21 us
    pallas_call x1, Pallas kernels, on_device(): pl.pallas_call(lambda *refs: mixer_body(peers, *refs), out_shape=[shape((...  2.62 us
    pallas_call x1, Pallas kernels, on_device(): pl.pallas_call(lambda *refs: attend_body(peers, *refs), out_shape=[shape(...  1.47 us
    pallas_call x1, Pallas kernels, on_device(): pl.pallas_call(lambda *refs: half_body(peers, *refs), out_shape=[shape((1...  1.45 us
    pallas_call x1, Pallas kernels, on_device(): pl.pallas_call(lambda *refs: pack_body(bits, *refs), out_shape=[shape((KV...  1.32 us
    pallas_call x1, Pallas kernels, on_device(): pl.pallas_call(own_body, out_shape=[shape((GROUPS, W + 8, W), F32), shape...  1.04 us
    pallas_call x1, Pallas kernels, on_device(): pl.pallas_call(lambda *refs: finish_body(peers, dp, *refs), out_shape=[sh...  0.82 us
  transfers between devices with their start and end apart: 12, of which 5 were waited for; matrix products, arithmetic and copies ran while one was open for 0% of the time, Pallas kernels for 18%

profile of v4, /device:TPU:0, one launch (start us, length us, event | category | flops | bytes accessed | tf_op | source)
XLA Modules:
  0.0 40.5 jit_solution(1582540274796944805)
XLA Ops:
  0.7 1.3 %pack.1 = (bf16[256,128]{1,0:T(8,128)(2,1)S(1)}, bf16[656,128]{1,0:T(8,128)(2,1)S(1)}, bf16[656,128]{1,0:T(8,128)(2,1)S(1)}, f32[16,128]{1,0:T(8,128)S(1)}) custom-call(bf16[1,128,768]{2,1,0:T(8,128)(2,1)} %refs_0_.5, f32[1,4,128]{2,1,0:T(4,128)} %bitcast.2, bf16[1,128,512]{2,1,0:T(8,128)(2,1)} %refs_4_.3, bf16[1,128,128]{2,1,0:T(8,128)(2,1)} %refs_1_.3, ...), custom_call_target="tpu_custom_call" | custom-call | tf_op jit(solution)/shard_map/pack/pallas_call | solution.py:577
  2.0 3.1 %collective-permute-start.1 = (bf16[656,128]{1,0:T(8,128)(2,1)S(1)}, bf16[656,128]{1,0:T(8,128)(2,1)S(1)}, u32[]{:S(2)}, u32[]{:S(2)}) collective-permute-start(bf16[656,128]{1,0:T(8,128)(2,1)S(1)} %get-tuple-element.52), channel_id=1, source_target_pairs={{0,2},{1,3},{2,0},{3,1},{4,6},{5,7},{6,4},{7,5},{8,10},{9,11},{10,... | collective-permute-start | bytes 503816 | tf_op jit(solution)/shard_map/ppermute | solution.py:610
  5.1 1.4 %collective-permute-start.2 = (bf16[656,128]{1,0:T(8,128)(2,1)S(1)}, bf16[656,128]{1,0:T(8,128)(2,1)S(1)}, u32[]{:S(2)}, u32[]{:S(2)}) collective-permute-start(bf16[656,128]{1,0:T(8,128)(2,1)S(1)} %get-tuple-element.52), channel_id=1, source_target_pairs={{0,3},{1,2},{2,1},{3,0},{4,7},{5,6},{6,5},{7,4},{8,11},{9,10},{10,... | collective-permute-start | bytes 503816 | tf_op jit(solution)/shard_map/ppermute | solution.py:610
  6.5 0.1 collective-permute-start
  6.6 3.8 %collective-permute-start.3 = (bf16[256,128]{1,0:T(8,128)(2,1)S(1)}, bf16[256,128]{1,0:T(8,128)(2,1)S(1)}, u32[]{:S(2)}, u32[]{:S(2)}) collective-permute-start(bf16[256,128]{1,0:T(8,128)(2,1)S(1)} %get-tuple-element.57), channel_id=1, source_target_pairs={{0,1},{2,3},{4,5},{6,7},{8,9},{10,11},{12,13},{14,15},{16,17},{18,... | collective-permute-start | bytes 196616 | tf_op jit(solution)/shard_map/ppermute | solution.py:610
  10.4 3.4 %collective-permute-start.4 = (bf16[256,128]{1,0:T(8,128)(2,1)S(1)}, bf16[256,128]{1,0:T(8,128)(2,1)S(1)}, u32[]{:S(2)}, u32[]{:S(2)}) collective-permute-start(bf16[256,128]{1,0:T(8,128)(2,1)S(1)} %get-tuple-element.57), channel_id=1, source_target_pairs={{0,2},{1,3},{4,6},{5,7},{8,10},{9,11},{12,14},{13,15},{16,18},{17,... | collective-permute-start | bytes 196616 | tf_op jit(solution)/shard_map/ppermute | solution.py:610
  13.9 0.0 collective-permute-done.1.refs_12_
  13.9 4.3 %collective-permute-start.5 = (bf16[256,128]{1,0:T(8,128)(2,1)S(1)}, bf16[256,128]{1,0:T(8,128)(2,1)S(1)}, u32[]{:S(2)}, u32[]{:S(2)}) collective-permute-start(bf16[256,128]{1,0:T(8,128)(2,1)S(1)} %get-tuple-element.57), channel_id=1, source_target_pairs={{0,3},{1,2},{4,7},{5,6},{8,11},{9,10},{12,15},{13,14},{16,19},{17,... | collective-permute-start | bytes 196616 | tf_op jit(solution)/shard_map/ppermute | solution.py:610
  18.3 1.0 %own.1 = (f32[6,136,128]{2,1,0:T(8,128)S(1)}, f32[6,128,128]{2,1,0:T(8,128)S(1)}, f32[6,128,128]{2,1,0:T(8,128)S(1)}, f32[4,128,128]{2,1,0:T(8,128)S(1)}, f32[2,...) custom-call(bf16[1,128,768]{2,1,0:T(8,128)(2,1)S(1)} %copy-done, f32[1,4,128]{2,1,0:T(4,128)S(1)} %bitcast.3, ...), custom_call_target="tpu_custom_call" | custom-call | tf_op jit(solution)/shard_map/own/pallas_call | solution.py:615
  19.3 0.0 collective-permute-done.2.refs_13_
  19.3 0.0 collective-permute-done.refs_11_
  19.3 0.0 copy-start.2
  19.3 0.0 copy-start.3
  19.3 2.6 %mixer.3 = (f32[6,136,128]{2,1,0:T(8,128)S(1)}, f32[48,128]{1,0:T(8,128)S(1)}, f32[40,128]{1,0:T(8,128)S(1)}) custom-call(bf16[1,128,768]{2,1,0:T(8,128)(2,1)S(1)} %copy-done, f32[1,4,128]{2,1,0:T(4,128)S(1)} %bitcast.4, f32[4,768]{1,0:T(4,128)S(1)} %copy-done.6, f32[16,128]{1,0:T(8,128)S(1)} %get-tuple-element.44.consts.refs_3_, ...), custom_call_target="tpu_custom_call" | custom-call | tf_op jit(solution)/shard_map/mixer/pallas_call | solution.py:637
  22.0 0.1 collective-permute-start.6
  22.0 1.2 %collective-permute-done.6 = f32[40,128]{1,0:T(8,128)S(1)} collective-permute-done((f32[40,128]{1,0:T(8,128)S(1)}, f32[40,128]{1,0:T(8,128)S(1)}, u32[]{:S(2)}, u32[]{:S(2)}) %collective-permute-start.6) | collective-permute-done | bytes 20512 | tf_op jit(solution)/shard_map/ppermute | solution.py:610
  23.2 1.6 %collective-permute-start.7 = (f32[40,128]{1,0:T(8,128)S(1)}, f32[40,128]{1,0:T(8,128)S(1)}, u32[]{:S(2)}, u32[]{:S(2)}) collective-permute-start(f32[40,128]{1,0:T(8,128)S(1)} %add.6), channel_id=1, source_target_pairs={{0,8},{4,12},{8,0},{12,4},{16,24},{20,28},{24,16},{28,20},{1,9},{5... | collective-permute-start | bytes 61448 | tf_op jit(solution)/shard_map/ppermute | solution.py:610
  24.9 2.2 %collective-permute-done.7 = f32[40,128]{1,0:T(8,128)S(1)} collective-permute-done((f32[40,128]{1,0:T(8,128)S(1)}, f32[40,128]{1,0:T(8,128)S(1)}, u32[]{:S(2)}, u32[]{:S(2)}) %collective-permute-start.7) | collective-permute-done | bytes 20512 | tf_op jit(solution)/shard_map/ppermute | solution.py:610
  27.1 2.6 %collective-permute-start.8 = (f32[40,128]{1,0:T(8,128)S(1)}, f32[40,128]{1,0:T(8,128)S(1)}, u32[]{:S(2)}, u32[]{:S(2)}) collective-permute-start(f32[40,128]{1,0:T(8,128)S(1)} %add.7.refs_0_), channel_id=1, source_target_pairs={{0,16},{4,20},{8,24},{12,28},{16,0},{20,4},{24,8},{28,12},{1,17},{... | collective-permute-start | bytes 61448 | tf_op jit(solution)/shard_map/ppermute | solution.py:610
  29.7 0.0 collective-permute-done.3.refs_4_
  29.7 0.0 collective-permute-done.4.refs_5_
  29.7 1.5 %half.1 = (bf16[1,128,256]{2,1,0:T(8,128)(2,1)S(1)}, f32[2,512,128]{2,1,0:T(8,128)S(1)}) custom-call(bf16[1,128,512]{2,1,0:T(8,128)(2,1)S(1)} %copy-done.2, bf16[1,128,128]{2,1,0:T(8,128)(2,1)S(1)} %copy-done.4, bf16[1,128,128]{2,1,0:T(8,128)(2,1)S(1)} %copy-done.5, bf16[1,128,512]{2,1,0:T(8,128)(2,1)S(1)} %copy-done.3, ...), custom_call_target="tpu_custom_call" | custom-call | tf_op jit(solution)/shard_map/half/pallas_call | solution.py:681
  31.2 1.5 %attend.1 = (bf16[1,128,256]{2,1,0:T(8,128)(2,1)S(1)}, f32[256,128]{1,0:T(8,128)S(1)}, bf16[256,128]{1,0:T(8,128)(2,1)S(1)}, bf16[256,128]{1,0:T(8,128)(2,1)S(1)}, bf16[256,128]{1,0:T(8,128)(2,1)S(1)}) custom-call(bf16[1,128,512]{2,1,0:T(8,128)(2,1)S(1)} %copy-done.2, bf16[1,128,128]{2,1,0:T(8,128)(2,1)S(1)} %copy-done.4, ...), custom_call_target="tpu_custom_call" | custom-call | tf_op jit(solution)/shard_map/attend/pallas_call | solution.py:693
  32.7 0.0 collective-permute-done.8.refs_1_
  32.7 0.1 collective-permute-start.10
  32.8 1.4 %collective-permute-start.11 = (bf16[352,128]{1,0:T(8,128)(2,1)S(1)}, bf16[352,128]{1,0:T(8,128)(2,1)S(1)}, u32[]{:S(2)}, u32[]{:S(2)}) collective-permute-start(bf16[352,128]{1,0:T(8,128)(2,1)S(1)} %get-tuple-element.69), channel_id=1, source_target_pairs={{0,3},{1,2},{2,1},{3,0},{4,7},{5,6},{6,5},{7,4},{8,11},{9,10},{10,... | collective-permute-start | bytes 270344 | tf_op jit(solution)/shard_map/ppermute | solution.py:610
  34.2 2.1 %collective-permute-start.9 = (bf16[352,128]{1,0:T(8,128)(2,1)S(1)}, bf16[352,128]{1,0:T(8,128)(2,1)S(1)}, u32[]{:S(2)}, u32[]{:S(2)}) collective-permute-start(bf16[352,128]{1,0:T(8,128)(2,1)S(1)} %get-tuple-element.67), channel_id=1, source_target_pairs={{0,1},{1,0},{2,3},{3,2},{4,5},{5,4},{6,7},{7,6},{8,9},{9,8},{10,11... | collective-permute-start | bytes 270344 | tf_op jit(solution)/shard_map/ppermute | solution.py:610
  36.3 0.7 %rows.1 = (bf16[1,128,768]{2,1,0:T(8,128)(2,1)S(1)}, f32[16,768]{1,0:T(8,128)S(1)}, f32[1,4,128]{2,1,0:T(4,128)}) custom-call(f32[6,136,128]{2,1,0:T(8,128)S(1)} %get-tuple-element.53.grads, f32[4,768]{1,0:T(4,128)S(1)} %copy-done.6, f32[40,128]{1,0:T(8,128)S(1)} %get-tuple-element.54.pay), custom_call_target="tpu_custom_call" | custom-call | tf_op jit(solution)/shard_map/rows/pallas_call | solution.py:668
  36.9 0.4 collective-permute-done.10.refs_8_
  37.3 1.0 %collective-permute-done.11.refs_9_ = bf16[352,128]{1,0:T(8,128)(2,1)S(1)} collective-permute-done((bf16[352,128]{1,0:T(8,128)(2,1)S(1)}, bf16[352,128]{1,0:T(8,128)(2,1)S(1)}, u32[]{:S(2)}, u32[]{:S(2)}) %collective-permute-start.11) | collective-permute-done | bytes 90144 | tf_op jit(solution)/shard_map/ppermute | solution.py:610
  38.3 1.5 %collective-permute-done.9.refs_7_ = bf16[352,128]{1,0:T(8,128)(2,1)S(1)} collective-permute-done((bf16[352,128]{1,0:T(8,128)(2,1)S(1)}, bf16[352,128]{1,0:T(8,128)(2,1)S(1)}, u32[]{:S(2)}, u32[]{:S(2)}) %collective-permute-start.9) | collective-permute-done | bytes 90144 | tf_op jit(solution)/shard_map/ppermute | solution.py:610
  39.7 0.8 %finish.1 = (bf16[1,128,768]{2,1,0:T(8,128)(2,1)}, bf16[1,128,128]{2,1,0:T(8,128)(2,1)}, bf16[1,128,128]{2,1,0:T(8,128)(2,1)}, f32[4,768]{1,0:T(4,128)}, bf16[1,...) custom-call(bf16[1,128,768]{2,1,0:T(8,128)(2,1)S(1)} %get-tuple-element.55.refs_0_, ...), custom_call_target="tpu_custom_call" | custom-call | tf_op jit(solution)/shard_map/finish/pallas_call | solution.py:717
  (18 shorter events, 0.1 us)
Async XLA Ops:
  0.6 17.6 %copy-start = (bf16[1,128,768]{2,1,0:T(8,128)(2,1)S(1)}, bf16[1,128,768]{2,1,0:T(8,128)(2,1)}, u32[]{:S(2)}) copy-start(bf16[1,128,768]{2,1,0:T(8,128)(2,1)} %refs_0_.5) | copy-start | bytes 589828
  0.7 17.6 %copy-start.1 = (bf16[1,128,512]{2,1,0:T(8,128)(2,1)S(1)}, bf16[1,128,512]{2,1,0:T(8,128)(2,1)}, u32[]{:S(2)}) copy-start(bf16[1,128,512]{2,1,0:T(8,128)(2,1)} %refs_4_.3) | copy-start | bytes 393220
  0.7 17.6 %copy-start.6 = (f32[4,768]{1,0:T(4,128)S(1)}, f32[4,768]{1,0:T(4,128)}, u32[]{:S(2)}) copy-start(f32[4,768]{1,0:T(4,128)} %refs_2_.9) | copy-start | bytes 36868
  2.0 11.9 %collective-permute-start.1 = (bf16[656,128]{1,0:T(8,128)(2,1)S(1)}, bf16[656,128]{1,0:T(8,128)(2,1)S(1)}, u32[]{:S(2)}, u32[]{:S(2)}) collective-permute-start(bf16[656,128]{1,0:T(8,128)(2,1)S(1)} %get-tuple-element.52), channel_id=1, source_target_pairs={{0,2},{1,3},{2,0},{3,1},{4,6},{5,7},{6,4},{7,5},{8,10},{9,11},{10,... | collective-permute-start | bytes 503816 | tf_op jit(solution)/shard_map/ppermute | solution.py:610
  5.1 14.2 %collective-permute-start.2 = (bf16[656,128]{1,0:T(8,128)(2,1)S(1)}, bf16[656,128]{1,0:T(8,128)(2,1)S(1)}, u32[]{:S(2)}, u32[]{:S(2)}) collective-permute-start(bf16[656,128]{1,0:T(8,128)(2,1)S(1)} %get-tuple-element.52), channel_id=1, source_target_pairs={{0,3},{1,2},{2,1},{3,0},{4,7},{5,6},{6,5},{7,4},{8,11},{9,10},{10,... | collective-permute-start | bytes 503816 | tf_op jit(solution)/shard_map/ppermute | solution.py:610
  6.5 11.8 %copy-start.7 = (f32[1,128,4]{1,2,0:T(4,128)S(1)}, f32[1,128,4]{1,2,0:T(4,128)}, u32[]{:S(2)}) copy-start(f32[1,128,4]{1,2,0:T(4,128)} %param.12) | copy-start | bytes 6148
  6.5 12.8 %collective-permute-start = (bf16[656,128]{1,0:T(8,128)(2,1)S(1)}, bf16[656,128]{1,0:T(8,128)(2,1)S(1)}, u32[]{:S(2)}, u32[]{:S(2)}) collective-permute-start(bf16[656,128]{1,0:T(8,128)(2,1)S(1)} %get-tuple-element.51), channel_id=1, source_target_pairs={{0,1},{1,0},{2,3},{3,2},{4,5},{5,4},{6,7},{7,6},{8,9},{9,8},{10,11... | collective-permute-start | bytes 503816 | tf_op jit(solution)/shard_map/ppermute | solution.py:610
  6.6 23.1 %collective-permute-start.3 = (bf16[256,128]{1,0:T(8,128)(2,1)S(1)}, bf16[256,128]{1,0:T(8,128)(2,1)S(1)}, u32[]{:S(2)}, u32[]{:S(2)}) collective-permute-start(bf16[256,128]{1,0:T(8,128)(2,1)S(1)} %get-tuple-element.57), channel_id=1, source_target_pairs={{0,1},{2,3},{4,5},{6,7},{8,9},{10,11},{12,13},{14,15},{16,17},{18,... | collective-permute-start | bytes 196616 | tf_op jit(solution)/shard_map/ppermute | solution.py:610
  10.4 19.2 %collective-permute-start.4 = (bf16[256,128]{1,0:T(8,128)(2,1)S(1)}, bf16[256,128]{1,0:T(8,128)(2,1)S(1)}, u32[]{:S(2)}, u32[]{:S(2)}) collective-permute-start(bf16[256,128]{1,0:T(8,128)(2,1)S(1)} %get-tuple-element.57), channel_id=1, source_target_pairs={{0,2},{1,3},{4,6},{5,7},{8,10},{9,11},{12,14},{13,15},{16,18},{17,... | collective-permute-start | bytes 196616 | tf_op jit(solution)/shard_map/ppermute | solution.py:610
  13.9 15.8 %collective-permute-start.5 = (bf16[256,128]{1,0:T(8,128)(2,1)S(1)}, bf16[256,128]{1,0:T(8,128)(2,1)S(1)}, u32[]{:S(2)}, u32[]{:S(2)}) collective-permute-start(bf16[256,128]{1,0:T(8,128)(2,1)S(1)} %get-tuple-element.57), channel_id=1, source_target_pairs={{0,3},{1,2},{4,7},{5,6},{8,11},{9,10},{12,15},{13,14},{16,19},{17,... | collective-permute-start | bytes 196616 | tf_op jit(solution)/shard_map/ppermute | solution.py:610
  19.3 10.4 %copy-start.2 = (bf16[1,128,512]{2,1,0:T(8,128)(2,1)S(1)}, bf16[1,128,512]{2,1,0:T(8,128)(2,1)}, u32[]{:S(2)}) copy-start(bf16[1,128,512]{2,1,0:T(8,128)(2,1)} %refs_0_.7) | copy-start | bytes 393220
  19.3 10.4 %copy-start.3 = (bf16[1,128,512]{2,1,0:T(8,128)(2,1)S(1)}, bf16[1,128,512]{2,1,0:T(8,128)(2,1)}, u32[]{:S(2)}) copy-start(bf16[1,128,512]{2,1,0:T(8,128)(2,1)} %refs_3_.5) | copy-start | bytes 393220
  22.0 1.3 %collective-permute-start.6 = (f32[40,128]{1,0:T(8,128)S(1)}, f32[40,128]{1,0:T(8,128)S(1)}, u32[]{:S(2)}, u32[]{:S(2)}) collective-permute-start(f32[40,128]{1,0:T(8,128)S(1)} %get-tuple-element.54.pay), channel_id=1, source_target_pairs={{0,4},{4,0},{8,12},{12,8},{16,20},{20,16},{24,28},{28,24},{1,5},{5... | collective-permute-start | bytes 61448 | tf_op jit(solution)/shard_map/ppermute | solution.py:610
  23.2 6.5 %copy-start.5 = (bf16[1,128,128]{2,1,0:T(8,128)(2,1)S(1)}, bf16[1,128,128]{2,1,0:T(8,128)(2,1)}, u32[]{:S(2)}) copy-start(bf16[1,128,128]{2,1,0:T(8,128)(2,1)} %refs_2_.8) | copy-start | bytes 98308
  23.2 6.5 %copy-start.4 = (bf16[1,128,128]{2,1,0:T(8,128)(2,1)S(1)}, bf16[1,128,128]{2,1,0:T(8,128)(2,1)}, u32[]{:S(2)}) copy-start(bf16[1,128,128]{2,1,0:T(8,128)(2,1)} %refs_1_.3) | copy-start | bytes 98308
  23.2 3.8 %collective-permute-start.7 = (f32[40,128]{1,0:T(8,128)S(1)}, f32[40,128]{1,0:T(8,128)S(1)}, u32[]{:S(2)}, u32[]{:S(2)}) collective-permute-start(f32[40,128]{1,0:T(8,128)S(1)} %add.6), channel_id=1, source_target_pairs={{0,8},{4,12},{8,0},{12,4},{16,24},{20,28},{24,16},{28,20},{1,9},{5... | collective-permute-start | bytes 61448 | tf_op jit(solution)/shard_map/ppermute | solution.py:610
  27.1 5.6 %collective-permute-start.8 = (f32[40,128]{1,0:T(8,128)S(1)}, f32[40,128]{1,0:T(8,128)S(1)}, u32[]{:S(2)}, u32[]{:S(2)}) collective-permute-start(f32[40,128]{1,0:T(8,128)S(1)} %add.7.refs_0_), channel_id=1, source_target_pairs={{0,16},{4,20},{8,24},{12,28},{16,0},{20,4},{24,8},{28,12},{1,17},{... | collective-permute-start | bytes 61448 | tf_op jit(solution)/shard_map/ppermute | solution.py:610
  32.7 4.6 %collective-permute-start.10 = (bf16[352,128]{1,0:T(8,128)(2,1)S(1)}, bf16[352,128]{1,0:T(8,128)(2,1)S(1)}, u32[]{:S(2)}, u32[]{:S(2)}) collective-permute-start(bf16[352,128]{1,0:T(8,128)(2,1)S(1)} %get-tuple-element.68), channel_id=1, source_target_pairs={{0,2},{1,3},{2,0},{3,1},{4,6},{5,7},{6,4},{7,5},{8,10},{9,11},{10,... | collective-permute-start | bytes 270344 | tf_op jit(solution)/shard_map/ppermute | solution.py:610
  32.8 5.5 %collective-permute-start.11 = (bf16[352,128]{1,0:T(8,128)(2,1)S(1)}, bf16[352,128]{1,0:T(8,128)(2,1)S(1)}, u32[]{:S(2)}, u32[]{:S(2)}) collective-permute-start(bf16[352,128]{1,0:T(8,128)(2,1)S(1)} %get-tuple-element.69), channel_id=1, source_target_pairs={{0,3},{1,2},{2,1},{3,0},{4,7},{5,6},{6,5},{7,4},{8,11},{9,10},{10,... | collective-permute-start | bytes 270344 | tf_op jit(solution)/shard_map/ppermute | solution.py:610
  34.2 5.5 %collective-permute-start.9 = (bf16[352,128]{1,0:T(8,128)(2,1)S(1)}, bf16[352,128]{1,0:T(8,128)(2,1)S(1)}, u32[]{:S(2)}, u32[]{:S(2)}) collective-permute-start(bf16[352,128]{1,0:T(8,128)(2,1)S(1)} %get-tuple-element.67), channel_id=1, source_target_pairs={{0,1},{1,0},{2,3},{3,2},{4,5},{5,4},{6,7},{7,6},{8,9},{9,8},{10,11... | collective-permute-start | bytes 270344 | tf_op jit(solution)/shard_map/ppermute | solution.py:610
